TPU v7x, 32 devices: a whole 2x2x4 slice. The times are simulated.
32 devices in a mesh: dp: 4 (over z), shard: 8 (over y, x, core).
Axes of the slice: x: 2, y: 2, z: 4, core: 2. Of those that a mesh axis runs over, the one named last changes fastest.
Arguments:
- tokens: bfloat16 [16384, 1024], P(('dp', 'shard')), may hold values from -6 to 6
- targets: bfloat16 [16384, 1024], P(('dp', 'shard')), may hold values from -6 to 6
- segments: int32 [16384], P('dp'), may hold values from 0 to 511, as said below
- valid: int32 [16384], P(('dp', 'shard')), may hold values from 0 to 1, as said below
- master: float32 [1024, 12288], P('shard')
- vectors: float32 [13312], P('shard')
- left_stat: float32 [8, 96, 128, 128], P('shard'), as said below
- right_stat: float32 [8, 96, 128, 128], P('shard'), as said below
- left_root: bfloat16 [8, 96, 128, 128], P('shard'), as said below
- right_root: bfloat16 [8, 96, 128, 128], P('shard'), as said below
- vector_stat: float32 [13312], P('shard'), may hold values from 0.01 to 1
Outputs:
- input_grad: float32 [16384, 1024], P(('dp', 'shard'))
- grad_norm: float32 [], replicated
- new_left: float32 [8, 96, 128, 128], P('shard')
- new_right: float32 [8, 96, 128, 128], P('shard')
- new_master: float32 [1024, 12288], P('shard')
- master_copy: bfloat16 [1024, 12288], P('shard')
- new_vectors: float32 [13312], P('shard')
- new_vector_stat: float32 [13312], P('shard')
Inputs may be any that keep to these rules, and one draw needn't show every extreme that they name: `segments`: taken in order of positions, within each sequence the numbers start at 0 and never fall, rising by at most one from a position to the next; positions 128 to 384 lie in one document, and so do positions 640 to 896. The row of position 0 of every sequence is valid. `left_stat`: every block is symmetric. `right_stat`: every block is symmetric. `left_root`: every block is symmetric. `right_root`: every block is symmetric.
All inputs are finite; a program needn't handle non-finite values.
Results may differ from a plain program's by a relative error of at most 0.012.
Values may be sent and summed in bfloat16 or wider, within the bound.
A program may use at most 320 MiB of HBM per device.

v0:
```python
from functools import partial
import math

import jax
import jax.numpy as jnp
from jax import lax
from jax.sharding import PartitionSpec as P

HD = 64
ROT = 16
BS = 128


EPS = 1e-05
NEG = -1e30
LEARN = 0.5
LEARN_VEC = 0.15
HIGHEST = lax.Precision.HIGHEST


def partner(shard, axis, distance):
    return lax.ppermute(shard, axis, [(i, i ^ 1 << distance) for i in range(lax.axis_size(axis))])


def layer_norm(values, gain, shift):
    row_mean = jnp.mean(values, axis=-1, keepdims=True)
    centred = values - row_mean
    spread = jnp.mean(centred * centred, axis=-1, keepdims=True)
    return centred * lax.rsqrt(spread + EPS) * gain + shift


def rotate(values, cosine_grid, sine_grid):
    half_rot = ROT // 2
    first = values[..., :half_rot]
    second = values[..., half_rot:ROT]
    return jnp.concatenate(
        [
            first * cosine_grid - second * sine_grid,
            second * cosine_grid + first * sine_grid,
            values[..., ROT:],
        ],
        axis=-1,
    )


def angles(positions):
    half_rot = ROT // 2
    frequency = jnp.power(10000.0, -2.0 * jnp.arange(half_rot, dtype=jnp.float32) / ROT)
    angle_grid = positions.astype(jnp.float32)[:, None] * frequency[None, :]
    return (jnp.cos(angle_grid)[:, None, :], jnp.sin(angle_grid)[:, None, :])


def place_rows(parity, row_count):
    half_rows = row_count // 2
    local = jnp.arange(row_count, dtype=jnp.int32)
    block = 2 * parity + local // half_rows
    quarter = jnp.where(block == 0, 0, jnp.where(block == 1, 3, block - 1))
    return quarter * half_rows + local % half_rows


def body(
    tokens,
    targets,
    segments,
    valid,
    master,
    vectors,
    left_stat,
    right_stat,
    left_root,
    right_root,
    vector_stat,
):
    row_count, model_width = tokens.shape
    head_count = model_width // HD
    stack_width = master.shape[1]
    hidden_width = (stack_width - 4 * model_width) // 2
    shard_count = lax.axis_size("shard")
    data_count = lax.axis_size("dp")
    shard_index = lax.axis_index("shard")
    is_later = shard_index % 2
    partner_index = shard_index + 1 - 2 * is_later
    weights, vector_copy = (
        lax.all_gather(master.astype(jnp.bfloat16), "shard", axis=0, tiled=True),
        lax.all_gather(vectors.astype(jnp.bfloat16), "shard", axis=0, tiled=True),
    )
    valid_float = valid.astype(jnp.float32)
    valid_total = lax.psum(jnp.sum(valid_float), ("dp", "shard"))
    params = vector_copy.astype(jnp.float32)
    gain_one = params[0:model_width]
    shift_one = params[model_width : 2 * model_width]
    gain_two = params[2 * model_width : 3 * model_width]
    shift_two = params[3 * model_width : 4 * model_width]
    bias_qkv = params[4 * model_width : 7 * model_width]
    bias_out = params[7 * model_width : 8 * model_width]
    bias_up = params[8 * model_width : 8 * model_width + hidden_width]
    bias_down = params[8 * model_width + hidden_width :]
    w_qkv = weights[:, : 3 * model_width]
    w_out = weights[:, 3 * model_width : 4 * model_width]
    w_up = weights[:, 4 * model_width : 4 * model_width + hidden_width]
    w_down = weights[:, 4 * model_width + hidden_width :]
    inputs = tokens.astype(jnp.float32)
    norm_one, back_one = jax.vjp(layer_norm, inputs, gain_one, shift_one)
    norm_two, back_two = jax.vjp(layer_norm, inputs, gain_two, shift_two)
    one_low = norm_one.astype(jnp.bfloat16)
    two_low = norm_two.astype(jnp.bfloat16)
    projected = jnp.dot(one_low, w_qkv, preferred_element_type=jnp.float32) + bias_qkv
    head_shape = (row_count, head_count, HD)
    positions = place_rows(is_later, row_count)
    partner_pos = place_rows(1 - is_later, row_count)
    cosine_grid, sine_grid = angles(positions)
    turner = partial(rotate, cosine_grid=cosine_grid, sine_grid=sine_grid)
    query_rot, query_back = jax.vjp(turner, projected[:, :model_width].reshape(head_shape))
    key_rot, key_back = jax.vjp(
        turner, projected[:, model_width : 2 * model_width].reshape(head_shape)
    )
    query_low = query_rot.astype(jnp.bfloat16)
    key_low = key_rot.astype(jnp.bfloat16).reshape(row_count, model_width)
    value_low = projected[:, 2 * model_width :].astype(jnp.bfloat16)
    prior_key, prior_value = partner((key_low, value_low), "shard", 0)
    own_ids = lax.dynamic_slice_in_dim(segments, shard_index * row_count, row_count)
    partner_ids = lax.dynamic_slice_in_dim(segments, partner_index * row_count, row_count)
    key_ids = jnp.concatenate([partner_ids, own_ids])
    key_pos = jnp.concatenate([partner_pos, positions])
    allowed = (key_pos[None, :] <= positions[:, None]) & (key_ids[None, :] == own_ids[:, None])
    key_shape = (2 * row_count, head_count, HD)
    key_all = jnp.concatenate([prior_key, key_low], axis=0).reshape(key_shape)
    value_all = jnp.concatenate([prior_value, value_low], axis=0).reshape(key_shape)

    def masked_scores(key_part):
        scores = jnp.einsum(
            "qhe,khe->hqk", query_low, key_part, preferred_element_type=jnp.float32
        ) * HD ** (-0.5)
        return jnp.where(allowed[None], scores, NEG)

    scores = masked_scores(key_all)
    row_max = jnp.max(scores, axis=-1, keepdims=True)
    exponent = jnp.exp(scores - row_max)
    row_sum = jnp.sum(exponent, axis=-1, keepdims=True)
    soft_weights = exponent / row_sum
    attention = jnp.einsum(
        "hqk,khe->qhe",
        soft_weights.astype(jnp.bfloat16),
        value_all,
        preferred_element_type=jnp.float32,
    )
    attention_low = attention.reshape(row_count, model_width).astype(jnp.bfloat16)
    branch = jnp.dot(attention_low, w_out, preferred_element_type=jnp.float32) + bias_out
    up_value = jnp.dot(two_low, w_up, preferred_element_type=jnp.float32) + bias_up
    active, active_back = jax.vjp(partial(jax.nn.gelu, approximate=False), up_value)
    active_low = active.astype(jnp.bfloat16)
    feed_out = (
        jnp.einsum("tf,df->td", active_low, w_down, preferred_element_type=jnp.float32) + bias_down
    )
    outputs = inputs + (branch + feed_out)
    tokens_all = row_count * shard_count * data_count
    grad_out = (
        tokens_all / valid_total * valid_float[:, None] * (outputs - targets.astype(jnp.float32))
    )
    grad_low = grad_out.astype(jnp.bfloat16)
    grad_attention = jnp.einsum("te,de->td", grad_low, w_out, preferred_element_type=jnp.float32)
    grad_attention_low = grad_attention.astype(jnp.bfloat16).reshape(head_shape)
    grad_active = jnp.dot(grad_low, w_down, preferred_element_type=jnp.float32)
    up_low = active_back(grad_active)[0].astype(jnp.bfloat16)
    grad_two = jnp.einsum("tf,df->td", up_low, w_up, preferred_element_type=jnp.float32)
    back_keys, back_values = (key_all, value_all)
    weights_again = jnp.exp(masked_scores(back_keys) - row_max) / row_sum
    grad_weights = jnp.einsum(
        "qhe,khe->hqk", grad_attention_low, back_values, preferred_element_type=jnp.float32
    )
    weighted_sum = jnp.sum(weights_again * grad_weights, axis=-1, keepdims=True)
    grad_scores = (weights_again * (grad_weights - weighted_sum)).astype(jnp.bfloat16)
    grad_query = jnp.einsum(
        "hqk,khe->qhe", grad_scores, back_keys, preferred_element_type=jnp.float32
    ) * HD ** (-0.5)
    grad_keys = jnp.einsum(
        "hqk,qhe->khe", grad_scores, query_low, preferred_element_type=jnp.float32
    ) * HD ** (-0.5)
    grad_values = jnp.einsum(
        "hqk,qhe->khe",
        weights_again.astype(jnp.bfloat16),
        grad_attention_low,
        preferred_element_type=jnp.float32,
    )
    back_key, back_value = (
        partner(
            grad_keys[:row_count].reshape(row_count, model_width).astype(jnp.bfloat16), "shard", 0
        ).astype(jnp.float32),
        partner(
            grad_values[:row_count].reshape(row_count, model_width).astype(jnp.bfloat16), "shard", 0
        ).astype(jnp.float32),
    )
    own_key_grad = grad_keys[row_count:].reshape(row_count, model_width) + back_key
    own_value_grad = grad_values[row_count:].reshape(row_count, model_width) + back_value
    query_pre = query_back(grad_query)[0].reshape(row_count, model_width)
    key_pre = key_back(own_key_grad.reshape(head_shape))[0].reshape(row_count, model_width)
    qkv_low = jnp.concatenate([query_pre, key_pre, own_value_grad], axis=1).astype(jnp.bfloat16)
    grad_one = jnp.einsum("tc,dc->td", qkv_low, w_qkv, preferred_element_type=jnp.float32)
    input_one, gain_one_grad, shift_one_grad = back_one(grad_one)
    input_two, gain_two_grad, shift_two_grad = back_two(grad_two)
    input_grad = grad_out + input_one + input_two
    grad_low_sum = jnp.sum(grad_low.astype(jnp.float32), axis=0)
    vector_grad = jnp.concatenate(
        [
            gain_one_grad,
            shift_one_grad,
            gain_two_grad,
            shift_two_grad,
            jnp.sum(qkv_low.astype(jnp.float32), axis=0),
            grad_low_sum,
            jnp.sum(up_low.astype(jnp.float32), axis=0),
            grad_low_sum,
        ]
    )
    weight_grad = jnp.concatenate(
        [
            jnp.einsum("td,tc->dc", one_low, qkv_low, preferred_element_type=jnp.float32),
            jnp.einsum("td,te->de", attention_low, grad_low, preferred_element_type=jnp.float32),
            jnp.einsum("td,tf->df", two_low, up_low, preferred_element_type=jnp.float32),
            jnp.einsum("te,tf->ef", grad_low, active_low, preferred_element_type=jnp.float32),
        ],
        axis=1,
    )
    spread_vec = vector_grad.reshape(shard_count, data_count, -1).transpose(1, 0, 2).reshape(-1)
    part_weight, part_vector = (
        lax.psum_scatter(weight_grad, "dp", scatter_dimension=1, tiled=True),
        lax.psum_scatter(spread_vec, "dp", scatter_dimension=0, tiled=True),
    )
    part_weight, part_vector = (
        lax.psum_scatter(part_weight, "shard", scatter_dimension=0, tiled=True),
        lax.psum_scatter(part_vector, "shard", scatter_dimension=0, tiled=True),
    )
    own_weight, own_vector = (
        lax.all_gather(part_weight, "dp", axis=1, tiled=True),
        lax.all_gather(part_vector, "dp", axis=0, tiled=True),
    )
    square_sum = jnp.sum(own_weight * own_weight) + jnp.sum(own_vector * own_vector)
    grad_norm = jnp.sqrt(lax.psum(square_sum, "shard"))
    factor = jnp.minimum(1.0, math.sqrt(model_width * stack_width / BS) / grad_norm)
    own_rows = own_weight.shape[0]
    tiles = (own_weight * factor).reshape(own_rows // BS, BS, stack_width // BS, BS)
    new_left = 0.5 * left_stat + 0.5 * jnp.einsum(
        "iajb,icjb->ijac", tiles, tiles, precision=HIGHEST
    )
    new_right = 0.5 * right_stat + 0.5 * jnp.einsum(
        "iajb,iajd->ijbd", tiles, tiles, precision=HIGHEST
    )
    tiles_low = tiles.astype(jnp.bfloat16)
    left_mixed = jnp.einsum(
        "ijac,icjd->iajd", left_root, tiles_low, preferred_element_type=jnp.float32
    ).astype(jnp.bfloat16)
    update = jnp.einsum(
        "iajd,ijdb->iajb", left_mixed, right_root, preferred_element_type=jnp.float32
    ).reshape(own_rows, stack_width)
    new_master = master - LEARN * update
    scaled_vec = own_vector * factor
    new_vstat = 0.5 * vector_stat + 0.5 * scaled_vec * scaled_vec
    new_vectors = vectors - LEARN_VEC * scaled_vec / jnp.sqrt(new_vstat)
    return (
        input_grad,
        grad_norm,
        new_left,
        new_right,
        new_master,
        new_master.astype(jnp.bfloat16),
        new_vectors,
        new_vstat,
    )


def solution(mesh):
    return jax.shard_map(
        body,
        mesh=mesh,
        in_specs=(
            P(("dp", "shard"), None),
            P(("dp", "shard"), None),
            P("dp"),
            P(("dp", "shard")),
            P("shard", None),
            P("shard"),
            P("shard", None, None, None),
            P("shard", None, None, None),
            P("shard", None, None, None),
            P("shard", None, None, None),
            P("shard"),
        ),
        out_specs=(
            P(("dp", "shard"), None),
            P(),
            P("shard", None, None, None),
            P("shard", None, None, None),
            P("shard", None),
            P("shard", None),
            P("shard"),
            P("shard"),
        ),
        check_vma=False,
    )
```

profile of v0, /device:TPU:0, one launch (start us, length us, event | category | flops | bytes accessed | tf_op | source)
XLA Modules:
  0.0 1619.8 jit_solution(14062656077153369523)
XLA Ops:
  7.3 5.0 convert_element_type.116
  12.9 42.6 %psum.14 = f32[]{:T(128)} all-reduce(f32[]{:T(128)} %convert_reduce_fusion.4), channel_id=1, replica_groups=mesh['dp'=4,'shard'=8] {'dp','shard'}, use_global_device_ids=true, to_apply=%region_1.2 | all-reduce | flops 1 | bytes 8 | tf_op jit(solution)/shard_map/psum | solution.py:88
  55.6 10.1 all-gather
  67.4 1.4 convert_reduce_fusion.2
  68.8 2.0 fusion.86
  72.7 1.3 compare_and_fusion
  74.0 67.4 %all-gather.4.cloned.1.call-done = bf16[1024,12288]{1,0:T(8,128)(2,1)} async-done(((bf16[128,12288]{1,0:T(8,128)(2,1)}), bf16[1024,12288]{1,0:T(8,128)(2,1)}) %all-gather.4.cloned.1.call-update) | async-done | bytes 25165840 | tf_op jit(solution)/shard_map/all_gather | solution.py:84
  141.4 6.1 fusion.35
  147.6 1.1 slice.167
  148.7 2.5 fusion.135
  151.5 2.9 copy.67
  154.3 1.5 slice.116
  155.9 1.1 multiply_subtract_fusion
  157.0 1.1 maximum_convert_fusion
  158.4 26.6 %multiply_convert_fusion.1 = (bf16[512,4096]{1,0:T(8,128)(2,1)}, f32[512,4096]{1,0:T(8,128)}, f32[512,4096]{1,0:T(8,128)}) fusion(f32[4096]{0:T(1024)S(1)} %slice.122, bf16[1024,12288]{1,0:T(8,128)(2,1)} %all-gather.4.cloned.1.call-done, bf16[512,1024]{1,0:T(8,128)(2,1)} %param.11, f32[1024]{0:T(1024)S(1)} %get-tuple-element.42, ...), kind=kOutput, calls=%fused_computation.15 | convolution fusion | flops 4436525056 | bytes 30437376 | tf_op jit(solution)/shard_map/dot_general | solution.py:149
  185.0 2.9 copy.66
  187.9 2.4 slice.168
  191.5 3.1 pad_maximum_fusion.2
  194.6 4.4 copy.65
  199.0 17.4 %fusion.104 = f32[16,512,1024]{2,1,0:T(8,128)} fusion(bf16[512,16,64]{0,2,1:T(8,128)(2,1)} %maximum_convert_fusion, bf16[512,16,64]{0,2,1:T(8,128)(2,1)} %bitcast.5, bf16[512,16,48]{0,2,1:T(8,128)(2,1)} %slice.168, bf16[512,16,8]{0,2,1:T(8,128)(2,1)S(1)} %get-tuple-element.35, bf16[512,16,8]{0,2,1:T(8,128)(2,1)S(1)} %get-tuple-element.34), kind=kOutput, calls=%fused_computation.119 | convolution fusion | flops 1081081856 | bytes 36700160 | tf_op jit(solution)/shard_map/qhe,khe->hqk/dot_general | solution.py:131
  216.4 38.1 %fusion.139 = (f32[16,512]{1,0:T(8,128)S(1)}, f32[16,512,1024]{2,1,0:T(8,128)}) fusion(f32[16,512,1024]{2,1,0:T(8,128)} %fusion.104, pred[512,1024]{1,0:T(8,128)(4,1)} %compare_and_fusion), kind=kOutput, calls=%fused_computation.189 | output fusion | flops 50332672 | bytes 67665920 | tf_op jit(solution)/shard_map/sub | solution.py:138
  254.5 15.2 fusion.98
  269.7 3.2 fusion.94
  272.9 12.1 convert_reduce_fusion.3
  286.0 3.9 fusion.101
  289.9 2.3 copy.68
  292.2 14.9 fusion.75
  307.1 22.4 %multiply_reduce_fusion = (f32[16,512]{1,0:T(8,128)S(1)}, f32[16,512,1024]{2,1,0:T(8,128)}) fusion(f32[16,512,1024]{2,1,0:T(8,128)} %get-tuple-element.57, f32[16,512]{1,0:T(8,128)S(1)} %get-tuple-element.56, bf16[512,16,64]{0,2,1:T(8,128)(2,1)S(1)} %bitcast.119, bf16[1024,16,64]{0,2,1:T(8,128)(2,1)S(1)} %bitcast.115), kind=kOutput, calls=%fused_computation.3 | convolution fusion | flops 1098899456 | bytes 70320128 | tf_op jit(solution)/shard_map/qhe,khe->hqk/dot_general | solution.py:168
  329.6 8.1 fusion.141
  337.7 1.1 slice.165
  339.1 27.8 %multiply_convert_fusion = bf16[16,512,1024]{2,1,0:T(8,128)(2,1)} fusion(f32[16,512,1024]{2,1,0:T(8,128)} %get-tuple-element.61, f32[16,512]{1,0:T(8,128)S(1)} %get-tuple-element.60, f32[16,512,1024]{2,1,0:T(8,128)} %get-tuple-element.57, f32[16,512]{1,0:T(8,128)S(1)} %get-tuple-element.56), kind=kLoop, calls=%fused_computation.2 | loop fusion | flops 33554432 | bytes 83951616 | tf_op jit(solution)/shard_map/convert_element_type | solution.py:172
  366.9 9.1 multiply_bitcast_fusion.2
  376.1 1.3 slice.166
  378.4 13.2 convert_reduce_fusion
  391.6 2.0 copy-done.56
  393.6 8.9 fusion.122
  402.5 12.9 multiply_bitcast_fusion.3
  415.5 4.9 fusion.140
  420.4 2.2 slice-done
  422.6 1.7 bitcast_add_fusion.3
  425.1 1.9 slice-done.2
  427.0 1.7 fusion.91
  429.7 9.8 fusion.125
  439.5 33.4 %pad_maximum_fusion = f32[1024,12288]{1,0:T(8,128)} fusion(f32[1024,4096]{1,0:T(8,128)} %fusion.141, f32[1024,4096]{1,0:T(8,128)} %fusion.122, f32[1024,1024]{1,0:T(8,128)} %fusion.140, f32[1024,3072]{1,0:T(8,128)} %fusion.125), kind=kLoop, calls=%fused_computation.1 | loop fusion | flops 37748736 | bytes 100663296 | tf_op jit(solution)/shard_map/concatenate | solution.py:215
  473.0 820.8 %reduce-scatter.3.cloned.1.call-done = f32[1024,3072]{1,0:T(8,128)} async-done(((f32[1024,12288]{1,0:T(8,128)}), f32[1024,3072]{1,0:T(8,128)}) %reduce-scatter.3.cloned.1.call-update) | async-done | bytes 12582928 | tf_op jit(solution)/shard_map/reduce_scatter | solution.py:226
  1293.8 98.3 %reduce-scatter.5.cloned.1.call-done = f32[128,3072]{1,0:T(8,128)} async-done(((f32[1024,3072]{1,0:T(8,128)}), f32[128,3072]{1,0:T(8,128)}) %reduce-scatter.5.cloned.1.call-update) | async-done | bytes 1572880 | tf_op jit(solution)/shard_map/reduce_scatter | solution.py:230
  1395.4 8.5 fusion.19
  1404.0 7.9 fusion.131
  1412.0 2.0 fusion.85
  1415.3 21.6 %all-reduce.7 = f32[13312]{0:T(1024)S(1)} all-reduce(f32[13312]{0:T(1024)S(1)} %reshape.306), channel_id=4, replica_groups=mesh['dp'=4,'shard'=8] {'dp'}, use_global_device_ids=true, to_apply=%region_21.22.clone | all-reduce | flops 13312 | bytes 106496
  1437.0 25.6 %all-reduce.8 = f32[3328]{0:T(1024)S(1)} all-reduce(f32[3328]{0:T(1024)S(1)} %dynamic-slice.2), channel_id=5, replica_groups=mesh['dp'=4,'shard'=8] {'shard'}, use_global_device_ids=true, to_apply=%region_22.23.clone | all-reduce | flops 3328 | bytes 26624
  1462.7 11.3 all-reduce.6
  1474.6 37.0 %all-gather.6.cloned.1.call-done = f32[128,12288]{1,0:T(8,128)} async-done(((f32[128,3072]{1,0:T(8,128)}), f32[128,12288]{1,0:T(8,128)}) %all-gather.6.cloned.1.call-update) | async-done | bytes 6291472 | tf_op jit(solution)/shard_map/all_gather | solution.py:234
  1511.6 5.0 multiply_reduce_fusion.1
  1517.9 4.8 add_add_fusion.2
  1522.7 14.5 psum.15
  1537.9 6.6 multiply_bitcast_fusion.1
  1544.5 3.8 copy.83
  1548.3 6.6 copy.73
  1554.9 18.9 %fusion.28 = f32[1,96,128,128]{3,2,1,0:T(8,128)} fusion(f32[1,96,128,128]{3,2,1,0:T(8,128)} %param.17, f32[16,96,8,128]{3,2,1,0:T(8,128)} %get-tuple-element.27), kind=kOutput, calls=%fused_computation.48 | convolution fusion | flops 2419064832 | bytes 18874368 | tf_op jit(solution)/shard_map/iajb,icjb->ijac/dot_general | solution.py:242
  1573.8 11.7 fusion.27
  1585.5 9.7 broadcast_multiply_fusion
  1595.2 6.6 copy.78
  1601.8 9.3 fusion.133
  (177 shorter events, 13.3 us)
Async XLA Ops:
  7.2 1578.3 %copy-start = (bf16[1,96,128,128]{3,2,1,0:T(8,128)(2,1)S(1)}, bf16[1,96,128,128]{3,2,1,0:T(8,128)(2,1)}, u32[]{:S(2)}) copy-start(bf16[1,96,128,128]{3,2,1,0:T(8,128)(2,1)} %param.20) | copy-start | bytes 9437188
  7.2 5.1 copy-start.45
  7.2 48.3 %copy-start.36 = (f32[1664]{0:T(1024)S(1)}, f32[1664]{0:T(1024)}, u32[]{:S(2)}) copy-start(f32[1664]{0:T(1024)} %param.16) | copy-start | bytes 19972
  7.2 134.2 %all-gather.4.cloned.1.call-start = ((), (), s32[]{:S(2)}) async-start(), calls=%async_computation.2 | async-start | bytes 28311552 | tf_op jit(solution)/shard_map/all_gather | solution.py:84
  12.3 1281.5 %reduce-scatter.3.cloned.1.call-start = ((), (), s32[]{:S(2)}) async-start(), calls=%async_computation.3 | async-start | bytes 62914560 | tf_op jit(solution)/shard_map/reduce_scatter | solution.py:226
  65.7 92.7 %copy-start.42 = (f32[4096]{0:T(1024)}, f32[4096]{0:T(1024)S(1)}, u32[]{:S(2)}) copy-start(f32[4096]{0:T(1024)S(1)} %slice.122) | copy-start | bytes 49156
  68.8 89.6 %copy-start.34 = (f32[512]{0:T(512)}, f32[512]{0:T(512)S(1)}, u32[]{:S(2)}) copy-start(f32[512]{0:T(512)S(1)} %broadcast_multiply_fusion.1) | copy-start | bytes 6148
  71.4 87.0 %copy-start.38 = (f32[512]{0:T(512)}, f32[512]{0:T(512)S(1)}, u32[]{:S(2)}) copy-start(f32[512]{0:T(512)S(1)} %fusion.115) | copy-start | bytes 6148
  72.6 75.0 %copy-start.32 = (f32[1024]{0:T(1024)}, f32[1024]{0:T(1024)S(1)}, u32[]{:S(2)}) copy-start(f32[1024]{0:T(1024)S(1)} %get-tuple-element.45) | copy-start | bytes 12292
  72.6 75.0 %copy-start.47 = (f32[1024]{0:T(1024)}, f32[1024]{0:T(1024)S(1)}, u32[]{:S(2)}) copy-start(f32[1024]{0:T(1024)S(1)} %get-tuple-element.44) | copy-start | bytes 12292
  72.6 85.8 %copy-start.30 = (f32[1024]{0:T(1024)}, f32[1024]{0:T(1024)S(1)}, u32[]{:S(2)}) copy-start(f32[1024]{0:T(1024)S(1)} %get-tuple-element.43) | copy-start | bytes 12292
  72.6 85.8 %copy-start.49 = (f32[1024]{0:T(1024)}, f32[1024]{0:T(1024)S(1)}, u32[]{:S(2)}) copy-start(f32[1024]{0:T(1024)S(1)} %get-tuple-element.42) | copy-start | bytes 12292
  72.7 117.6 %copy-start.26 = (f32[512,8]{0,1:T(8,128)}, f32[512,8]{0,1:T(8,128)S(1)}, u32[]{:S(2)}) copy-start(f32[512,8]{0,1:T(8,128)S(1)} %get-tuple-element.50) | copy-start | bytes 49156
  72.7 117.6 %copy-start.28 = (f32[512,8]{0,1:T(8,128)}, f32[512,8]{0,1:T(8,128)S(1)}, u32[]{:S(2)}) copy-start(f32[512,8]{0,1:T(8,128)S(1)} %get-tuple-element.51) | copy-start | bytes 49156
  151.2 40.2 %collective-permute-start = (bf16[512,1024]{1,0:T(8,128)(2,1)}, bf16[512,1024]{1,0:T(8,128)(2,1)}, u32[]{:S(2)}, u32[]{:S(2)}) collective-permute-start(bf16[512,1024]{1,0:T(8,128)(2,1)} %slice.167), channel_id=1, source_target_pairs={{0,1},{1,0},{2,3},{3,2},{4,5},{5,4},{6,7},{7,6},{8,9},{9,8},{10,11... | collective-permute-start | bytes 3145736 | tf_op jit(solution)/shard_map/ppermute | solution.py:22
  158.1 40.8 %collective-permute-start.1 = (bf16[512,1024]{0,1:T(8,128)(2,1)}, bf16[512,1024]{0,1:T(8,128)(2,1)}, u32[]{:S(2)}, u32[]{:S(2)}) collective-permute-start(bf16[512,1024]{0,1:T(8,128)(2,1)} %bitcast.4), channel_id=1, source_target_pairs={{0,1},{1,0},{2,3},{3,2},{4,5},{5,4},{6,7},{7,6},{8,9},{9,8},{10,11... | collective-permute-start | bytes 3145736 | tf_op jit(solution)/shard_map/ppermute | solution.py:22
  191.4 24.9 %copy-start.18 = (bf16[512,16,8]{0,2,1:T(8,128)(2,1)}, bf16[512,16,8]{0,2,1:T(8,128)(2,1)S(1)}, u32[]{:S(2)}) copy-start(bf16[512,16,8]{0,2,1:T(8,128)(2,1)S(1)} %get-tuple-element.34) | copy-start | bytes 393220
  191.4 24.9 %copy-start.20 = (bf16[512,16,8]{0,2,1:T(8,128)(2,1)}, bf16[512,16,8]{0,2,1:T(8,128)(2,1)S(1)}, u32[]{:S(2)}) copy-start(bf16[512,16,8]{0,2,1:T(8,128)(2,1)S(1)} %get-tuple-element.35) | copy-start | bytes 393220
  254.5 18.4 %copy-start.51 = (f32[1024]{0:T(1024)S(1)}, f32[1024]{0:T(1024)}, u32[]{:S(2)}) copy-start(f32[1024]{0:T(1024)} %get-tuple-element.40) | copy-start | bytes 12292
  254.5 18.4 %copy-start.52 = (f32[1024]{0:T(1024)S(1)}, f32[1024]{0:T(1024)}, u32[]{:S(2)}) copy-start(f32[1024]{0:T(1024)} %get-tuple-element.41) | copy-start | bytes 12292
  254.5 18.4 %copy-start.54 = (f32[512]{0:T(512)S(1)}, f32[512]{0:T(512)}, u32[]{:S(2)}) copy-start(f32[512]{0:T(512)} %convert_multiply_fusion) | copy-start | bytes 6148
  292.2 14.9 copy-start.17
  292.2 14.9 copy-start.22
  307.1 22.5 %copy-start.16 = (bf16[512,4096]{1,0:T(8,128)(2,1)S(1)}, bf16[512,4096]{1,0:T(8,128)(2,1)}, u32[]{:S(2)}) copy-start(bf16[512,4096]{1,0:T(8,128)(2,1)} %get-tuple-element.24) | copy-start | bytes 12582916
  307.1 22.5 %copy-start.24 = (bf16[512,1024]{1,0:T(8,128)(2,1)S(1)}, bf16[512,1024]{1,0:T(8,128)(2,1)}, u32[]{:S(2)}) copy-start(bf16[512,1024]{1,0:T(8,128)(2,1)} %copy-done.23) | copy-start | bytes 3145732
  329.6 8.2 copy-start.7
  338.9 86.2 %collective-permute-start.3 = (bf16[512,1024]{0,1:T(8,128)(2,1)}, bf16[512,1024]{0,1:T(8,128)(2,1)}, u32[]{:S(2)}, u32[]{:S(2)}) collective-permute-start(bf16[512,1024]{0,1:T(8,128)(2,1)} %bitcast.18), channel_id=1, source_target_pairs={{0,1},{1,0},{2,3},{3,2},{4,5},{5,4},{6,7},{7,6},{8,9},{9,8},{10,11... | collective-permute-start | bytes 3145736 | tf_op jit(solution)/shard_map/ppermute | solution.py:22
  339.1 27.8 %copy-start.19 = (bf16[512,16,8]{0,2,1:T(8,128)(2,1)S(1)}, bf16[512,16,8]{0,2,1:T(8,128)(2,1)}, u32[]{:S(2)}) copy-start(bf16[512,16,8]{0,2,1:T(8,128)(2,1)} %copy-done.18) | copy-start | bytes 393220
  339.1 27.8 %copy-start.21 = (bf16[512,16,8]{0,2,1:T(8,128)(2,1)S(1)}, bf16[512,16,8]{0,2,1:T(8,128)(2,1)}, u32[]{:S(2)}) copy-start(bf16[512,16,8]{0,2,1:T(8,128)(2,1)} %copy-done.20) | copy-start | bytes 393220
  366.9 11.5 copy-start.25
  366.9 11.5 copy-start.43
  376.1 2.3 copy-start.5
  377.4 43.0 %collective-permute-start.2 = (bf16[512,1024]{0,1:T(8,128)(2,1)}, bf16[512,1024]{0,1:T(8,128)(2,1)}, u32[]{:S(2)}, u32[]{:S(2)}) collective-permute-start(bf16[512,1024]{0,1:T(8,128)(2,1)} %bitcast.13), channel_id=1, source_target_pairs={{0,1},{1,0},{2,3},{3,2},{4,5},{5,4},{6,7},{7,6},{8,9},{9,8},{10,11... | collective-permute-start | bytes 3145736 | tf_op jit(solution)/shard_map/ppermute | solution.py:22
  378.4 15.2 copy-start.2
  378.4 15.2 copy-start.31
  378.4 15.2 copy-start.35
  378.4 15.2 copy-start.39
  378.4 15.2 copy-start.50
  420.3 2.3 slice-start
  420.3 4.2 copy-start.6
  420.3 4.2 copy-start.27
  420.3 4.2 copy-start.29
  420.3 4.6 slice-start.1
  424.3 2.7 slice-start.2
  424.5 5.2 copy-start.3
  424.6 5.2 copy-start.33
  424.6 5.2 copy-start.48
  424.9 3.8 copy-start.10
  425.1 3.7 copy-start.12
  472.9 919.2 %reduce-scatter.5.cloned.1.call-start = ((), (), s32[]{:S(2)}) async-start(), calls=%async_computation.4 | async-start | bytes 14155776 | tf_op jit(solution)/shard_map/reduce_scatter | solution.py:230
  1293.8 98.4 %copy-start.55 = (u32[32]{0:T(128)S(1)}, u32[32]{0:T(128)}, u32[]{:S(2)}) copy-start(u32[32]{0:T(128)} %constant.199) | copy-start | bytes 388
  1293.8 99.0 %copy-start.53 = (u32[32]{0:T(128)S(1)}, u32[32]{0:T(128)}, u32[]{:S(2)}) copy-start(u32[32]{0:T(128)} %constant.189) | copy-start | bytes 388
  1293.8 217.8 %all-gather.6.cloned.1.call-start = ((), (), s32[]{:S(2)}) async-start(), calls=%async_computation.5 | async-start | bytes 7864320 | tf_op jit(solution)/shard_map/all_gather | solution.py:234
  1395.3 8.6 copy-start.4
  1395.3 8.6 copy-start.11
  1395.4 8.6 copy-start.13
  1395.4 8.6 copy-start.15
  1404.0 8.0 copy-start.8
  1404.0 8.0 copy-start.41
  1411.9 2.0 copy-start.9
  1411.9 3.1 copy-start.44
  1554.9 18.9 %copy-start.1 = (f32[128,96,128]{0,2,1:T(8,128)S(1)}, f32[128,96,128]{0,2,1:T(8,128)}, u32[]{:S(2)}) copy-start(f32[128,96,128]{0,2,1:T(8,128)} %copy.73) | copy-start | bytes 18874372
  1601.8 9.3 copy-start.37
  1601.8 9.3 copy-start.46
  (4 other events, 4.6 us)
Sparse Core Ops, SparseCore 0:
  12.4 129.0 all-gather.3
  473.1 820.6 reduce-scatter.2
  1297.7 94.4 reduce-scatter.4
  1393.7 117.8 all-gather.5
where the time goes:
time: 1630 us; the launch traced here: 1620 us
  waiting for transfers between devices  1020 us (63%)
  matrix products  245 us (15%)
  other arithmetic  151 us (9%)
  blocking collectives  126 us (8%)
  local copies, waits for them, and re-layouts  52.4 us (3%)
  between operations  20.9 us (1%)
    reduce_scatter x1, waiting for transfers between devices, body(): lax.psum_scatter(weight_grad, 'dp', scatter_dimension=1, tiled=True)  821 us
    reduce_scatter x1, waiting for transfers between devices, body(): lax.psum_scatter(part_weight, 'shard', scatter_dimension=0, tiled=True)  98.3 us
    all_gather x1, waiting for transfers between devices, body(): lax.all_gather(master.astype(jnp.bfloat16), 'shard', axis=0, tiled=True)  67.4 us
    unnamed x3, blocking collectives  58.4 us
    psum x1, blocking collectives, body(): valid_total = lax.psum(jnp.sum(valid_float), ('dp', 'shard'))  42.6 us
    sub x1, other arithmetic, body(): exponent = jnp.exp(scores - row_max)  38.1 us
    all_gather x1, waiting for transfers between devices, body(): lax.all_gather(part_weight, 'dp', axis=1, tiled=True)  37 us
    concatenate x1, other arithmetic, body(): jnp.concatenate([jnp.einsum('td,tc->dc', one_low, qkv_low, preferred_elem...  33.4 us
  transfers between devices with their start and end apart: 8, of which 4 were waited for; matrix products, arithmetic and copies ran while one was open for 10% of the time, Pallas kernels for 0%

commit v1 on v0

v1 whole, which is shorter than its diff:
```python
from functools import partial
import math

import jax
import jax.numpy as jnp
from jax import lax
from jax.experimental import pallas as pl
from jax.experimental.pallas import tpu as pltpu
from jax.sharding import PartitionSpec as P

HD = 64
ROT = 16
BS = 128
LANES = 128
EPS = 1e-05
NEG = -1e30
BIG = 3e38
LEARN = 0.5
LEARN_VEC = 0.15
F32 = jnp.float32
BF16 = jnp.bfloat16
MIB = 1 << 20


def dot(a, b, dims=((1,), (0,))):
    return lax.dot_general(a, b, (dims, ((), ())), preferred_element_type=F32)


def dot_nt(a, b):
    return dot(a, b, ((1,), (1,)))


def call(kernel, grid, in_specs, out_specs, out_shape, scratch=(), vmem=48, prefetch=0, cost=None):
    return pl.pallas_call(
        kernel,
        out_shape=out_shape,
        grid_spec=pltpu.PrefetchScalarGridSpec(
            num_scalar_prefetch=prefetch,
            grid=grid,
            in_specs=in_specs,
            out_specs=out_specs,
            scratch_shapes=list(scratch),
        ),
        compiler_params=pltpu.CompilerParams(
            vmem_limit_bytes=vmem * MIB, dimension_semantics=("arbitrary",) * len(grid)
        ),
        cost_estimate=cost,
    )


def cost(flops, nbytes, trans=0):
    return pl.CostEstimate(flops=int(flops), bytes_accessed=int(nbytes), transcendentals=int(trans))


def whole(shape):
    rank = len(shape)
    return pl.BlockSpec(shape, lambda *g: (0,) * rank)


def sds(shape, dtype):
    return jax.ShapeDtypeStruct(shape, dtype)


def normed(x):
    mean = jnp.mean(x, axis=-1, keepdims=True)
    centred = x - mean
    rstd = lax.rsqrt(jnp.mean(centred * centred, axis=-1, keepdims=True) + EPS)
    return centred * rstd, rstd


def turn(values, c, lo, hi):
    return values * c + pltpu.roll(values, LANES - ROT // 2, 1) * lo + pltpu.roll(values, ROT // 2, 1) * hi


def pre_kernel(x_ref, vec_ref, w_ref, b_ref, c_ref, lo_ref, hi_ref, n1t_ref, n2_ref, n2t_ref, q_ref, kv_ref, n1_ref):
    j = pl.program_id(0)
    rows, width = x_ref.shape
    step = 128

    @pl.when(j == 0)
    def _():
        def chunk(i, carry):
            at = pl.ds(pl.multiple_of(i * step, step), step)
            xh, _ = normed(x_ref[at, :].astype(F32))
            one = (xh * vec_ref[0:1, :] + vec_ref[1:2, :]).astype(BF16)
            two = (xh * vec_ref[2:3, :] + vec_ref[3:4, :]).astype(BF16)
            n1_ref[at, :] = one
            n2_ref[at, :] = two
            n1t_ref[:, at] = one.T
            n2t_ref[:, at] = two.T
            return carry

        lax.fori_loop(0, rows // step, chunk, 0)

    cols = w_ref.shape[1]
    proj = dot(n1_ref[...], w_ref[...]) + b_ref[...]

    def emit(out, turned):
        for g in range(cols // LANES):
            part = proj[:, g * LANES : (g + 1) * LANES]
            if turned:
                part = turn(part, c_ref[...], lo_ref[...], hi_ref[...])
            out[:, g * LANES : (g + 1) * LANES] = part.astype(BF16)

    nq = width // cols

    @pl.when(j < nq)
    def _():
        emit(q_ref, True)

    @pl.when((j >= nq) & (j < 2 * nq))
    def _():
        emit(kv_ref, True)

    @pl.when(j >= 2 * nq)
    def _():
        emit(kv_ref, False)


def pre(x, vec4, w, b, tables):
    rows, width = x.shape
    cols = 512
    steps = 3 * width // cols
    nq = width // cols
    return call(
        pre_kernel,
        (steps,),
        [
            whole((rows, width)),
            whole(vec4.shape),
            pl.BlockSpec((width, cols), lambda j: (0, j)),
            pl.BlockSpec((1, cols), lambda j: (0, j)),
            whole((rows, LANES)),
            whole((rows, LANES)),
            whole((rows, LANES)),
        ],
        [
            whole((width, rows)),
            whole((rows, width)),
            whole((width, rows)),
            pl.BlockSpec((rows, cols), lambda j: (0, jnp.minimum(j, nq - 1))),
            pl.BlockSpec((rows, cols), lambda j: (0, jnp.maximum(j - nq, 0))),
        ],
        [
            sds((width, rows), BF16),
            sds((rows, width), BF16),
            sds((width, rows), BF16),
            sds((rows, width), BF16),
            sds((rows, 2 * width), BF16),
        ],
        [pltpu.VMEM((rows, width), BF16)],
        cost=cost(6 * rows * width * width, 2 * (3 * width * width + 7 * rows * width)),
    )(x, vec4, w, b, *tables)


def place_keys(own_ref, other_ref, out_ref, parity):
    half = own_ref.shape[0] // 2
    for ref, who in ((own_ref, parity), (other_ref, 1 - parity)):
        for b in range(2):
            quarter = who if b == 0 else 3 - who
            out_ref[pl.ds(pl.multiple_of(quarter * half, half), half), :] = ref[b * half : (b + 1) * half, :]


def att_fwd_kernel(par_ref, q_ref, k_ref, v_ref, ko_ref, vo_ref, qseg_ref, kseg_ref, o_ref, ot_ref, lse_ref, mask, kpos, vpos, sc):
    rows = q_ref.shape[0]
    half = rows // 2
    parity = par_ref[0]
    lane = lax.broadcasted_iota(jnp.int32, (half, LANES), 1)

    @pl.when(pl.program_id(0) == 0)
    def _():
        for b in range(2):
            quarter = parity if b == 0 else 3 - parity

            def one(j, carry):
                qpos = quarter * half + lax.broadcasted_iota(jnp.int32, (half, half), 0)
                kpos_ = j * half + lax.broadcasted_iota(jnp.int32, (half, half), 1)
                same = qseg_ref[b * half : (b + 1) * half, :] == kseg_ref[pl.ds(j, 1), :]
                mask[b, j] = jnp.where((kpos_ <= qpos) & same, BIG, NEG)
                return carry

            lax.fori_loop(0, 4, one, 0)
        for j in range(4):
            vpos[j * half : (j + 1) * half, LANES:] = jnp.ones((half, LANES), BF16)

    place_keys(k_ref, ko_ref, kpos, parity)
    place_keys(v_ref, vo_ref, vpos.at[:, 0:LANES], parity)
    for b in range(2):
        quarter = parity if b == 0 else 3 - parity
        at = slice(b * half, (b + 1) * half)
        both = q_ref[at, :] * jnp.asarray(HD**-0.5, BF16)
        outs = []
        for h in range(2):
            mine = (lane < HD) if h == 0 else (lane >= HD)
            qh = jnp.where(mine, both, jnp.zeros_like(both))

            def score(j, top):
                keys = kpos[pl.ds(pl.multiple_of(j * half, half), half), :]
                s = jnp.minimum(dot_nt(qh, keys), mask[b, j])
                sc[j] = s
                for g in range(half // LANES):
                    top = jnp.maximum(top, s[:, g * LANES : (g + 1) * LANES])
                return top

            top = lax.fori_loop(0, quarter + 1, score, jnp.full((half, LANES), NEG, F32))
            top = jnp.broadcast_to(jnp.max(top, axis=1, keepdims=True), (half, LANES))
            top_wide = jnp.concatenate([top] * (half // LANES), axis=1)

            def weigh(j, acc):
                p = jnp.exp(sc[j] - top_wide).astype(BF16)
                return acc + dot(p, vpos[pl.ds(pl.multiple_of(j * half, half), half), :])

            acc = lax.fori_loop(0, quarter + 1, weigh, jnp.zeros((half, 2 * LANES), F32))
            den = acc[:, LANES:]
            outs.append(acc[:, :LANES] / den)
            lse = top + jnp.log(den)
            lse_ref[0, h : h + 1, at] = lse.T[0:1, :]
        out = jnp.where(lane < HD, outs[0], outs[1]).astype(BF16)
        o_ref[at, :] = out
        ot_ref[0, :, at] = out.T


def att_fwd(parity, q, kv, kvo, qseg, kseg):
    rows, width = q.shape
    pairs = width // LANES
    half = rows // 2
    col = lambda off: pl.BlockSpec((rows, LANES), lambda p, r: (0, p + off))
    return call(
        att_fwd_kernel,
        (pairs,),
        [col(0), col(0), col(pairs), col(0), col(pairs), whole((rows, 1)), whole((4, half))],
        [
            col(0),
            pl.BlockSpec((1, LANES, rows), lambda p, r: (p, 0, 0)),
            pl.BlockSpec((1, 2, rows), lambda p, r: (p, 0, 0)),
        ],
        [sds((rows, width), BF16), sds((pairs, LANES, rows), BF16), sds((pairs, 2, rows), F32)],
        [
            pltpu.VMEM((2, 4, half, half), F32),
            pltpu.VMEM((2 * rows, LANES), BF16),
            pltpu.VMEM((2 * rows, 2 * LANES), BF16),
            pltpu.VMEM((4, half, half), F32),
        ],
        prefetch=1,
        cost=cost(4 * rows * 2 * rows * width, 2 * 8 * rows * width, 2 * rows * rows * width // HD),
    )(parity, q, kv, kv, kvo, kvo, qseg, kseg)


def att_bwd_kernel(
    par_ref, q_ref, k_ref, v_ref, ko_ref, vo_ref, g_ref, o_ref, lse_ref, qseg_ref, kseg_ref, c_ref, lo_ref, hi_ref,
    dq_ref, dk_ref, dv_ref, dko_ref, dvo_ref, mask, kpos, vpos, dkpos, dvpos,
):
    rows = q_ref.shape[0]
    half = rows // 2
    parity = par_ref[0]
    lane = lax.broadcasted_iota(jnp.int32, (half, LANES), 1)
    lane_k = lane

    @pl.when(pl.program_id(0) == 0)
    def _():
        for b in range(2):
            quarter = parity if b == 0 else 3 - parity

            def one(j, carry):
                kp = j * half + lax.broadcasted_iota(jnp.int32, (half, half), 0)
                qp = quarter * half + lax.broadcasted_iota(jnp.int32, (half, half), 1)
                same = kseg_ref[pl.ds(pl.multiple_of(j * half, half), half), :] == qseg_ref[b : b + 1, :]
                mask[b, j] = jnp.where((kp <= qp) & same, BIG, NEG)
                return carry

            lax.fori_loop(0, 4, one, 0)

    place_keys(k_ref, ko_ref, kpos, parity)
    place_keys(v_ref, vo_ref, vpos, parity)
    dkpos[...] = jnp.zeros_like(dkpos)
    dvpos[...] = jnp.zeros_like(dvpos)
    scale = HD**-0.5
    for b in range(2):
        quarter = parity if b == 0 else 3 - parity
        at = slice(b * half, (b + 1) * half)
        qs = q_ref[at, :] * jnp.asarray(scale, BF16)
        gs = g_ref[at, :]
        prod = (gs.astype(F32) * o_ref[at, :].astype(F32)).T
        zero = jnp.zeros_like(qs)
        parts = []
        for h in range(2):
            mine = (lane < HD) if h == 0 else (lane >= HD)
            qh = jnp.where(mine, qs, zero)
            gh = jnp.where(mine, gs, zero)
            lse = lse_ref[0, h : h + 1, at]
            delta = jnp.sum(prod[h * HD : (h + 1) * HD, :], axis=0, keepdims=True)

            def tile(j, acc):
                ks = pl.ds(pl.multiple_of(j * half, half), half)
                keys = kpos[ks, :]
                s = jnp.minimum(dot_nt(keys, qh), mask[b, j])
                p = jnp.exp(s - lse)
                dp = dot_nt(vpos[ks, :], gh)
                ds = (p * (dp - delta)).astype(BF16)
                dvpos[ks, :] += dot(p.astype(BF16), gh)
                dkpos[ks, :] += dot(ds, qh)
                return acc + dot(ds, keys, ((0,), (0,)))

            parts.append(lax.fori_loop(0, quarter + 1, tile, jnp.zeros((half, LANES), F32)))
        dq = jnp.where(lane < HD, parts[0], parts[1]) * scale
        dq_ref[at, :] = turn(dq, c_ref[at, :], -lo_ref[at, :], -hi_ref[at, :]).astype(BF16)
    for src, mine, theirs in ((dkpos, dk_ref, dko_ref), (dvpos, dv_ref, dvo_ref)):
        for b in range(2):
            at = slice(b * half, (b + 1) * half)
            own = parity if b == 0 else 3 - parity
            other = 1 - parity if b == 0 else 2 + parity
            mine[at, :] = src[pl.ds(pl.multiple_of(own * half, half), half), :].astype(mine.dtype)
            theirs[at, :] = src[pl.ds(pl.multiple_of(other * half, half), half), :].astype(BF16)


def att_bwd(parity, q, kv, kvo, gob, ob, lse, qseg, kseg, tables):
    rows, width = q.shape
    pairs = width // LANES
    half = rows // 2
    col = lambda off: pl.BlockSpec((rows, LANES), lambda p, r: (0, p + off))
    out = sds((rows, width), F32)
    low = sds((rows, width), BF16)
    return call(
        att_bwd_kernel,
        (pairs,),
        [
            col(0), col(0), col(pairs), col(0), col(pairs), col(0), col(0),
            pl.BlockSpec((1, 2, rows), lambda p, r: (p, 0, 0)),
            whole((2, half)), whole((2 * rows, 1)),
            whole((rows, LANES)), whole((rows, LANES)), whole((rows, LANES)),
        ],
        [col(0)] * 5,
        [low, out, out, low, low],
        [
            pltpu.VMEM((2, 4, half, half), F32),
            pltpu.VMEM((2 * rows, LANES), BF16),
            pltpu.VMEM((2 * rows, LANES), BF16),
            pltpu.VMEM((2 * rows, LANES), F32),
            pltpu.VMEM((2 * rows, LANES), F32),
        ],
        prefetch=1,
        cost=cost(10 * rows * 2 * rows * width, 2 * 16 * rows * width, 2 * rows * rows * width // HD),
    )(parity, q, kv, kv, kvo, kvo, gob, ob, lse, qseg, kseg, *tables)


def up_kernel(n2_ref, w_ref, b_ref, h_ref, dg_ref):
    u_all = dot(n2_ref[...], w_ref[...]) + b_ref[...]
    for g in range(u_all.shape[1] // LANES):
        at = slice(g * LANES, (g + 1) * LANES)
        u = u_all[:, at]
        cdf = 0.5 * (1.0 + lax.erf(u * (1.0 / math.sqrt(2.0))))
        h_ref[:, at] = (u * cdf).astype(BF16)
        pdf = jnp.exp(-0.5 * u * u) * (1.0 / math.sqrt(2.0 * math.pi))
        dg_ref[:, at] = (cdf + u * pdf).astype(BF16)


def up(n2, w, b):
    rows, width = n2.shape
    hidden = w.shape[1]
    cols = 512
    blk = pl.BlockSpec((rows, cols), lambda j: (0, j))
    return call(
        up_kernel,
        (hidden // cols,),
        [whole((rows, width)), pl.BlockSpec((width, cols), lambda j: (0, j)), pl.BlockSpec((1, cols), lambda j: (0, j))],
        [blk, blk],
        [sds((rows, hidden), BF16), sds((rows, hidden), BF16)],
        cost=cost(2 * rows * width * hidden, 2 * (width * hidden + 2 * rows * hidden), 2 * rows * hidden),
    )(n2, w, b)


def out_kernel(ob_ref, hb_ref, wo_ref, wd_ref, bo_ref, bd_ref, x_ref, t_ref, valid_ref, gy_ref, gb_ref, gbt_ref, sum_ref):
    branch = dot(ob_ref[...], wo_ref[...]) + bo_ref[...]
    feed = dot_nt(hb_ref[...], wd_ref[...]) + bd_ref[...]
    y = x_ref[...].astype(F32) + (branch + feed)
    g = valid_ref[...] * (y - t_ref[...].astype(F32))
    low = g.astype(BF16)
    gy_ref[...] = g
    gb_ref[...] = low
    gbt_ref[...] = low.T
    sum_ref[...] = jnp.sum(low.astype(F32), axis=0, keepdims=True)


def out_grad(ob, hb, wo, wd, bo, bd, x, t, valid):
    rows, width = ob.shape
    hidden = hb.shape[1]
    cols = 256
    col = pl.BlockSpec((rows, cols), lambda j: (0, j))
    vec = pl.BlockSpec((1, cols), lambda j: (0, j))
    return call(
        out_kernel,
        (width // cols,),
        [
            whole((rows, width)), whole((rows, hidden)),
            pl.BlockSpec((width, cols), lambda j: (0, j)), pl.BlockSpec((cols, hidden), lambda j: (j, 0)),
            vec, vec, col, col, whole((rows, 1)),
        ],
        [col, col, pl.BlockSpec((cols, rows), lambda j: (j, 0)), vec],
        [sds((rows, width), F32), sds((rows, width), BF16), sds((width, rows), BF16), sds((1, width), F32)],
        cost=cost(2 * rows * width * (width + hidden), 2 * (width * (width + hidden) + 6 * rows * width)),
    )(ob, hb, wo, wd, bo, bd, x, t, valid)


def dgrad_kernel(gb_ref, wo_ref, wd_ref, wu_ref, dg_ref, gob_ref, gub_ref, sum_ref, gn2_ref):
    @pl.when(pl.program_id(0) == 0)
    def _():
        gob_ref[...] = dot_nt(gb_ref[...], wo_ref[...]).astype(BF16)
        gn2_ref[...] = jnp.zeros_like(gn2_ref)

    act = dot(gb_ref[...], wd_ref[...])
    gub = (act * dg_ref[...].astype(F32)).astype(BF16)
    gub_ref[...] = gub
    sum_ref[...] = jnp.sum(gub.astype(F32), axis=0, keepdims=True)
    gn2_ref[...] += dot_nt(gub, wu_ref[...])


def dgrad(gb, wo, wd, wu, dg):
    rows, width = gb.shape
    hidden = dg.shape[1]
    cols = 512
    blk = pl.BlockSpec((rows, cols), lambda j: (0, j))
    wblk = pl.BlockSpec((width, cols), lambda j: (0, j))
    return call(
        dgrad_kernel,
        (hidden // cols,),
        [whole((rows, width)), whole((width, width)), wblk, wblk, blk],
        [whole((rows, width)), blk, pl.BlockSpec((1, cols), lambda j: (0, j)), whole((rows, width))],
        [sds((rows, width), BF16), sds((rows, hidden), BF16), sds((1, hidden), F32), sds((rows, width), F32)],
        cost=cost(2 * rows * width * (width + 2 * hidden), 2 * (width * (width + 2 * hidden) + 6 * rows * width)),
    )(gb, wo, wd, wu, dg)


def last_kernel(
    dq_ref, dk_ref, dv_ref, dko_ref, dvo_ref, c_ref, lo_ref, hi_ref, w_ref, x_ref, vec_ref, gn2_ref, gy_ref, scale_ref,
    gqkv_ref, in_ref, vg_ref, sum_ref, gn1,
):
    j = pl.program_id(0)
    rows, width = x_ref.shape
    cols = w_ref.shape[1]
    nq = width // cols

    @pl.when(j == 0)
    def _():
        gn1[...] = jnp.zeros_like(gn1)

    @pl.when(j < nq)
    def _():
        gqkv_ref[...] = dq_ref[...]

    @pl.when((j >= nq) & (j < 2 * nq))
    def _():
        for g in range(cols // LANES):
            at = slice(g * LANES, (g + 1) * LANES)
            grad = dk_ref[:, at] + dko_ref[:, at].astype(F32)
            gqkv_ref[:, at] = turn(grad, c_ref[...], -lo_ref[...], -hi_ref[...]).astype(BF16)

    @pl.when(j >= 2 * nq)
    def _():
        gqkv_ref[...] = (dv_ref[...] + dvo_ref[...].astype(F32)).astype(BF16)

    low = gqkv_ref[...]
    sum_ref[...] = jnp.sum(low.astype(F32), axis=0, keepdims=True)
    gn1[...] += dot_nt(low, w_ref[...])

    @pl.when(j == 3 * nq - 1)
    def _():
        step = 64
        vg_ref[...] = jnp.zeros_like(vg_ref)
        scale = scale_ref[0, 0]

        def chunk(i, carry):
            at = pl.ds(pl.multiple_of(i * step, step), step)
            xh, rstd = normed(x_ref[at, :].astype(F32))
            total = gy_ref[at, :]
            sums = []
            for g_n, gain in ((gn1[at, :], vec_ref[0:1, :]), (gn2_ref[at, :], vec_ref[2:3, :])):
                sums.append(jnp.sum(g_n * xh, axis=0, keepdims=True))
                sums.append(jnp.sum(g_n, axis=0, keepdims=True))
                e = g_n * gain
                mean = jnp.mean(e, axis=-1, keepdims=True)
                along = jnp.mean(e * xh, axis=-1, keepdims=True)
                total = total + rstd * (e - mean - xh * along)
            in_ref[at, :] = total * scale
            vg_ref[...] += jnp.concatenate(sums, axis=0)
            return carry

        lax.fori_loop(0, rows // step, chunk, 0)


def last(dq, dk, dv, dko, dvo, tables, w, x, vec4, gn2, gy, scale):
    rows, width = x.shape
    cols = 512
    nq = width // cols
    at = lambda lo: pl.BlockSpec((rows, cols), lambda j: (0, jnp.clip(j - lo * nq, 0, nq - 1)))
    return call(
        last_kernel,
        (3 * nq,),
        [
            at(0), at(1), at(2), at(1), at(2),
            whole((rows, LANES)), whole((rows, LANES)), whole((rows, LANES)),
            pl.BlockSpec((width, cols), lambda j: (0, j)),
            whole((rows, width)), whole(vec4.shape), whole((rows, width)), whole((rows, width)),
            pl.BlockSpec(memory_space=pltpu.SMEM),
        ],
        [
            pl.BlockSpec((rows, cols), lambda j: (0, j)), whole((rows, width)), whole((4, width)),
            pl.BlockSpec((1, cols), lambda j: (0, j)),
        ],
        [sds((rows, 3 * width), BF16), sds((rows, width), F32), sds((4, width), F32), sds((1, 3 * width), F32)],
        [pltpu.VMEM((rows, width), F32)],
        cost=cost(6 * rows * width * width, 2 * (3 * width * width + 20 * rows * width)),
    )(dq, dk, dv, dko, dvo, *tables, w, x, vec4, gn2, gy, scale)


def wgrad_kernel(core_ref, a_ref, ao_ref, b_ref, bo_ref, out_ref):
    blocks, size = a_ref.shape[0], a_ref.shape[2]
    tokens = a_ref.shape[3]
    a = a_ref[...].reshape(blocks * size, tokens)
    ao = ao_ref[...].reshape(blocks * size, tokens)
    out_ref[...] = (dot(a, b_ref[...]) + dot(ao, bo_ref[...])).astype(BF16)


def wgrad(core, at_own, at_other, b_own, b_other):
    width, tokens = at_own.shape
    blocks = width // (2 * BS)
    total = b_own.shape[1]
    cols = 512
    return call(
        wgrad_kernel,
        (total // cols,),
        [
            pl.BlockSpec((blocks, 1, BS, tokens), lambda j, c: (0, c[0], 0, 0)),
            whole((blocks, 1, BS, tokens)),
            pl.BlockSpec((tokens, cols), lambda j, c: (0, j)),
            pl.BlockSpec((tokens, cols), lambda j, c: (0, j)),
        ],
        pl.BlockSpec((blocks * BS, cols), lambda j, c: (0, j)),
        sds((blocks * BS, total), BF16),
        prefetch=1,
        cost=cost(2 * tokens * width * total, 2 * total * (2 * tokens + width // 2)),
    )(core, at_own.reshape(blocks, 2, BS, tokens), at_other, b_own, b_other)


def update_kernel(f_ref, g_ref, ls_ref, rs_ref, lr_ref, rr_ref, m_ref, nl_ref, nr_ref, nm_ref, mc_ref):
    factor = f_ref[0, 0]
    half_sq = 0.5 * factor * factor
    for k in range(ls_ref.shape[1]):
        at = slice(k * BS, (k + 1) * BS)
        g = g_ref[:, at]
        gt = g.T
        nl_ref[0, k] = 0.5 * ls_ref[0, k] + half_sq * dot(g, gt)
        nr_ref[0, k] = 0.5 * rs_ref[0, k] + half_sq * dot(gt, g)
        tb = (g.astype(F32) * factor).astype(BF16)
        mb = dot(lr_ref[0, k], tb).astype(BF16)
        new = m_ref[:, at] - LEARN * dot(mb, rr_ref[0, k])
        nm_ref[:, at] = new
        mc_ref[:, at] = new.astype(BF16)


def update(factor, g, ls, rs, lr, rr, m):
    rows, total = g.shape
    count = ls.shape[1]
    per = 8
    blk = pl.BlockSpec((1, per, BS, BS), lambda j: (0, j, 0, 0))
    col = pl.BlockSpec((rows, per * BS), lambda j: (0, j))
    return call(
        update_kernel,
        (count // per,),
        [pl.BlockSpec(memory_space=pltpu.SMEM), col, blk, blk, blk, blk, col],
        [blk, blk, col, col],
        [sds(ls.shape, F32), sds(rs.shape, F32), sds(m.shape, F32), sds(m.shape, BF16)],
        cost=cost(8 * rows * total * BS, rows * total * 32),
    )(factor, g, ls, rs, lr, rr, m)


def angles(positions):
    half_rot = ROT // 2
    frequency = jnp.power(10000.0, -2.0 * jnp.arange(half_rot, dtype=F32) / ROT)
    grid = positions.astype(F32)[:, None] * frequency[None, :]
    cosine, sine = jnp.cos(grid), jnp.sin(grid)
    rows = positions.shape[0]
    ones = jnp.ones((rows, HD - ROT), F32)
    zero = jnp.zeros((rows, HD - ROT), F32)
    blank = jnp.zeros((rows, half_rot), F32)
    c = jnp.concatenate([cosine, cosine, ones] * 2, axis=1)
    lo = jnp.concatenate([-sine, blank, zero] * 2, axis=1)
    hi = jnp.concatenate([blank, sine, zero] * 2, axis=1)
    return c, lo, hi


def body(
    tokens, targets, segments, valid, master, vectors, left_stat, right_stat, left_root, right_root, vector_stat,
):
    rows, width = tokens.shape
    stack = master.shape[1]
    hidden = (stack - 4 * width) // 2
    half = rows // 2
    shards = lax.axis_size("shard")
    replicas = lax.axis_size("dp")
    index = lax.axis_index("shard")
    parity = index % 2
    par = parity.astype(jnp.int32).reshape(1)
    swap = [(i, i ^ 1) for i in range(shards)]
    groups = [[i for i in range(shards) if i % 2 == c] for c in range(2)]

    low = master.astype(BF16)
    w_qkv = lax.all_gather(low[:, : 3 * width], "shard", axis=0, tiled=True)
    w_rest = lax.all_gather(low[:, 3 * width :], "shard", axis=0, tiled=True)
    params = lax.all_gather(vectors.astype(BF16), "shard", axis=0, tiled=True).astype(F32)
    w_out = w_rest[:, :width]
    w_up = w_rest[:, width : width + hidden]
    w_down = w_rest[:, width + hidden :]

    vec4 = params[: 4 * width].reshape(4, width)
    b_qkv = params[4 * width : 7 * width].reshape(1, -1)
    b_out = params[7 * width : 8 * width].reshape(1, -1)
    b_up = params[8 * width : 8 * width + hidden].reshape(1, -1)
    b_down = params[8 * width + hidden :].reshape(1, -1)

    valid_float = valid.astype(F32)
    count = lax.psum(lax.psum(jnp.sum(valid_float), "shard"), "dp")
    scale = rows * shards * replicas / count

    local = jnp.arange(half, dtype=jnp.int32)
    positions = jnp.concatenate([parity * half + local, (3 - parity) * half + local])
    tables = angles(positions)
    start = (index - parity) * rows
    sequence = lax.dynamic_slice_in_dim(segments, start, 2 * rows).reshape(4, half)
    key_seg = jnp.stack([sequence[0], sequence[2], sequence[3], sequence[1]])
    own_seg = lax.dynamic_slice_in_dim(segments, index * rows, rows)

    n1t, n2, n2t, q, kv = pre(tokens, vec4, w_qkv, b_qkv, tables)
    kvo = lax.ppermute(kv, "shard", swap)
    hb, dg = up(n2, w_up, b_up)
    ob, obt, lse = att_fwd(par, q, kv, kvo, own_seg.reshape(rows, 1), key_seg)
    obt = obt.reshape(width, rows)
    gy, gb, gbt, gb_sum = out_grad(
        ob, hb, w_out, w_down, b_out, b_down, tokens, targets, valid_float.reshape(rows, 1)
    )
    gob, gub, gub_sum, gn2 = dgrad(gb, w_out, w_down, w_up, dg)

    other = 1 - parity
    pick = lambda a: lax.dynamic_slice_in_dim(a.reshape(-1, 2, BS, rows), other, 1, axis=1)
    hb_o, gb_o, gub_o, gbt_o, obt_o, n2t_o, n1t_o = (
        lax.ppermute(a, "shard", swap) for a in (hb, gb, gub, pick(gbt), pick(obt), pick(n2t), pick(n1t))
    )
    dw_down = wgrad(par, gbt, gbt_o, hb, hb_o)
    dw_out = wgrad(par, obt, obt_o, gb, gb_o)
    dw_up = wgrad(par, n2t, n2t_o, gub, gub_o)

    def reduce(part):
        part = lax.psum_scatter(part, "shard", scatter_dimension=0, axis_index_groups=groups, tiled=True)
        part = lax.psum_scatter(part, "dp", scatter_dimension=1, tiled=True)
        return lax.all_gather(part, "dp", axis=1, tiled=True)

    g_down, g_out, g_up = reduce(dw_down), reduce(dw_out), reduce(dw_up)

    dq, dk, dv, dk_o, dv_o = att_bwd(
        par, q, kv, kvo, gob, ob, lse, own_seg.reshape(2, half), key_seg.reshape(2 * rows, 1), tables
    )
    dk_r = lax.ppermute(dk_o, "shard", swap)
    dv_r = lax.ppermute(dv_o, "shard", swap)
    gqkv, input_grad, vec_grad, gqkv_sum = last(
        dq, dk, dv, dk_r, dv_r, tables, w_qkv, tokens, vec4, gn2, gy, scale.reshape(1, 1)
    )
    gqkv_o = lax.ppermute(gqkv, "shard", swap)
    g_qkv = reduce(wgrad(par, n1t, n1t_o, gqkv, gqkv_o))

    vector_grad = jnp.concatenate(
        [vec_grad.reshape(-1), gqkv_sum.reshape(-1), gb_sum.reshape(-1), gub_sum.reshape(-1), gb_sum.reshape(-1)]
    )
    vector_grad = lax.psum(lax.psum(vector_grad, "shard"), "dp")
    own_len = vectors.shape[0]
    own_vector = lax.dynamic_slice_in_dim(vector_grad, index * own_len, own_len)

    grads = jnp.concatenate([g_qkv, g_out, g_up, g_down], axis=1)
    square_sum = jnp.sum(jnp.square(grads.astype(F32))) + jnp.sum(own_vector * own_vector)
    grad_norm = scale * jnp.sqrt(lax.psum(square_sum, "shard"))
    factor = scale * jnp.minimum(1.0, math.sqrt(width * stack / BS) / grad_norm)
    new_left, new_right, new_master, master_copy = update(
        factor.reshape(1, 1), grads, left_stat, right_stat, left_root, right_root, master
    )
    scaled_vec = own_vector * factor
    new_vstat = 0.5 * vector_stat + 0.5 * scaled_vec * scaled_vec
    new_vectors = vectors - LEARN_VEC * scaled_vec / jnp.sqrt(new_vstat)
    return (input_grad, grad_norm, new_left, new_right, new_master, master_copy, new_vectors, new_vstat)


def solution(mesh):
    rows = P(("dp", "shard"), None)
    quad = P("shard", None, None, None)
    return jax.shard_map(
        body,
        mesh=mesh,
        in_specs=(
            rows, rows, P("dp"), P(("dp", "shard")), P("shard", None), P("shard"), quad, quad, quad, quad, P("shard"),
        ),
        out_specs=(rows, P(), quad, quad, P("shard", None), P("shard", None), P("shard"), P("shard")),
        check_vma=False,
    )
```

time: 1630 us -> 666 us (0.41)
  waiting for transfers between devices: 1020 us -> 237 us
  matrix products: 245 us -> 0 us
  Pallas kernels: 0 us -> 209 us
  other arithmetic: 151 us -> 8.44 us
    reduce_scatter x2 -> x8, waiting for transfers between devices: 919 us -> 119 us  [the longest x4 61.2 us: reduce(): lax.psum_scatter(part, 'shard', scatter_dimension=0, axis_index_groups=gr...]
    dot_general x21 -> x0, matrix products: 245 us -> none  [the longest x1 26.6 us: body(): jnp.dot(two_low, w_up, preferred_element_type=jnp.float32) + bias_up]
    pallas_call x0 -> x12, Pallas kernels: none -> 209 us  [the longest x1 49.1 us: att_bwd(): call(att_bwd_kernel, (pairs,), [col(0), col(0), col(pairs), col(0), col(p...]
    unnamed x3 -> x0, blocking collectives: 58.4 us -> none
    all_gather x1 -> x3, blocking collectives: 10.1 us -> 52.2 us  [the longest x2 41.5 us: reduce(): return lax.all_gather(part, 'dp', axis=1, tiled=True)]
    convert_element_type x7 -> x5, other arithmetic: 43.3 us -> 3.23 us  [the longest x1 3.16 us: body(): low = master.astype(BF16)]
    sub x2 -> x0, other arithmetic: 39.2 us -> none  [the longest x1 38.1 us: body(): exponent = jnp.exp(scores - row_max)]
    concatenate x3 -> x0, other arithmetic: 36.6 us -> none  [the longest x1 33.4 us: body(): jnp.concatenate([jnp.einsum('td,tc->dc', one_low, qkv_low, preferred_elem...]
  transfers between devices with their start and end apart: 8 -> 23, of which waited for: 4 -> 12; matrix products, arithmetic and copies ran while one was open for 10% -> 2% of each run, Pallas kernels for 0% -> 21%
where the time goes in v1:
time: 666 us; the launch traced here: 664 us
  waiting for transfers between devices  237 us (36%)
  Pallas kernels  209 us (31%)
  blocking collectives  137 us (21%)
  local copies, waits for them, and re-layouts  50.5 us (8%)
  between operations  18.6 us (3%)
  other arithmetic  8.44 us (1%)
    reduce_scatter x4, waiting for transfers between devices, reduce(): lax.psum_scatter(part, 'shard', scatter_dimension=0, axis_index_groups=gr...  61.2 us
    reduce_scatter x4, waiting for transfers between devices, reduce(): part = lax.psum_scatter(part, 'dp', scatter_dimension=1, tiled=True)  57.5 us
    pallas_call x1, Pallas kernels, att_bwd(): call(att_bwd_kernel, (pairs,), [col(0), col(0), col(pairs), col(0), col(p...  49.1 us
    psum x2, blocking collectives, body(): vector_grad = lax.psum(lax.psum(vector_grad, 'shard'), 'dp')  44.2 us
    pallas_call x1, Pallas kernels, att_fwd(): call(att_fwd_kernel, (pairs,), [col(0), col(0), col(pairs), col(0), col(p...  43.5 us
    all_gather x2, blocking collectives, reduce(): return lax.all_gather(part, 'dp', axis=1, tiled=True)  41.5 us
    all_gather x1, waiting for transfers between devices, body(): w_rest = lax.all_gather(low[:, 3 * width:], 'shard', axis=0, tiled=True)  33.8 us
    all_gather x1, waiting for transfers between devices, body(): w_qkv = lax.all_gather(low[:, :3 * width], 'shard', axis=0, tiled=True)  33.4 us
  transfers between devices with their start and end apart: 23, of which 12 were waited for; matrix products, arithmetic and copies ran while one was open for 2% of the time, Pallas kernels for 21%

profile of v1, /device:TPU:0, one launch (start us, length us, event | category | flops | bytes accessed | tf_op | source)
XLA Modules:
  0.0 663.8 jit_solution(2451391924492666216)
XLA Ops:
  7.2 3.2 convert_element_type.24
  10.4 0.9 slice.84
  11.4 1.6 slice.86
  13.1 10.6 %all-gather = bf16[8,1,1664]{2,1,0:T(2,128)(2,1)S(1)} all-gather(bf16[1,1,1664]{2,1,0:T(2,128)(2,1)S(1)} %reshape.124), channel_id=1, replica_groups=mesh['dp'=4,'shard'=8] {'shard'}, dimensions={0}, use_global_device_ids=true | all-gather | bytes 29952 | tf_op jit(solution)/shard_map/all_gather | solution.py:609
  23.9 1.0 multiply_sine_fusion
  26.3 33.4 %all-gather.6.cloned.1.call-done.w_ref = bf16[1024,3072]{1,0:T(8,128)(2,1)} async-done(((bf16[128,3072]{1,0:T(8,128)(2,1)}), bf16[1024,3072]{1,0:T(8,128)(2,1)}) %all-gather.6.cloned.1.call-update) | async-done | bytes 6291472 | tf_op jit(solution)/shard_map/all_gather | solution.py:607
  59.7 11.7 %shard_map.170 = (bf16[1024,512]{1,0:T(8,128)(2,1)S(1)}, bf16[512,1024]{1,0:T(8,128)(2,1)S(1)}, bf16[1024,512]{1,0:T(8,128)(2,1)S(1)}, bf16[512,1024]{1,0:T(8,128)(2,1)S(1)}, bf16[512,2048]{1,0:T(8,128)(2,1)}) custom-call(bf16[512,1024]{1,0:T(8,128)(2,1)S(1)} %copy-done.3, f32[4,1024]{1,0:T(4,128)S(1)} %slice.65.vec_ref, ...), custom_call_target="tpu_custom_call" | custom-call | flops 3221225472 | bytes 13631488 | tf_op jit(solution)/shard_map/pallas_call | solution.py:125
  71.4 1.0 copy-done.8
  72.4 1.0 copy-done.10
  73.4 1.0 copy-done.19
  74.4 1.0 copy-done.22
  75.6 0.8 dynamic_slice.21
  76.4 0.8 dynamic_slice.22
  77.5 2.3 collective-permute-done.ko_ref.vo_ref
  79.9 1.6 copy-done.15
  81.4 1.2 copy-done.20
  82.7 43.5 %shard_map.171 = (bf16[512,1024]{1,0:T(8,128)(2,1)S(1)}, bf16[8,128,512]{2,1,0:T(8,128)(2,1)S(1)}, f32[8,2,512]{2,1,0:T(2,128)S(1)}) custom-call(s32[1]{0:T(128)} %bitcast.par_ref.core_ref, bf16[512,1024]{1,0:T(8,128)(2,1)S(1)} %copy-done.20, bf16[512,2048]{1,0:T(8,128)(2,1)S(1)} %copy-done.15, bf16[512,2048]{1,0:T(8,128)(2,1)S(1)} %copy-done.15, ...), custom_call_target="tpu_custom_call" | custom-call | flops 2147483648 | bytes 8388608 | tf_op jit(solution)/shard_map/pallas_call | solution.py:228
  126.2 1.0 copy-done.17
  127.2 33.8 %all-gather.8.cloned.1.call-done = bf16[1024,9216]{1,0:T(8,128)(2,1)} async-done(((bf16[128,9216]{1,0:T(8,128)(2,1)}), bf16[1024,9216]{1,0:T(8,128)(2,1)}) %all-gather.8.cloned.1.call-update) | async-done | bytes 18874384 | tf_op jit(solution)/shard_map/all_gather | solution.py:608
  161.0 12.0 %fusion.4 = (bf16[1024,4096]{1,0:T(8,128)(2,1)}, bf16[1024,4096]{1,0:T(8,128)(2,1)}) fusion(bf16[1024,9216]{1,0:T(8,128)(2,1)} %all-gather.8.cloned.1.call-done), kind=kLoop, calls=%fused_computation.28 | loop fusion | bytes 33554432 | tf_op jit(solution)/shard_map/slice | solution.py:612
  172.9 12.1 %shard_map.172 = (bf16[512,4096]{1,0:T(8,128)(2,1)S(1)}, bf16[512,4096]{1,0:T(8,128)(2,1)}) custom-call(bf16[512,1024]{1,0:T(8,128)(2,1)S(1)} %copy-done.23, bf16[1024,4096]{1,0:T(8,128)(2,1)} %get-tuple-element.73.w_ref.wu_ref, f32[1,4096]{1,0:T(1,128)S(1)} %bitcast.42), custom_call_target="tpu_custom_call" | custom-call | flops 4294967296 | bytes 16777216 | tf_op jit(solution)/shard_map/pallas_call | solution.py:362
  185.1 4.6 slice.89.wo_ref
  189.7 10.8 %shard_map.173 = (f32[512,1024]{1,0:T(8,128)}, bf16[512,1024]{1,0:T(8,128)(2,1)S(1)}, bf16[1024,512]{1,0:T(8,128)(2,1)S(1)}, f32[1,1024]{1,0:T(1,128)S(1)}) custom-call(bf16[512,1024]{1,0:T(8,128)(2,1)S(1)} %copy-done.18, bf16[512,4096]{1,0:T(8,128)(2,1)} %copy-done.14, bf16[1024,1024]{1,0:T(8,128)(2,1)} %slice.89.wo_ref, ...), custom_call_target="tpu_custom_call" | custom-call | flops 5368709120 | bytes 16777216 | tf_op jit(solution)/shard_map/pallas_call | solution.py:390
  200.5 1.0 copy-done.12
  201.5 16.5 %shard_map.174 = (bf16[512,1024]{1,0:T(8,128)(2,1)S(1)}, bf16[512,4096]{1,0:T(8,128)(2,1)}, f32[1,4096]{1,0:T(1,128)S(1)}, f32[512,1024]{1,0:T(8,128)S(1)}) custom-call(bf16[512,1024]{1,0:T(8,128)(2,1)S(1)} %get-tuple-element.44.gb_ref.b_ref, bf16[1024,1024]{1,0:T(8,128)(2,1)} %slice.89.wo_ref, bf16[1024,4096]{1,0:T(8,128)(2,1)} %get-tuple-element.72.wd_ref, ...), custom_call_target="tpu_custom_call" | custom-call | flops 9663676416 | bytes 25165824 | tf_op jit(solution)/shard_map/pallas_call | solution.py:423
  218.0 1.4 copy-done.2
  219.4 1.0 copy-done.24
  220.6 1.1 constant_dynamic-slice_fusion.1
  222.0 6.3 collective-permute-done.7.ao_ref
  228.2 1.2 copy-done.11
  229.5 8.8 %shard_map.179 = bf16[512,4096]{1,0:T(8,128)(2,1)S(1)} custom-call(s32[1]{0:T(128)} %bitcast.par_ref.core_ref, bf16[4,2,128,512]{3,2,1,0:T(8,128)(2,1)S(1)} %bitcast.35, bf16[4,1,128,512]{3,2,1,0:T(8,128)(2,1)S(1)} %collective-permute-done.7.ao_ref, bf16[512,4096]{1,0:T(8,128)(2,1)} %get-tuple-element.60.b_ref, bf16[512,4096]{1,0:T(8,128)(2,1)} %collective-permute-done.8.bo_ref), custom_call_target="tpu_custom_call" | custom-call | flops 4294967296 | bytes 12582912 | tf_op jit(solution)/shard_map/pallas_call | solution.py:528
  238.3 2.0 copy-done
  240.7 1.1 constant_dynamic-slice_fusion
  242.1 6.3 collective-permute-done.9.ao_ref
  248.3 2.0 copy-done.28
  250.3 1.2 copy-done.13
  251.6 8.9 %shard_map.180 = bf16[512,4096]{1,0:T(8,128)(2,1)S(1)} custom-call(s32[1]{0:T(128)} %bitcast.par_ref.core_ref, bf16[4,2,128,512]{3,2,1,0:T(8,128)(2,1)S(1)} %bitcast.37, bf16[4,1,128,512]{3,2,1,0:T(8,128)(2,1)S(1)} %collective-permute-done.9.ao_ref, bf16[512,4096]{1,0:T(8,128)(2,1)} %copy-done.14, bf16[512,4096]{1,0:T(8,128)(2,1)} %copy-done.28), custom_call_target="tpu_custom_call" | custom-call | flops 4294967296 | bytes 12582912 | tf_op jit(solution)/shard_map/pallas_call | solution.py:528
  260.5 2.0 copy-done.1
  262.9 1.2 copy-done.21
  264.1 49.1 %shard_map.175 = (bf16[512,1024]{1,0:T(8,128)(2,1)S(1)}, f32[512,1024]{1,0:T(8,128)}, f32[512,1024]{1,0:T(8,128)}, bf16[512,1024]{1,0:T(8,128)(2,1)}, bf16[512,1024]{1,0:T(8,128)(2,1)}) custom-call(s32[1]{0:T(128)} %bitcast.par_ref.core_ref, bf16[512,1024]{1,0:T(8,128)(2,1)S(1)} %copy-done.21, bf16[512,2048]{1,0:T(8,128)(2,1)} %get-tuple-element.40.k_ref.v_ref, ...), custom_call_target="tpu_custom_call" | custom-call | flops 5368709120 | bytes 16777216 | tf_op jit(solution)/shard_map/pallas_call | solution.py:323
  313.2 1.0 copy-done.6
  315.3 13.9 %psum.35 = f32[]{:T(128)} all-reduce(f32[]{:T(128)} %convert_reduce_fusion), channel_id=1, replica_groups=mesh['dp'=4,'shard'=8] {'shard'}, use_global_device_ids=true, to_apply=%region_1.2 | all-reduce | flops 1 | bytes 8 | tf_op jit(solution)/shard_map/psum | solution.py:621
  329.2 12.3 %psum.36 = f32[]{:T(128)} all-reduce(f32[]{:T(128)} %psum.35), channel_id=1, replica_groups=mesh['dp'=4,'shard'=8] {'dp'}, use_global_device_ids=true, to_apply=%region_2.3 | all-reduce | flops 1 | bytes 8 | tf_op jit(solution)/shard_map/psum | solution.py:621
  342.2 1.2 copy-done.7
  343.5 16.8 %shard_map.176 = (bf16[512,3072]{1,0:T(8,128)(2,1)}, f32[512,1024]{1,0:T(8,128)}, f32[4,1024]{1,0:T(4,128)S(1)}, f32[1,3072]{1,0:T(1,128)S(1)}) custom-call(bf16[512,1024]{1,0:T(8,128)(2,1)S(1)} %copy-done.7, f32[512,1024]{1,0:T(8,128)} %get-tuple-element.49.dk_ref, f32[512,1024]{1,0:T(8,128)} %get-tuple-element.50.dv_ref, ...), custom_call_target="tpu_custom_call" | custom-call | flops 3221225472 | bytes 27262976 | tf_op jit(solution)/shard_map/pallas_call | solution.py:495
  360.9 6.8 %collective-permute-done.5.ao_ref = bf16[4,1,128,512]{3,2,1,0:T(8,128)(2,1)S(1)} collective-permute-done((bf16[4,1,128,512]{3,2,1,0:T(8,128)(2,1)S(1)}, bf16[4,1,128,512]{3,2,1,0:T(8,128)(2,1)S(1)}, u32[]{:S(2)}, u32[]{:S(2)}) %collective-permute-start.5) | collective-permute-done | bytes 524320 | tf_op jit(solution)/shard_map/ppermute | solution.py:645
  367.8 2.5 shard_map.178
  370.9 1.5 collective-permute-done.3.ao_ref
  372.4 7.9 %shard_map.177 = bf16[512,3072]{1,0:T(8,128)(2,1)} custom-call(s32[1]{0:T(128)} %bitcast.par_ref.core_ref, bf16[4,2,128,512]{3,2,1,0:T(8,128)(2,1)S(1)} %bitcast.33, bf16[4,1,128,512]{3,2,1,0:T(8,128)(2,1)S(1)} %collective-permute-done.3.ao_ref, bf16[512,3072]{1,0:T(8,128)(2,1)} %get-tuple-element.57.b_ref, bf16[512,3072]{1,0:T(8,128)(2,1)} %collective-permute-done.4.bo_ref), custom_call_target="tpu_custom_call" | custom-call | flops 3221225472 | bytes 9437184 | tf_op jit(solution)/shard_map/pallas_call | solution.py:528
  381.9 13.5 %reduce-scatter.13.cloned.1.call-done = bf16[128,1024]{1,0:T(8,128)(2,1)} async-done(((bf16[512,1024]{1,0:T(8,128)(2,1)}), bf16[128,1024]{1,0:T(8,128)(2,1)}) %reduce-scatter.13.cloned.1.call-update) | async-done | bytes 262160 | tf_op jit(solution)/shard_map/reduce_scatter | solution.py:652
  395.5 47.6 %reduce-scatter.9.cloned.1.call-done = bf16[128,3072]{1,0:T(8,128)(2,1)} async-done(((bf16[512,3072]{1,0:T(8,128)(2,1)}), bf16[128,3072]{1,0:T(8,128)(2,1)}) %reduce-scatter.9.cloned.1.call-update) | async-done | bytes 786448 | tf_op jit(solution)/shard_map/reduce_scatter | solution.py:652
  443.1 29.5 %reduce-scatter.19.cloned.1.call-done = bf16[128,1024]{1,0:T(8,128)(2,1)} async-done(((bf16[128,4096]{1,0:T(8,128)(2,1)}), bf16[128,1024]{1,0:T(8,128)(2,1)}) %reduce-scatter.19.cloned.1.call-update) | async-done | bytes 262160 | tf_op jit(solution)/shard_map/reduce_scatter | solution.py:653
  472.7 28.0 %reduce-scatter.23.cloned.1.call-done = bf16[128,1024]{1,0:T(8,128)(2,1)} async-done(((bf16[128,4096]{1,0:T(8,128)(2,1)}), bf16[128,1024]{1,0:T(8,128)(2,1)}) %reduce-scatter.23.cloned.1.call-update) | async-done | bytes 262160 | tf_op jit(solution)/shard_map/reduce_scatter | solution.py:653
  500.8 24.3 %psum.37 = f32[13312]{0:T(1024)S(1)} all-reduce(f32[13312]{0:T(1024)S(1)} %constant_dynamic-update-slice_fusion.6), channel_id=1, replica_groups=mesh['dp'=4,'shard'=8] {'shard'}, use_global_device_ids=true, to_apply=%region_12.13 | all-reduce | flops 13312 | bytes 106496 | tf_op jit(solution)/shard_map/psum | solution.py:672
  525.1 19.9 %psum.38 = f32[13312]{0:T(1024)S(1)} all-reduce(f32[13312]{0:T(1024)S(1)} %psum.37), channel_id=1, replica_groups=mesh['dp'=4,'shard'=8] {'dp'}, use_global_device_ids=true, to_apply=%region_13.14 | all-reduce | flops 13312 | bytes 106496 | tf_op jit(solution)/shard_map/psum | solution.py:672
  545.7 15.4 %all_gather.25 = bf16[128,1024]{1,0:T(8,128)(2,1)S(1)} all-gather(bf16[128,256]{1,0:T(8,128)(2,1)} %reduce-scatter.15.cloned.1.call-done), channel_id=1, replica_groups=mesh['dp'=4,'shard'=8] {'dp'}, dimensions={1}, use_global_device_ids=true | all-gather | bytes 327680 | tf_op jit(solution)/shard_map/all_gather | solution.py:654
  561.0 26.2 %all_gather.24 = bf16[128,3072]{1,0:T(8,128)(2,1)S(1)} all-gather(bf16[128,768]{1,0:T(8,128)(2,1)} %reduce-scatter.11.cloned.1.call-done), channel_id=1, replica_groups=mesh['dp'=4,'shard'=8] {'dp'}, dimensions={1}, use_global_device_ids=true | all-gather | bytes 983040 | tf_op jit(solution)/shard_map/all_gather | solution.py:654
  587.3 1.3 constant_dynamic-update-slice_fusion.1
  588.6 26.6 %all-gather.12.cloned.1.call-done = bf16[128,4096]{1,0:T(8,128)(2,1)} async-done(((bf16[128,1024]{1,0:T(8,128)(2,1)}), bf16[128,4096]{1,0:T(8,128)(2,1)}) %all-gather.12.cloned.1.call-update) | async-done | bytes 1048592 | tf_op jit(solution)/shard_map/all_gather | solution.py:654
  615.2 1.3 constant_dynamic-update-slice_fusion.g_ref
  616.5 2.2 multiply_reduce_fusion
  620.0 14.0 %psum.39 = f32[]{:T(128)} all-reduce(f32[]{:T(128)S(6)} %add.74), channel_id=1, replica_groups=mesh['dp'=4,'shard'=8] {'shard'}, use_global_device_ids=true, to_apply=%region_15.16 | all-reduce | flops 1 | bytes 8 | tf_op jit(solution)/shard_map/psum | solution.py:678
  634.7 0.7 multiply_subtract_fusion
  635.4 20.5 %shard_map.181 = (f32[1,96,128,128]{3,2,1,0:T(8,128)}, f32[1,96,128,128]{3,2,1,0:T(8,128)}, f32[128,12288]{1,0:T(8,128)}, bf16[128,12288]{1,0:T(8,128)(2,1)}) custom-call(f32[1,1]{1,0:T(1,128)} %bitcast.20.f_ref, bf16[128,12288]{1,0:T(8,128)(2,1)S(1)} %constant_dynamic-update-slice_fusion.g_ref, f32[1,96,128,128]{3,2,1,0:T(8,128)} %ls_ref.1, ...), custom_call_target="tpu_custom_call" | custom-call | flops 1610612736 | bytes 50331648 | tf_op jit(solution)/shard_map/pallas_call | solution.py:566
  (121 shorter events, 8.7 us)
Async XLA Ops:
  7.2 52.6 %all-gather.6.cloned.1.call-start = ((), (), s32[]{:S(2)}) async-start(), calls=%async_computation.8 | async-start | bytes 7077888 | tf_op jit(solution)/shard_map/all_gather | solution.py:607
  11.3 1.8 copy-start.25
  11.4 149.6 %all-gather.8.cloned.1.call-start = ((), (), s32[]{:S(2)}) async-start(), calls=%async_computation.9 | async-start | bytes 21233664 | tf_op jit(solution)/shard_map/all_gather | solution.py:608
  13.0 367.3 %reduce-scatter.17.cloned.1.call-start = ((), (), s32[]{:S(2)}) async-start(), calls=%async_computation.14 | async-start | bytes 5242880 | tf_op jit(solution)/shard_map/reduce_scatter | solution.py:652
  24.9 34.8 %copy-start.3 = (bf16[512,1024]{1,0:T(8,128)(2,1)S(1)}, bf16[512,1024]{1,0:T(8,128)(2,1)}, u32[]{:S(2)}) copy-start(bf16[512,1024]{1,0:T(8,128)(2,1)} %x_ref.5) | copy-start | bytes 3145732
  59.7 15.9 %copy-start.26 = (s32[512]{0:T(512)S(1)}, s32[512]{0:T(512)}, u32[]{:S(2)}) copy-start(s32[512]{0:T(512)} %param.14) | copy-start | bytes 6148
  71.4 1.0 copy-start.8
  72.4 1.0 copy-start.10
  73.4 1.0 copy-start.19
  74.4 1.0 copy-start.22
  75.4 4.5 collective-permute-start
  79.9 1.6 copy-start.15
  81.4 1.2 copy-start.20
  126.2 1.0 copy-start.17
  161.0 12.0 %copy-start.23 = (bf16[512,1024]{1,0:T(8,128)(2,1)S(1)}, bf16[512,1024]{1,0:T(8,128)(2,1)}, u32[]{:S(2)}) copy-start(bf16[512,1024]{1,0:T(8,128)(2,1)} %copy-done.22) | copy-start | bytes 3145732
  185.0 4.7 copy-start.14
  185.0 4.7 copy-start.16
  185.0 4.7 copy-start.18
  200.5 1.0 copy-start.12
  201.5 16.5 %copy-start.4 = (bf16[512,1024]{1,0:T(8,128)(2,1)}, bf16[512,1024]{1,0:T(8,128)(2,1)S(1)}, u32[]{:S(2)}) copy-start(bf16[512,1024]{1,0:T(8,128)(2,1)S(1)} %get-tuple-element.44.gb_ref.b_ref) | copy-start | bytes 3145732
  218.0 1.4 copy-start.2
  219.4 1.0 copy-start.24
  220.3 7.9 %collective-permute-start.8 = (bf16[512,4096]{1,0:T(8,128)(2,1)}, bf16[512,4096]{1,0:T(8,128)(2,1)}, u32[]{:S(2)}, u32[]{:S(2)}) collective-permute-start(bf16[512,4096]{1,0:T(8,128)(2,1)} %get-tuple-element.60.b_ref), channel_id=1, source_target_pairs={{0,1},{1,0},{2,3},{3,2},{4,5},{5,4},{6,7},{7,6},{8,9},{9,8},{10,11... | collective-permute-start | bytes 12582920 | tf_op jit(solution)/shard_map/ppermute | solution.py:645
  221.7 6.6 collective-permute-start.7
  228.2 1.2 copy-start.11
  238.3 2.0 copy-start
  240.3 140.8 %reduce-scatter.21.cloned.1.call-start = ((), (), s32[]{:S(2)}) async-start(), calls=%async_computation.17 | async-start | bytes 5242880 | tf_op jit(solution)/shard_map/reduce_scatter | solution.py:652
  240.3 8.0 %collective-permute-start.10 = (bf16[512,4096]{1,0:T(8,128)(2,1)}, bf16[512,4096]{1,0:T(8,128)(2,1)S(1)}, u32[]{:S(2)}, u32[]{:S(2)}) collective-permute-start(bf16[512,4096]{1,0:T(8,128)(2,1)} %copy-done.14), channel_id=1, source_target_pairs={{0,1},{1,0},{2,3},{3,2},{4,5},{5,4},{6,7},{7,6},{8,9},{9,8},{10,11... | collective-permute-start | bytes 12582920 | tf_op jit(solution)/shard_map/ppermute | solution.py:645
  241.7 6.6 collective-permute-start.9
  248.3 2.0 copy-start.28
  250.3 1.2 copy-start.13
  260.5 2.0 copy-start.1
  262.5 132.9 %reduce-scatter.13.cloned.1.call-start = ((), (), s32[]{:S(2)}) async-start(), calls=%async_computation.12 | async-start | bytes 1310720 | tf_op jit(solution)/shard_map/reduce_scatter | solution.py:652
  262.9 1.2 copy-start.21
  313.2 1.0 copy-start.6
  314.2 28.0 %collective-permute-start.1 = (bf16[512,1024]{1,0:T(8,128)(2,1)}, bf16[512,1024]{1,0:T(8,128)(2,1)}, u32[]{:S(2)}, u32[]{:S(2)}) collective-permute-start(bf16[512,1024]{1,0:T(8,128)(2,1)} %get-tuple-element.51), channel_id=1, source_target_pairs={{0,1},{1,0},{2,3},{3,2},{4,5},{5,4},{6,7},{7,6},{8,9},{9,8},{10,11... | collective-permute-start | bytes 3145736 | tf_op jit(solution)/shard_map/ppermute | solution.py:661
  314.3 27.9 %collective-permute-start.2 = (bf16[512,1024]{1,0:T(8,128)(2,1)}, bf16[512,1024]{1,0:T(8,128)(2,1)}, u32[]{:S(2)}, u32[]{:S(2)}) collective-permute-start(bf16[512,1024]{1,0:T(8,128)(2,1)} %get-tuple-element.52), channel_id=1, source_target_pairs={{0,1},{1,0},{2,3},{3,2},{4,5},{5,4},{6,7},{7,6},{8,9},{9,8},{10,11... | collective-permute-start | bytes 3145736 | tf_op jit(solution)/shard_map/ppermute | solution.py:662
  342.2 1.2 copy-start.7
  343.5 16.8 %copy-start.5 = (bf16[512,1024]{1,0:T(8,128)(2,1)S(1)}, bf16[512,1024]{1,0:T(8,128)(2,1)}, u32[]{:S(2)}) copy-start(bf16[512,1024]{1,0:T(8,128)(2,1)} %copy-done.4) | copy-start | bytes 3145732
  360.2 12.2 %collective-permute-start.4 = (bf16[512,3072]{1,0:T(8,128)(2,1)}, bf16[512,3072]{1,0:T(8,128)(2,1)}, u32[]{:S(2)}, u32[]{:S(2)}) collective-permute-start(bf16[512,3072]{1,0:T(8,128)(2,1)} %get-tuple-element.57.b_ref), channel_id=1, source_target_pairs={{0,1},{1,0},{2,3},{3,2},{4,5},{5,4},{6,7},{7,6},{8,9},{9,8},{10,11... | collective-permute-start | bytes 9437192 | tf_op jit(solution)/shard_map/ppermute | solution.py:666
  360.3 7.5 %collective-permute-start.6 = (bf16[512,1024]{1,0:T(8,128)(2,1)S(1)}, bf16[512,1024]{1,0:T(8,128)(2,1)S(1)}, u32[]{:S(2)}, u32[]{:S(2)}) collective-permute-start(bf16[512,1024]{1,0:T(8,128)(2,1)S(1)} %copy-done.5), channel_id=1, source_target_pairs={{0,1},{1,0},{2,3},{3,2},{4,5},{5,4},{6,7},{7,6},{8,9},{9,8},{10,11... | collective-permute-start | bytes 3145736 | tf_op jit(solution)/shard_map/ppermute | solution.py:645
  360.8 9.6 %copy-start.9 = (bf16[1024,512]{1,0:T(8,128)(2,1)S(1)}, bf16[1024,512]{1,0:T(8,128)(2,1)}, u32[]{:S(2)}) copy-start(bf16[1024,512]{1,0:T(8,128)(2,1)} %copy-done.8) | copy-start | bytes 3145732
  360.8 7.0 %collective-permute-start.5 = (bf16[4,1,128,512]{3,2,1,0:T(8,128)(2,1)S(1)}, bf16[4,1,128,512]{3,2,1,0:T(8,128)(2,1)S(1)}, u32[]{:S(2)}, u32[]{:S(2)}) collective-permute-start(bf16[4,1,128,512]{3,2,1,0:T(8,128)(2,1)S(1)} %constant_dynamic-slice_fusion.2), channel_id=1, source_target_pairs={{0,1},{1,0},{2,3},{3,2},{4,5},{5,4},{6,7},{7,6},{8,9},{9,8},{10,11... | collective-permute-start | bytes 1572872 | tf_op jit(solution)/shard_map/ppermute | solution.py:645
  370.3 72.7 %reduce-scatter.9.cloned.1.call-start = ((), (), s32[]{:S(2)}) async-start(), calls=%async_computation.10 | async-start | bytes 3932160 | tf_op jit(solution)/shard_map/reduce_scatter | solution.py:652
  370.4 2.0 collective-permute-start.3
  380.3 92.3 %reduce-scatter.19.cloned.1.call-start = ((), (), s32[]{:S(2)}) async-start(), calls=%async_computation.15 | async-start | bytes 1310720 | tf_op jit(solution)/shard_map/reduce_scatter | solution.py:653
  381.1 119.7 %reduce-scatter.23.cloned.1.call-start = ((), (), s32[]{:S(2)}) async-start(), calls=%async_computation.18 | async-start | bytes 1310720 | tf_op jit(solution)/shard_map/reduce_scatter | solution.py:653
  381.8 163.8 %reduce-scatter.15.cloned.1.call-start = ((), (), s32[]{:S(2)}) async-start(), calls=%async_computation.13 | async-start | bytes 327680 | tf_op jit(solution)/shard_map/reduce_scatter | solution.py:653
  395.4 165.6 %reduce-scatter.11.cloned.1.call-start = ((), (), s32[]{:S(2)}) async-start(), calls=%async_computation.11 | async-start | bytes 983040 | tf_op jit(solution)/shard_map/reduce_scatter | solution.py:653
  443.1 144.2 %all-gather.10.cloned.1.call-start = ((), (), s32[]{:S(2)}) async-start(), calls=%async_computation.16 | async-start | bytes 1310720 | tf_op jit(solution)/shard_map/all_gather | solution.py:654
  472.7 142.5 %all-gather.12.cloned.1.call-start = ((), (), s32[]{:S(2)}) async-start(), calls=%async_computation.19 | async-start | bytes 1310720 | tf_op jit(solution)/shard_map/all_gather | solution.py:654
  588.6 46.1 %copy-start.27 = (f32[1664]{0:T(1024)S(1)}, f32[1664]{0:T(1024)}, u32[]{:S(2)}) copy-start(f32[1664]{0:T(1024)} %param.21) | copy-start | bytes 19972
Sparse Core Ops, SparseCore 0:
  11.5 48.2 all-gather.5
  62.2 98.7 all-gather.7
  240.4 52.6 reduce-scatter.16
  296.8 52.9 reduce-scatter.20
  370.4 24.9 reduce-scatter.12
  399.1 43.9 reduce-scatter.8
  445.5 27.1 reduce-scatter.18
  474.9 25.7 reduce-scatter.22
  503.1 18.3 reduce-scatter.14
  523.6 23.0 reduce-scatter.10
  548.3 38.7 all-gather.9
  588.6 26.5 all-gather.11

commit v2 on v1

--- a/solution.py
+++ b/solution.py
@@ -431,7 +431,7 @@
 
 
 def last_kernel(
-    dq_ref, dk_ref, dv_ref, dko_ref, dvo_ref, c_ref, lo_ref, hi_ref, w_ref, x_ref, vec_ref, gn2_ref, gy_ref, scale_ref,
+    dq_ref, dk_ref, dv_ref, dko_ref, dvo_ref, c_ref, lo_ref, hi_ref, w_ref, x_ref, vec_ref, gn2_ref, gy_ref,
     gqkv_ref, in_ref, vg_ref, sum_ref, gn1,
 ):
     j = pl.program_id(0)
@@ -466,7 +466,6 @@
     def _():
         step = 64
         vg_ref[...] = jnp.zeros_like(vg_ref)
-        scale = scale_ref[0, 0]
 
         def chunk(i, carry):
             at = pl.ds(pl.multiple_of(i * step, step), step)
@@ -480,14 +479,14 @@
                 mean = jnp.mean(e, axis=-1, keepdims=True)
                 along = jnp.mean(e * xh, axis=-1, keepdims=True)
                 total = total + rstd * (e - mean - xh * along)
-            in_ref[at, :] = total * scale
+            in_ref[at, :] = total
             vg_ref[...] += jnp.concatenate(sums, axis=0)
             return carry
 
         lax.fori_loop(0, rows // step, chunk, 0)
 
 
-def last(dq, dk, dv, dko, dvo, tables, w, x, vec4, gn2, gy, scale):
+def last(dq, dk, dv, dko, dvo, tables, w, x, vec4, gn2, gy):
     rows, width = x.shape
     cols = 512
     nq = width // cols
@@ -500,7 +499,6 @@
             whole((rows, LANES)), whole((rows, LANES)), whole((rows, LANES)),
             pl.BlockSpec((width, cols), lambda j: (0, j)),
             whole((rows, width)), whole(vec4.shape), whole((rows, width)), whole((rows, width)),
-            pl.BlockSpec(memory_space=pltpu.SMEM),
         ],
         [
             pl.BlockSpec((rows, cols), lambda j: (0, j)), whole((rows, width)), whole((4, width)),
@@ -509,36 +507,7 @@
         [sds((rows, 3 * width), BF16), sds((rows, width), F32), sds((4, width), F32), sds((1, 3 * width), F32)],
         [pltpu.VMEM((rows, width), F32)],
         cost=cost(6 * rows * width * width, 2 * (3 * width * width + 20 * rows * width)),
-    )(dq, dk, dv, dko, dvo, *tables, w, x, vec4, gn2, gy, scale)
-
-
-def wgrad_kernel(core_ref, a_ref, ao_ref, b_ref, bo_ref, out_ref):
-    blocks, size = a_ref.shape[0], a_ref.shape[2]
-    tokens = a_ref.shape[3]
-    a = a_ref[...].reshape(blocks * size, tokens)
-    ao = ao_ref[...].reshape(blocks * size, tokens)
-    out_ref[...] = (dot(a, b_ref[...]) + dot(ao, bo_ref[...])).astype(BF16)
-
-
-def wgrad(core, at_own, at_other, b_own, b_other):
-    width, tokens = at_own.shape
-    blocks = width // (2 * BS)
-    total = b_own.shape[1]
-    cols = 512
-    return call(
-        wgrad_kernel,
-        (total // cols,),
-        [
-            pl.BlockSpec((blocks, 1, BS, tokens), lambda j, c: (0, c[0], 0, 0)),
-            whole((blocks, 1, BS, tokens)),
-            pl.BlockSpec((tokens, cols), lambda j, c: (0, j)),
-            pl.BlockSpec((tokens, cols), lambda j, c: (0, j)),
-        ],
-        pl.BlockSpec((blocks * BS, cols), lambda j, c: (0, j)),
-        sds((blocks * BS, total), BF16),
-        prefetch=1,
-        cost=cost(2 * tokens * width * total, 2 * total * (2 * tokens + width // 2)),
-    )(core, at_own.reshape(blocks, 2, BS, tokens), at_other, b_own, b_other)
+    )(dq, dk, dv, dko, dvo, *tables, w, x, vec4, gn2, gy)
 
 
 def update_kernel(f_ref, g_ref, ls_ref, rs_ref, lr_ref, rr_ref, m_ref, nl_ref, nr_ref, nm_ref, mc_ref):
@@ -573,6 +542,301 @@
     )(factor, g, ls, rs, lr, rr, m)
 
 
+PAIR = 1024
+TILE = PAIR // 2
+
+
+def bits_of(index, count):
+    return [(index // (1 << b)) % 2 for b in range(count)]
+
+
+def reduce_kernel(plan, levels, replica_bits, *refs):
+    groups = len(plan)
+    pairs = sum(plan)
+    at_refs, b_refs = refs[:groups], refs[groups : 2 * groups]
+    v_ref, g_out, vec_out, sq_out = refs[2 * groups : 2 * groups + 4]
+    (a_own, a_oth, b_own, b_oth, s1, r1, r2, zs, gs, vr, vd, sq, sq_in,
+     sem_l, sem_b, sem_as, sem_ar, sem_bs, sem_br, sem_1s, sem_1r, sem_2s, sem_2r,
+     sem_zs, sem_zr, sem_gs, sem_gr, sem_vs, sem_vr, sem_qs, sem_qr, sem_o) = refs[2 * groups + 4 :]
+    s = lax.axis_index("shard")
+    z = lax.axis_index("dp")
+    core, x, y = bits_of(s, 3)
+    zb = bits_of(z, replica_bits)
+    to_core = {"shard": s + 1 - 2 * core}
+    to_x = {"shard": s + 2 - 4 * x}
+    to_y = {"shard": s + 4 - 8 * y}
+    to_z = [{"dp": z + (1 - 2 * zb[l]) * (1 << l)} for l in range(replica_bits)]
+    peers = [to_core, to_x, to_y] + to_z
+
+    barrier = pltpu.get_barrier_semaphore()
+    for peer in peers:
+        pl.semaphore_signal(barrier, inc=1, device_id=peer, device_id_type=pl.DeviceIdType.MESH)
+    pl.semaphore_wait(barrier, len(peers))
+
+    def remote(src, dst, send, recv, peer):
+        return pltpu.make_async_remote_copy(
+            src_ref=src, dst_ref=dst, send_sem=send, recv_sem=recv, device_id=peer, device_id_type=pl.DeviceIdType.MESH
+        )
+
+    first = [sum(plan[:w]) for w in range(groups + 1)]
+
+    def a_local(w):
+        return pltpu.make_async_copy(at_refs[w].at[:, core], a_own.at[w], sem_l.at[w])
+
+    def a_send(w):
+        return remote(at_refs[w].at[:, 1 - core], a_oth.at[w], sem_as.at[w], sem_ar.at[w], to_core)
+
+    def b_cols(w, i):
+        return b_refs[w].at[:, pl.ds(pl.multiple_of((i - first[w]) * PAIR, PAIR), PAIR)]
+
+    def b_send(w, i):
+        return remote(b_cols(w, i), b_oth.at[i], sem_bs.at[i], sem_br.at[i], to_core)
+
+    def b_local(w, i):
+        return pltpu.make_async_copy(b_cols(w, i), b_own.at[i % 2], sem_b.at[i % 2])
+
+    for w in range(groups):
+        a_local(w).start()
+        a_send(w).start()
+        if w == 0:
+            b_local(0, 0).start()
+
+        def launch(i, carry, w=w):
+            b_send(w, i).start()
+            return carry
+
+        lax.fori_loop(first[w], first[w + 1], launch, 0)
+
+    v4 = v_ref
+    vecs = [
+        (v4.at[:, :, 1 - core], vr.at[0, :, :], to_core),
+        (vr.at[0, :, 1 - x], vr.at[1, 0, :], to_x),
+        (vr.at[1, 0, 1 - y], vr.at[1, 1, 0], to_y),
+    ]
+
+    def v_copy(k):
+        if k < 3:
+            src, dst, peer = vecs[k]
+        else:
+            src, dst, peer = vd.at[2 * (k - 3)], vd.at[2 * (k - 3) + 1], to_z[k - 3]
+        return remote(src, dst, sem_vs.at[k], sem_vr.at[k], peer)
+
+    def v_done(k):
+        v_copy(k).wait()
+        if k == 0:
+            vr[0] = vr[0] + v4[:, :, core]
+        elif k == 1:
+            vr[1, 0] = vr[1, 0] + vr[0, :, x]
+        else:
+            if k == 2:
+                total = vr[1, 1, 0] + vr[1, 0, y]
+            else:
+                total = vd[2 * (k - 3)] + vd[2 * (k - 3) + 1]
+            vd[2 * (k - 2)] = total
+
+    v_hops = 3 + replica_bits
+    v_copy(0).start()
+    sq[...] = jnp.zeros_like(sq)
+
+    def copy1(i, t):
+        src = s1.at[i, t, :, 1 - x] if t == 0 else s1.at[i, t, 1 - y]
+        return remote(src, r1.at[i, t], sem_1s.at[i, t], sem_1r.at[i, t], to_x if t == 0 else to_y)
+
+    def copy2(i, t):
+        bit = y if t == 0 else x
+        return remote(
+            r1.at[i, t, 1 - bit], r2.at[i, :, t * TILE : (t + 1) * TILE],
+            sem_2s.at[i, t], sem_2r.at[i, t], to_y if t == 0 else to_x,
+        )
+
+    starts = [0]
+    for l in range(levels):
+        starts.append(starts[l] + (BS >> (l + 1)))
+
+    def z_rows(l):
+        return pl.ds(starts[l], BS >> (l + 1))
+
+    def level_src(i, l, half):
+        size = BS >> (l + 1)
+        off = pl.multiple_of(half * size, size)
+        if l == 0:
+            return r2.at[i, pl.ds(off, size)]
+        return zs.at[i, pl.ds(pl.multiple_of(starts[l - 1] + off, size), size)]
+
+    def copy_z(i, l):
+        return remote(
+            level_src(i, l, 1 - zb[l]), zs.at[i, z_rows(l)], sem_zs.at[i, l], sem_zr.at[i, l], to_z[l]
+        )
+
+    def g_rows(l, mine):
+        base = sum((zb[m] * (BS >> (m + 1)) for m in range(l)), 0)
+        size = BS >> (l + 1)
+        half = zb[l] if mine else 1 - zb[l]
+        return pl.ds(pl.multiple_of(base + half * size, size), size)
+
+    def copy_g(i, l):
+        return remote(gs.at[i, g_rows(l, True)], gs.at[i, g_rows(l, True)], sem_gs.at[i, l], sem_gr.at[i, l], to_z[l])
+
+    def out_cols(i):
+        total = g_out.shape[1] // PAIR
+        spot = total - first[1] + i
+        spot = jnp.where(i >= first[1], i - first[1] + plan[3], spot)
+        spot = jnp.where(i >= first[3], i - first[3], spot)
+        return pl.ds(pl.multiple_of(spot * PAIR, PAIR), PAIR)
+
+    def out_copy(i):
+        src = gs.at[i] if levels else r2.at[i]
+        return pltpu.make_async_copy(src, g_out.at[:, out_cols(i)], sem_o.at[i])
+
+    def stage_a(i):
+        group = sum((jnp.where(i >= first[w], 1, 0) for w in range(1, groups)), 0)
+        for w in range(groups):
+            @pl.when(i == first[w])
+            def _():
+                a_local(w).wait()
+                a_send(w).wait()
+
+            @pl.when((i + 1 >= first[w]) & (i + 1 < first[w + 1]))
+            def _():
+                b_local(w, i + 1).start()
+
+        slot = i % 2
+        pltpu.make_async_copy(b_oth.at[i], b_own.at[slot], sem_b.at[slot]).wait()
+        remote(b_own.at[slot], b_oth.at[i], sem_bs.at[i], sem_br.at[i], to_core).wait()
+        size = 4 * BS
+        own = a_own[group].reshape(size, a_own.shape[-1])
+        oth = a_oth[group].reshape(size, a_oth.shape[-1])
+        for t in range(2):
+            at = slice(t * TILE, (t + 1) * TILE)
+            acc = dot(own, b_own[slot, :, at]) + dot(oth, b_oth[i, :, at])
+            s1[i, t] = acc.astype(BF16).reshape(2, 2, BS, TILE)
+            copy1(i, t).start()
+
+    def stage_b(i):
+        for t in range(2):
+            copy1(i, t).wait()
+            kept = s1[i, t, :, x] if t == 0 else s1[i, t, y]
+            r1[i, t] = (r1[i, t].astype(F32) + kept.astype(F32)).astype(BF16)
+            copy2(i, t).start()
+
+    def stage_c(i):
+        for t in range(2):
+            copy2(i, t).wait()
+            at = slice(t * TILE, (t + 1) * TILE)
+            bit = y if t == 0 else x
+            r2[i, :, at] = (r2[i, :, at].astype(F32) + r1[i, t, bit].astype(F32)).astype(BF16)
+        if levels:
+            copy_z(i, 0).start()
+        else:
+            out_copy(i).start()
+
+    def stage_z(l):
+        def run(i):
+            copy_z(i, l).wait()
+            total = zs[i, z_rows(l)].astype(F32) + level_src(i, l, zb[l])[...].astype(F32)
+            if l + 1 < levels:
+                zs[i, z_rows(l)] = total.astype(BF16)
+                copy_z(i, l + 1).start()
+            else:
+                gs[i, g_rows(l, True)] = total.astype(BF16)
+                copy_g(i, l).start()
+        return run
+
+    def stage_g(l):
+        def run(i):
+            copy_g(i, l).wait()
+            if l:
+                copy_g(i, l - 1).start()
+            else:
+                part = gs[i].astype(F32)
+                part = jnp.sum((part * part).reshape(BS // 8, 8, PAIR), axis=0)
+                sq[0] += sum(part[:, g * LANES : (g + 1) * LANES] for g in range(PAIR // LANES))
+                out_copy(i).start()
+        return run
+
+    stages = [stage_a, stage_b, stage_c]
+    stages += [stage_z(l) for l in range(levels)] + [stage_g(l) for l in reversed(range(levels))]
+    lags = len(stages)
+
+    def step(i, carry):
+        for lag, stage in enumerate(stages):
+            @pl.when((i >= lag) & (i < pairs + lag))
+            def _():
+                stage(i - lag)
+
+        for k in range(v_hops):
+            @pl.when(i == k + 1)
+            def _():
+                v_done(k)
+                if k + 1 < v_hops:
+                    v_copy(k + 1).start()
+        return carry
+
+    lax.fori_loop(0, pairs + lags - 1, step, 0)
+    total = vd[2 * replica_bits]
+    vec_out[...] = total
+    rows13 = lax.broadcasted_iota(jnp.int32, total.shape, 0) < 13
+    square = jnp.where(rows13, total * total, 0.0)
+    sq[0] += square[0:8] + square[8:16]
+    for k, peer in enumerate((to_core, to_x, to_y)):
+        hop = remote(sq.at[k], sq_in.at[k], sem_qs.at[k], sem_qr.at[k], peer)
+        hop.start()
+        hop.wait()
+        sq[k + 1] = sq[k] + sq_in[k]
+    sq_out[...] = sq[3]
+
+    def drain(i, carry):
+        out_copy(i).wait()
+        return carry
+
+    lax.fori_loop(0, pairs, drain, 0)
+
+
+def reduce_grads(ats, bs, vec, replicas):
+    plan = [b.shape[1] // PAIR for b in bs]
+    pairs = sum(plan)
+    tokens = bs[0].shape[0]
+    replica_bits = replicas.bit_length() - 1
+    assert replicas == 1 << replica_bits
+    levels = replica_bits if replicas <= 8 else 0
+    groups = len(plan)
+    dma = pltpu.SemaphoreType.DMA
+    lv, vh = max(levels, 1), 3 + replica_bits
+    scratch = [
+        pltpu.VMEM((groups, 4, BS, tokens), BF16),
+        pltpu.VMEM((groups, 4, BS, tokens), BF16),
+        pltpu.VMEM((2, tokens, PAIR), BF16),
+        pltpu.VMEM((pairs, tokens, PAIR), BF16),
+        pltpu.VMEM((pairs, 2, 2, 2, BS, TILE), BF16),
+        pltpu.VMEM((pairs, 2, 2, BS, TILE), BF16),
+        pltpu.VMEM((pairs, BS, PAIR), BF16),
+        pltpu.VMEM((pairs, BS if levels else 16, PAIR), BF16),
+        pltpu.VMEM((pairs if levels else 1, BS, PAIR), BF16),
+        pltpu.VMEM((2, 2, 2, 16, LANES), F32),
+        pltpu.VMEM((2 * replica_bits + 2, 16, LANES), F32),
+        pltpu.VMEM((4, 8, LANES), F32),
+        pltpu.VMEM((3, 8, LANES), F32),
+        dma((groups,)), dma((2,)), dma((groups,)), dma((groups,)), dma((pairs,)), dma((pairs,)),
+        dma((pairs, 2)), dma((pairs, 2)), dma((pairs, 2)), dma((pairs, 2)),
+        dma((pairs, lv)), dma((pairs, lv)), dma((pairs, lv)), dma((pairs, lv)),
+        dma((vh,)), dma((vh,)), dma((3,)), dma((3,)), dma((pairs,)),
+    ]
+    anyspace = pl.BlockSpec(memory_space=pl.ANY)
+    vmem = pl.BlockSpec(memory_space=pltpu.VMEM)
+    return pl.pallas_call(
+        partial(reduce_kernel, plan, levels, replica_bits),
+        out_shape=[
+            sds((BS, pairs * PAIR), BF16), sds((16, LANES), F32), sds((8, LANES), F32)
+        ],
+        in_specs=[anyspace] * (2 * groups) + [vmem],
+        out_specs=[anyspace, vmem, vmem],
+        scratch_shapes=scratch,
+        compiler_params=pltpu.CompilerParams(
+            collective_id=0, has_side_effects=True, vmem_limit_bytes=58 * MIB
+        ),
+    )(*[a.reshape(4, 2, BS, tokens) for a in ats], *bs, vec)
+
+
 def angles(positions):
     half_rot = ROT // 2
     frequency = jnp.power(10000.0, -2.0 * jnp.arange(half_rot, dtype=F32) / ROT)
@@ -601,7 +865,6 @@
     parity = index % 2
     par = parity.astype(jnp.int32).reshape(1)
     swap = [(i, i ^ 1) for i in range(shards)]
-    groups = [[i for i in range(shards) if i % 2 == c] for c in range(2)]
 
     low = master.astype(BF16)
     w_qkv = lax.all_gather(low[:, : 3 * width], "shard", axis=0, tiled=True)
@@ -618,8 +881,6 @@
     b_down = params[8 * width + hidden :].reshape(1, -1)
 
     valid_float = valid.astype(F32)
-    count = lax.psum(lax.psum(jnp.sum(valid_float), "shard"), "dp")
-    scale = rows * shards * replicas / count
 
     local = jnp.arange(half, dtype=jnp.int32)
     positions = jnp.concatenate([parity * half + local, (3 - parity) * half + local])
@@ -639,43 +900,32 @@
     )
     gob, gub, gub_sum, gn2 = dgrad(gb, w_out, w_down, w_up, dg)
 
-    other = 1 - parity
-    pick = lambda a: lax.dynamic_slice_in_dim(a.reshape(-1, 2, BS, rows), other, 1, axis=1)
-    hb_o, gb_o, gub_o, gbt_o, obt_o, n2t_o, n1t_o = (
-        lax.ppermute(a, "shard", swap) for a in (hb, gb, gub, pick(gbt), pick(obt), pick(n2t), pick(n1t))
-    )
-    dw_down = wgrad(par, gbt, gbt_o, hb, hb_o)
-    dw_out = wgrad(par, obt, obt_o, gb, gb_o)
-    dw_up = wgrad(par, n2t, n2t_o, gub, gub_o)
-
-    def reduce(part):
-        part = lax.psum_scatter(part, "shard", scatter_dimension=0, axis_index_groups=groups, tiled=True)
-        part = lax.psum_scatter(part, "dp", scatter_dimension=1, tiled=True)
-        return lax.all_gather(part, "dp", axis=1, tiled=True)
-
-    g_down, g_out, g_up = reduce(dw_down), reduce(dw_out), reduce(dw_up)
-
     dq, dk, dv, dk_o, dv_o = att_bwd(
         par, q, kv, kvo, gob, ob, lse, own_seg.reshape(2, half), key_seg.reshape(2 * rows, 1), tables
     )
     dk_r = lax.ppermute(dk_o, "shard", swap)
     dv_r = lax.ppermute(dv_o, "shard", swap)
     gqkv, input_grad, vec_grad, gqkv_sum = last(
-        dq, dk, dv, dk_r, dv_r, tables, w_qkv, tokens, vec4, gn2, gy, scale.reshape(1, 1)
+        dq, dk, dv, dk_r, dv_r, tables, w_qkv, tokens, vec4, gn2, gy
     )
-    gqkv_o = lax.ppermute(gqkv, "shard", swap)
-    g_qkv = reduce(wgrad(par, n1t, n1t_o, gqkv, gqkv_o))
-
+    own_len = vectors.shape[0]
+    lines = own_len // LANES
     vector_grad = jnp.concatenate(
         [vec_grad.reshape(-1), gqkv_sum.reshape(-1), gb_sum.reshape(-1), gub_sum.reshape(-1), gb_sum.reshape(-1)]
-    )
-    vector_grad = lax.psum(lax.psum(vector_grad, "shard"), "dp")
-    own_len = vectors.shape[0]
-    own_vector = lax.dynamic_slice_in_dim(vector_grad, index * own_len, own_len)
-
-    grads = jnp.concatenate([g_qkv, g_out, g_up, g_down], axis=1)
-    square_sum = jnp.sum(jnp.square(grads.astype(F32))) + jnp.sum(own_vector * own_vector)
-    grad_norm = scale * jnp.sqrt(lax.psum(square_sum, "shard"))
+    ).reshape(shards, lines, LANES)
+    tail = jnp.full((shards, 16 - lines, LANES), jnp.sum(valid.astype(F32)), F32)
+    packed = jnp.concatenate([vector_grad, tail], axis=1).reshape(2, 2, 2, 16, LANES)
+    grads, vec_total, squares = reduce_grads((gbt, obt, n2t, n1t), (hb, gb, gub, gqkv), packed, replicas)
+    own_vector = vec_total[:lines].reshape(own_len)
+    scale = rows * shards * replicas / vec_total[lines, 0]
+    if replicas <= 8:
+        square_sum = jnp.sum(squares)
+    else:
+        grads = lax.psum_scatter(grads, "dp", scatter_dimension=1, tiled=True)
+        grads = lax.all_gather(grads, "dp", axis=1, tiled=True)
+        square_sum = jnp.sum(squares) + lax.psum(jnp.sum(jnp.square(grads.astype(F32))), "shard")
+    input_grad = input_grad * scale
+    grad_norm = scale * jnp.sqrt(square_sum)
     factor = scale * jnp.minimum(1.0, math.sqrt(width * stack / BS) / grad_norm)
     new_left, new_right, new_master, master_copy = update(
         factor.reshape(1, 1), grads, left_stat, right_stat, left_root, right_root, master

time: 666 us -> 479 us (0.72)
  waiting for transfers between devices: 237 us -> 70.7 us
  blocking collectives: 137 us -> 10.6 us
  Pallas kernels: 209 us -> 331 us
  local copies, waits for them, and re-layouts: 50.5 us -> 37.7 us
    pallas_call x4 -> x1, Pallas kernels: 28.1 us -> 150 us  [reduce_grads(): pl.pallas_call(partial(reduce_kernel, plan, levels, replica_bits), out_sh...]
    reduce_scatter x8 -> x0, waiting for transfers between devices: 119 us -> none  [the longest x4 61.2 us: reduce(): lax.psum_scatter(part, 'shard', scatter_dimension=0, axis_index_groups=gr...]
    psum x5 -> x0, blocking collectives: 84.4 us -> none  [the longest x2 44.2 us: body(): vector_grad = lax.psum(lax.psum(vector_grad, 'shard'), 'dp')]
    all_gather x2 -> x0, blocking collectives: 41.5 us -> none  [reduce(): return lax.all_gather(part, 'dp', axis=1, tiled=True)]
    all_gather x2 -> x0, waiting for transfers between devices: 26.6 us -> none  [reduce(): return lax.all_gather(part, 'dp', axis=1, tiled=True)]
    ppermute x8 -> x0, waiting for transfers between devices: 20.9 us -> none  [the longest x7 20.9 us: body(): lax.ppermute(a, 'shard', swap)]
    unnamed x68 -> x55, local copies, waits for them, and re-layouts: 24.6 us -> 13.3 us
  transfers between devices with their start and end apart: 23 -> 5, of which waited for: 12 -> 5; matrix products, arithmetic and copies ran while one was open for 2% -> 2% of each run, Pallas kernels for 21% -> 12%
where the time goes in v2:
time: 479 us; the launch traced here: 478 us
  Pallas kernels  331 us (69%)
  waiting for transfers between devices  70.7 us (15%)
  local copies, waits for them, and re-layouts  37.7 us (8%)
  between operations  16.9 us (4%)
  blocking collectives  10.6 us (2%)
  other arithmetic  9.97 us (2%)
    pallas_call x1, Pallas kernels, reduce_grads(): pl.pallas_call(partial(reduce_kernel, plan, levels, replica_bits), out_sh...  150 us
    pallas_call x1, Pallas kernels, att_bwd(): call(att_bwd_kernel, (pairs,), [col(0), col(0), col(pairs), col(0), col(p...  49.5 us
    pallas_call x1, Pallas kernels, att_fwd(): call(att_fwd_kernel, (pairs,), [col(0), col(0), col(pairs), col(0), col(p...  43.5 us
    all_gather x1, waiting for transfers between devices, body(): w_qkv = lax.all_gather(low[:, :3 * width], 'shard', axis=0, tiled=True)  33.4 us
    all_gather x1, waiting for transfers between devices, body(): w_rest = lax.all_gather(low[:, 3 * width:], 'shard', axis=0, tiled=True)  32.8 us
    pallas_call x1, Pallas kernels, update(): call(update_kernel, (count // per,), [pl.BlockSpec(memory_space=pltpu.SME...  20.5 us
    pallas_call x1, Pallas kernels, dgrad(): call(dgrad_kernel, (hidden // cols,), [whole((rows, width)), whole((width...  16.9 us
    pallas_call x1, Pallas kernels, last(): call(last_kernel, (3 * nq,), [at(0), at(1), at(2), at(1), at(2), whole((r...  16.1 us
  transfers between devices with their start and end apart: 5, of which 5 were waited for; matrix products, arithmetic and copies ran while one was open for 2% of the time, Pallas kernels for 12%

profile of v2, /device:TPU:0, one launch (start us, length us, event | category | flops | bytes accessed | tf_op | source)
XLA Modules:
  0.0 477.5 jit_solution(5674102084047127288)
XLA Ops:
  7.2 0.0 all-gather.4.cloned.1.call-start
  7.2 3.2 convert_element_type.22
  10.4 0.9 slice.92
  11.3 0.0 all-gather.4.cloned.1.call-update
  11.4 0.0 copy-start.20
  11.4 0.0 all-gather.6.cloned.1.call-start
  11.4 1.6 slice.94
  13.0 0.0 all-gather.6.cloned.1.call-update
  13.1 10.6 %all-gather = bf16[8,1,1664]{2,1,0:T(2,128)(2,1)S(1)} all-gather(bf16[1,1,1664]{2,1,0:T(2,128)(2,1)S(1)} %reshape.130), channel_id=1, replica_groups=mesh['dp'=4,'shard'=8] {'shard'}, dimensions={0}, use_global_device_ids=true | all-gather | bytes 29952 | tf_op jit(solution)/shard_map/all_gather | solution.py:872
  23.7 0.1 convert_element_type.25
  23.9 1.0 multiply_sine_fusion
  24.9 0.0 copy-start.3
  24.9 0.4 concatenate.25.hi_ref
  25.4 0.4 concatenate.24.lo_ref
  25.9 0.4 concatenate.23.c_ref
  26.3 33.4 %all-gather.4.cloned.1.call-done.w_ref = bf16[1024,3072]{1,0:T(8,128)(2,1)} async-done(((bf16[128,3072]{1,0:T(8,128)(2,1)}), bf16[1024,3072]{1,0:T(8,128)(2,1)}) %all-gather.4.cloned.1.call-update) | async-done | bytes 6291472 | tf_op jit(solution)/shard_map/all_gather | solution.py:870
  59.7 0.0 copy-done.3
  59.7 11.7 %shard_map.170 = (bf16[1024,512]{1,0:T(8,128)(2,1)S(1)}, bf16[512,1024]{1,0:T(8,128)(2,1)S(1)}, bf16[1024,512]{1,0:T(8,128)(2,1)S(1)}, bf16[512,1024]{1,0:T(8,128)(2,1)S(1)}, bf16[512,2048]{1,0:T(8,128)(2,1)}) custom-call(bf16[512,1024]{1,0:T(8,128)(2,1)S(1)} %copy-done.3, f32[4,1024]{1,0:T(4,128)S(1)} %slice.71.vec_ref, ...), custom_call_target="tpu_custom_call" | custom-call | flops 3221225472 | bytes 13631488 | tf_op jit(solution)/shard_map/pallas_call | solution.py:125
  71.5 1.0 copy-done.4
  72.4 1.0 copy-done.5
  73.4 1.0 copy-done.14
  74.4 1.0 copy-done.17
  75.3 0.3 collective-permute-start
  75.6 0.8 dynamic_slice.6
  76.4 0.0 copy-done.21
  76.4 0.8 dynamic_slice.7
  77.2 0.9 copy.27.valid_ref
  78.1 0.1 copy.26.qseg_ref
  78.2 0.2 copy.30
  78.5 1.4 collective-permute-done.ko_ref.vo_ref
  79.8 1.6 copy-done.10
  81.4 1.2 copy-done.15
  82.7 43.5 %shard_map.171 = (bf16[512,1024]{1,0:T(8,128)(2,1)S(1)}, bf16[8,128,512]{2,1,0:T(8,128)(2,1)S(1)}, f32[8,2,512]{2,1,0:T(2,128)S(1)}) custom-call(s32[1]{0:T(128)} %bitcast.par_ref, bf16[512,1024]{1,0:T(8,128)(2,1)S(1)} %copy-done.15, bf16[512,2048]{1,0:T(8,128)(2,1)S(1)} %copy-done.10, bf16[512,2048]{1,0:T(8,128)(2,1)S(1)} %copy-done.10, ...), custom_call_target="tpu_custom_call" | custom-call | flops 2147483648 | bytes 8388608 | tf_op jit(solution)/shard_map/pallas_call | solution.py:228
  126.2 1.0 copy-done.6
  127.2 1.0 copy-done.12
  128.2 32.8 %all-gather.6.cloned.1.call-done = bf16[1024,9216]{1,0:T(8,128)(2,1)} async-done(((bf16[128,9216]{1,0:T(8,128)(2,1)}), bf16[1024,9216]{1,0:T(8,128)(2,1)}) %all-gather.6.cloned.1.call-update) | async-done | bytes 18874384 | tf_op jit(solution)/shard_map/all_gather | solution.py:871
  161.0 12.0 %fusion.6 = (bf16[1024,4096]{1,0:T(8,128)(2,1)}, bf16[1024,4096]{1,0:T(8,128)(2,1)}) fusion(bf16[1024,9216]{1,0:T(8,128)(2,1)} %all-gather.6.cloned.1.call-done), kind=kLoop, calls=%fused_computation.22 | loop fusion | bytes 33554432 | tf_op jit(solution)/shard_map/slice | solution.py:875
  173.0 12.1 %shard_map.172 = (bf16[512,4096]{1,0:T(8,128)(2,1)S(1)}, bf16[512,4096]{1,0:T(8,128)(2,1)}) custom-call(bf16[512,1024]{1,0:T(8,128)(2,1)S(1)} %copy-done.18, bf16[1024,4096]{1,0:T(8,128)(2,1)} %get-tuple-element.79.w_ref.wu_ref, f32[1,4096]{1,0:T(1,128)S(1)} %bitcast.47), custom_call_target="tpu_custom_call" | custom-call | flops 4294967296 | bytes 16777216 | tf_op jit(solution)/shard_map/pallas_call | solution.py:362
  185.1 2.0 copy-done
  187.1 3.2 slice.97.wo_ref
  190.3 0.0 copy-done.11
  190.3 10.8 %shard_map.173 = (f32[512,1024]{1,0:T(8,128)}, bf16[512,1024]{1,0:T(8,128)(2,1)S(1)}, bf16[1024,512]{1,0:T(8,128)(2,1)S(1)}, f32[1,1024]{1,0:T(1,128)S(1)}) custom-call(bf16[512,1024]{1,0:T(8,128)(2,1)S(1)} %copy-done.13, bf16[512,4096]{1,0:T(8,128)(2,1)} %copy-done, bf16[1024,1024]{1,0:T(8,128)(2,1)} %slice.97.wo_ref, ...), custom_call_target="tpu_custom_call" | custom-call | flops 5368709120 | bytes 16777216 | tf_op jit(solution)/shard_map/pallas_call | solution.py:390
  201.1 16.9 %shard_map.174 = (bf16[512,1024]{1,0:T(8,128)(2,1)S(1)}, bf16[512,4096]{1,0:T(8,128)(2,1)}, f32[1,4096]{1,0:T(1,128)S(1)}, f32[512,1024]{1,0:T(8,128)S(1)}) custom-call(bf16[512,1024]{1,0:T(8,128)(2,1)S(1)} %get-tuple-element.47.gb_ref.refs_5_, bf16[1024,1024]{1,0:T(8,128)(2,1)} %slice.97.wo_ref, bf16[1024,4096]{1,0:T(8,128)(2,1)} %get-tuple-element.78.wd_ref, ...), custom_call_target="tpu_custom_call" | custom-call | flops 9663676416 | bytes 25165824 | tf_op jit(solution)/shard_map/pallas_call | solution.py:423
  218.0 0.0 copy-done.8
  218.0 1.3 copy-done.2
  219.3 1.0 copy-done.19
  220.3 0.0 copy-done.16
  220.3 49.5 %shard_map.175 = (bf16[512,1024]{1,0:T(8,128)(2,1)S(1)}, f32[512,1024]{1,0:T(8,128)}, f32[512,1024]{1,0:T(8,128)}, bf16[512,1024]{1,0:T(8,128)(2,1)S(1)}, bf16[512,1024]{1,0:T(8,128)(2,1)S(1)}) custom-call(s32[1]{0:T(128)} %bitcast.par_ref, bf16[512,1024]{1,0:T(8,128)(2,1)S(1)} %copy-done.16, bf16[512,2048]{1,0:T(8,128)(2,1)} %get-tuple-element.43.k_ref.v_ref, ...), custom_call_target="tpu_custom_call" | custom-call | flops 5368709120 | bytes 16777216 | tf_op jit(solution)/shard_map/pallas_call | solution.py:323
  269.8 0.2 collective-permute-start.1
  270.0 0.3 collective-permute-start.2
  270.3 0.6 convert_reduce_fusion
  270.9 1.6 collective-permute-done.1.dko_ref
  272.4 1.5 collective-permute-done.2.dvo_ref
  273.9 16.1 %shard_map.176 = (bf16[512,3072]{1,0:T(8,128)(2,1)}, f32[512,1024]{1,0:T(8,128)}, f32[4,1024]{1,0:T(4,128)S(1)}, f32[1,3072]{1,0:T(1,128)S(1)}) custom-call(bf16[512,1024]{1,0:T(8,128)(2,1)S(1)} %get-tuple-element.51.dq_ref, f32[512,1024]{1,0:T(8,128)} %get-tuple-element.52.dk_ref, f32[512,1024]{1,0:T(8,128)} %get-tuple-element.53.dv_ref, ...), custom_call_target="tpu_custom_call" | custom-call | flops 3221225472 | bytes 27262976 | tf_op jit(solution)/shard_map/pallas_call | solution.py:494
  290.1 1.3 concatenate.27
  291.4 149.8 %shard_map.177 = (bf16[128,12288]{1,0:T(8,128)(2,1)}, f32[16,128]{1,0:T(8,128)}, f32[8,128]{1,0:T(8,128)}) custom-call(bf16[4,2,128,512]{3,2,1,0:T(8,128)(2,1)} %bitcast.41, bf16[4,2,128,512]{3,2,1,0:T(8,128)(2,1)} %bitcast.40, bf16[4,2,128,512]{3,2,1,0:T(8,128)(2,1)} %bitcast.39, bf16[4,2,128,512]{3,2,1,0:T(8,128)(2,1)} %bitcast.38, ...), custom_call_target="tpu_custom_call" | custom-call | tf_op jit(solution)/shard_map/pallas_call | solution.py:826
  441.2 0.0 copy-start.22
  441.2 0.0 copy-start.23
  441.2 0.0 copy-start.1
  441.2 1.3 slice.89
  442.6 1.3 reduce_sum.19
  445.2 3.2 broadcast_multiply_fusion
  448.5 0.6 fusion.3
  449.1 20.5 %shard_map.178 = (f32[1,96,128,128]{3,2,1,0:T(8,128)}, f32[1,96,128,128]{3,2,1,0:T(8,128)}, f32[128,12288]{1,0:T(8,128)}, bf16[128,12288]{1,0:T(8,128)(2,1)}) custom-call(f32[1,1]{1,0:T(1,128)} %bitcast.21.f_ref, bf16[128,12288]{1,0:T(8,128)(2,1)S(1)} %copy-done.1, f32[1,96,128,128]{3,2,1,0:T(8,128)} %ls_ref.1, f32[1,96,128,128]{3,2,1,0:T(8,128)} %rs_ref.1, ...), custom_call_target="tpu_custom_call" | custom-call | flops 1610612736 | bytes 50331648 | tf_op jit(solution)/shard_map/pallas_call | solution.py:535
  (50 shorter events, 0.2 us)
Async XLA Ops:
  7.2 52.6 %all-gather.4.cloned.1.call-start = ((), (), s32[]{:S(2)}) async-start(), calls=%async_computation | async-start | bytes 7077888 | tf_op jit(solution)/shard_map/all_gather | solution.py:870
  11.4 1.7 copy-start.20
  11.4 149.6 %all-gather.6.cloned.1.call-start = ((), (), s32[]{:S(2)}) async-start(), calls=%async_computation.1 | async-start | bytes 21233664 | tf_op jit(solution)/shard_map/all_gather | solution.py:871
  24.9 34.9 %copy-start.3 = (bf16[512,1024]{1,0:T(8,128)(2,1)S(1)}, bf16[512,1024]{1,0:T(8,128)(2,1)}, u32[]{:S(2)}) copy-start(bf16[512,1024]{1,0:T(8,128)(2,1)} %x_ref.5) | copy-start | bytes 3145732
  59.7 16.6 %copy-start.21 = (s32[512]{0:T(512)S(1)}, s32[512]{0:T(512)}, u32[]{:S(2)}) copy-start(s32[512]{0:T(512)} %param.14) | copy-start | bytes 6148
  71.5 1.0 copy-start.4
  72.4 1.0 copy-start.5
  73.4 1.0 copy-start.14
  74.4 1.0 copy-start.17
  75.3 4.5 collective-permute-start
  79.8 1.6 copy-start.10
  81.4 1.2 copy-start.15
  126.2 1.0 copy-start.6
  127.2 1.0 copy-start.12
  161.0 12.0 %copy-start.18 = (bf16[512,1024]{1,0:T(8,128)(2,1)S(1)}, bf16[512,1024]{1,0:T(8,128)(2,1)}, u32[]{:S(2)}) copy-start(bf16[512,1024]{1,0:T(8,128)(2,1)} %copy-done.17) | copy-start | bytes 3145732
  185.0 2.0 copy-start
  187.1 3.2 copy-start.9
  187.1 3.2 copy-start.11
  187.1 3.2 copy-start.13
  201.1 16.9 %copy-start.7 = (bf16[512,1024]{1,0:T(8,128)(2,1)}, bf16[512,1024]{1,0:T(8,128)(2,1)S(1)}, u32[]{:S(2)}) copy-start(bf16[512,1024]{1,0:T(8,128)(2,1)S(1)} %get-tuple-element.47.gb_ref.refs_5_) | copy-start | bytes 3145732
  201.1 16.9 %copy-start.8 = (bf16[1024,512]{1,0:T(8,128)(2,1)}, bf16[1024,512]{1,0:T(8,128)(2,1)S(1)}, u32[]{:S(2)}) copy-start(bf16[1024,512]{1,0:T(8,128)(2,1)S(1)} %get-tuple-element.59) | copy-start | bytes 3145732
  201.1 19.2 %copy-start.16 = (bf16[512,1024]{1,0:T(8,128)(2,1)S(1)}, bf16[512,1024]{1,0:T(8,128)(2,1)}, u32[]{:S(2)}) copy-start(bf16[512,1024]{1,0:T(8,128)(2,1)} %copy-done.14) | copy-start | bytes 3145732
  218.0 1.3 copy-start.2
  219.3 1.0 copy-start.19
  269.8 2.7 collective-permute-start.1
  270.0 3.9 collective-permute-start.2
  441.2 7.3 %copy-start.22 = (f32[1664]{0:T(1024)S(1)}, f32[1664]{0:T(1024)}, u32[]{:S(2)}) copy-start(f32[1664]{0:T(1024)} %param.21) | copy-start | bytes 19972
  441.2 7.3 %copy-start.23 = (f32[16,128]{1,0:T(8,128)S(1)}, f32[16,128]{1,0:T(8,128)}, u32[]{:S(2)}) copy-start(f32[16,128]{1,0:T(8,128)} %get-tuple-element.69) | copy-start | bytes 24580
  441.2 7.9 %copy-start.1 = (bf16[128,12288]{1,0:T(8,128)(2,1)S(1)}, bf16[128,12288]{1,0:T(8,128)(2,1)}, u32[]{:S(2)}) copy-start(bf16[128,12288]{1,0:T(8,128)(2,1)} %get-tuple-element.71.g_ref) | copy-start | bytes 9437188
Sparse Core Ops, SparseCore 0:
  11.5 48.2 all-gather.3
  62.2 98.7 all-gather.5

commit v3 on v2

--- a/solution.py
+++ b/solution.py
@@ -72,87 +72,6 @@
     return values * c + pltpu.roll(values, LANES - ROT // 2, 1) * lo + pltpu.roll(values, ROT // 2, 1) * hi
 
 
-def pre_kernel(x_ref, vec_ref, w_ref, b_ref, c_ref, lo_ref, hi_ref, n1t_ref, n2_ref, n2t_ref, q_ref, kv_ref, n1_ref):
-    j = pl.program_id(0)
-    rows, width = x_ref.shape
-    step = 128
-
-    @pl.when(j == 0)
-    def _():
-        def chunk(i, carry):
-            at = pl.ds(pl.multiple_of(i * step, step), step)
-            xh, _ = normed(x_ref[at, :].astype(F32))
-            one = (xh * vec_ref[0:1, :] + vec_ref[1:2, :]).astype(BF16)
-            two = (xh * vec_ref[2:3, :] + vec_ref[3:4, :]).astype(BF16)
-            n1_ref[at, :] = one
-            n2_ref[at, :] = two
-            n1t_ref[:, at] = one.T
-            n2t_ref[:, at] = two.T
-            return carry
-
-        lax.fori_loop(0, rows // step, chunk, 0)
-
-    cols = w_ref.shape[1]
-    proj = dot(n1_ref[...], w_ref[...]) + b_ref[...]
-
-    def emit(out, turned):
-        for g in range(cols // LANES):
-            part = proj[:, g * LANES : (g + 1) * LANES]
-            if turned:
-                part = turn(part, c_ref[...], lo_ref[...], hi_ref[...])
-            out[:, g * LANES : (g + 1) * LANES] = part.astype(BF16)
-
-    nq = width // cols
-
-    @pl.when(j < nq)
-    def _():
-        emit(q_ref, True)
-
-    @pl.when((j >= nq) & (j < 2 * nq))
-    def _():
-        emit(kv_ref, True)
-
-    @pl.when(j >= 2 * nq)
-    def _():
-        emit(kv_ref, False)
-
-
-def pre(x, vec4, w, b, tables):
-    rows, width = x.shape
-    cols = 512
-    steps = 3 * width // cols
-    nq = width // cols
-    return call(
-        pre_kernel,
-        (steps,),
-        [
-            whole((rows, width)),
-            whole(vec4.shape),
-            pl.BlockSpec((width, cols), lambda j: (0, j)),
-            pl.BlockSpec((1, cols), lambda j: (0, j)),
-            whole((rows, LANES)),
-            whole((rows, LANES)),
-            whole((rows, LANES)),
-        ],
-        [
-            whole((width, rows)),
-            whole((rows, width)),
-            whole((width, rows)),
-            pl.BlockSpec((rows, cols), lambda j: (0, jnp.minimum(j, nq - 1))),
-            pl.BlockSpec((rows, cols), lambda j: (0, jnp.maximum(j - nq, 0))),
-        ],
-        [
-            sds((width, rows), BF16),
-            sds((rows, width), BF16),
-            sds((width, rows), BF16),
-            sds((rows, width), BF16),
-            sds((rows, 2 * width), BF16),
-        ],
-        [pltpu.VMEM((rows, width), BF16)],
-        cost=cost(6 * rows * width * width, 2 * (3 * width * width + 7 * rows * width)),
-    )(x, vec4, w, b, *tables)
-
-
 def place_keys(own_ref, other_ref, out_ref, parity):
     half = own_ref.shape[0] // 2
     for ref, who in ((own_ref, parity), (other_ref, 1 - parity)):
@@ -161,148 +80,552 @@
             out_ref[pl.ds(pl.multiple_of(quarter * half, half), half), :] = ref[b * half : (b + 1) * half, :]
 
 
-def att_fwd_kernel(par_ref, q_ref, k_ref, v_ref, ko_ref, vo_ref, qseg_ref, kseg_ref, o_ref, ot_ref, lse_ref, mask, kpos, vpos, sc):
-    rows = q_ref.shape[0]
+def key_tile(t, parity):
+    first = parity + 1
+    b = jnp.where(t >= first, 1, 0)
+    return b, t - b * first
+
+
+def split_heads(pair):
+    lane = lax.broadcasted_iota(jnp.int32, pair.shape, 1)
+    zero = jnp.zeros_like(pair)
+    return jnp.concatenate([jnp.where(lane < HD, pair, zero), jnp.where(lane >= HD, pair, zero)], axis=0)
+
+
+def join_heads(both):
+    half = both.shape[0] // 2
+    lane = lax.broadcasted_iota(jnp.int32, (half, LANES), 1)
+    return jnp.where(lane < HD, both[:half], both[half:])
+
+
+CHUNK = 1024
+
+
+def bits_of(index, count):
+    return [(index // (1 << b)) % 2 for b in range(count)]
+
+
+def flipped(bits, mask):
+    return sum(((1 - bit) if (mask >> k) & 1 else bit) * (1 << k) for k, bit in enumerate(bits))
+
+
+def remote(src, dst, send, recv, peer):
+    return pltpu.make_async_remote_copy(
+        src_ref=src, dst_ref=dst, send_sem=send, recv_sem=recv, device_id=peer, device_id_type=pl.DeviceIdType.MESH
+    )
+
+
+def meet(peers):
+    barrier = pltpu.get_barrier_semaphore()
+    for peer in peers:
+        pl.semaphore_signal(barrier, inc=1, device_id=peer, device_id_type=pl.DeviceIdType.MESH)
+    pl.semaphore_wait(barrier, len(peers))
+
+
+def column(row):
+    return jnp.broadcast_to(row.astype(F32), (LANES, row.shape[1])).T
+
+
+def rotary_tables(parity, rows, c_ref, lo_ref, hi_ref):
     half = rows // 2
-    parity = par_ref[0]
-    lane = lax.broadcasted_iota(jnp.int32, (half, LANES), 1)
-
-    @pl.when(pl.program_id(0) == 0)
-    def _():
+    lane = lax.broadcasted_iota(jnp.int32, (1, LANES), 1) % HD
+    frequency = jnp.zeros((1, LANES), F32)
+    for k in range(ROT // 2):
+        value = 10000.0 ** (-2.0 * k / ROT)
+        frequency = jnp.where((lane < ROT) & (lane % (ROT // 2) == k), value, frequency)
+    step = 64
+
+    def chunk(i, carry):
+        row = i * step + lax.broadcasted_iota(jnp.int32, (step, LANES), 0)
+        late = (i * step) // half
+        quarter = parity + late * (3 - 2 * parity)
+        position = (row - late * half + quarter * half).astype(F32)
+        grid = position * frequency
+        at = pl.ds(pl.multiple_of(i * step, step), step)
+        sine = jnp.sin(grid)
+        c_ref[at, :] = jnp.cos(grid)
+        lo_ref[at, :] = jnp.where(lane < ROT // 2, -sine, 0.0)
+        hi_ref[at, :] = jnp.where((lane >= ROT // 2) & (lane < ROT), sine, 0.0)
+        return carry
+
+    lax.fori_loop(0, rows // step, chunk, 0)
+
+
+def fwd_kernel(
+    total, replica_bits,
+    m_ref, v_ref, x_ref, t_ref, valid_ref, seg_ref,
+    w_out, n1t_out, n2t_out, obt_out, gbt_out, q_out, kv_out, kvo_out, ob_out, hb_out, dg_out, gy_out, gb_out, tab_out,
+    lse_ref, sum_ref, par_ref, scale_ref,
+    w, stage, vbuf, n1, n2, n1t, n2t, qkv, kvo, hb, dg, ob, fy, sc, top, acc, mask, kpos, vpos, tab, cnt, cnt_in,
+    sem_m, sem_w, sem_s, sem_r, sem_vs, sem_vr, sem_ks, sem_kr, sem_cs, sem_cr, sem_o,
+):
+    rows, width = x_ref.shape
+    half = rows // 2
+    stack = m_ref.shape[1]
+    chunks = stack // CHUNK
+    hidden = (stack - 4 * width) // 2
+    per = hidden // CHUNK
+    s = lax.axis_index("shard")
+    z = lax.axis_index("dp")
+    sb = bits_of(s, 3)
+    zb = bits_of(z, replica_bits)
+    core, x, y = sb
+    parity = core
+    to = [{"shard": flipped(sb, k)} for k in range(8)]
+    to_z = [{"dp": z + (1 - 2 * zb[l]) * (1 << l)} for l in range(replica_bits)]
+    blk = [flipped(sb, k) for k in range(8)]
+    CORE, XX, YY = 1, 2, 4
+
+    def load(c):
+        return pltpu.make_async_copy(m_ref.at[:, c * CHUNK : (c + 1) * CHUNK], stage.at[c % 3], sem_m.at[c % 3])
+
+    for c in range(3):
+        load(c).start()
+    meet(to[1:] + to_z)
+
+    vbuf[pl.ds(s, 1)] = v_ref[...].reshape(1, 16, LANES)
+    v_sends = [remote(v_ref, vbuf.at[s], sem_vs.at[k - 1], sem_vr.at[k - 1], to[k]) for k in range(1, 8)]
+    for copy in v_sends:
+        copy.start()
+
+    def cols(c):
+        return pl.ds(pl.multiple_of(c * CHUNK, CHUNK), CHUNK)
+
+    def copy(kind, c):
+        at = cols(c)
+        top_half, low_half = pl.ds(0, BS // 2), pl.ds(BS // 2, BS // 2)
+        if kind < 3:
+            ref, peer = w.at[s, :, at], to[(XX, YY, CORE)[kind]]
+        elif kind == 3:
+            ref, peer = w.at[blk[XX], top_half, at], to[YY]
+        elif kind == 4:
+            ref, peer = w.at[blk[YY], low_half, at], to[XX]
+        else:
+            ref, peer = w.at[blk[(XX, YY, XX + YY)[kind - 5]], :, at], to[CORE]
+        return remote(ref, ref, sem_s.at[kind, c], sem_r.at[kind, c], peer)
+
+    def send(c):
+        for kind in range(3):
+            copy(kind, c).start()
+
+    def forward(c):
+        copy(0, c).wait()
+        copy(1, c).wait()
+        for kind in (3, 4, 5, 6):
+            copy(kind, c).start()
+
+    def corner(c):
+        copy(3, c).wait()
+        copy(4, c).wait()
+        copy(7, c).start()
+
+    def w_copy(c):
+        return pltpu.make_async_copy(w.at[:, :, cols(c)], w_out.at[:, :, cols(c)], sem_w.at[c])
+
+    def finish(c):
+        for kind in (2, 5, 6, 7):
+            copy(kind, c).wait()
+        w_copy(c).start()
+
+    for c in range(chunks):
+        load(c).wait()
+        w[pl.ds(s, 1), :, c * CHUNK : (c + 1) * CHUNK] = stage[c % 3].astype(BF16).reshape(1, BS, CHUNK)
+        if c + 3 < chunks:
+            load(c + 3).start()
+        if c < 2:
+            send(c)
+
+    def hop(k):
+        return remote(cnt.at[k], cnt_in.at[k], sem_cs.at[k], sem_cr.at[k], ([to[1], to[2], to[4]] + to_z)[k])
+
+    hops = 3 + replica_bits
+    cnt[0] = jnp.full((8, LANES), jnp.sum(valid_ref[...]), F32)
+    hop(0).start()
+
+    rotary_tables(parity, rows, tab.at[0], tab.at[1], tab.at[2])
+    for copy_v in v_sends:
+        copy_v.wait()
+    lines = total // (8 * LANES)
+    for k in range(8):
+        block = vbuf[k].astype(BF16).astype(F32)
+        for r in range(lines):
+            flat = (k * lines + r) * LANES
+            par_ref[0:1, flat : flat + LANES] = block[r : r + 1, :]
+
+    def param(start, size):
+        return par_ref[0:1, start : start + size]
+
+    step = 128
+
+    def norms(i, carry):
+        at = pl.ds(pl.multiple_of(i * step, step), step)
+        xh, _ = normed(x_ref[at, :].astype(F32))
+        one = (xh * param(0, width) + param(width, width)).astype(BF16)
+        two = (xh * param(2 * width, width) + param(3 * width, width)).astype(BF16)
+        n1[at, :] = one
+        n2[at, :] = two
+        for b in range(width // BS):
+            n1t[b, :, at] = one[:, b * BS : (b + 1) * BS].T
+            n2t[b, :, at] = two[:, b * BS : (b + 1) * BS].T
+        return carry
+
+    lax.fori_loop(0, rows // step, norms, 0)
+
+    def out(k, src, dst):
+        return pltpu.make_async_copy(src, dst, sem_o.at[k])
+
+    writes = [
+        out(0, n1t, n1t_out), out(1, n2t, n2t_out), out(2, tab, tab_out), out(3, qkv.at[0], q_out),
+        out(4, qkv.at[pl.ds(1, 2)], kv_out), out(5, kvo, kvo_out), out(6, ob, ob_out), out(7, hb, hb_out),
+        out(8, dg, dg_out), out(9, n2t, obt_out), out(10, n1t, gbt_out), out(11, n1, gb_out), out(12, fy, gy_out),
+    ]
+    for k in range(3):
+        writes[k].start()
+
+    first_row = 4 * (s // 2)
+
+    def see(t, carry):
+        b, j = key_tile(t, parity)
+        quarter = jnp.where(b == 0, parity, 3 - parity)
+        qrow = first_row + 2 * parity + b
+        krow = first_row + jnp.where(j == 0, 0, jnp.where(j == 3, 1, j + 1))
+        qseg = column(seg_ref[qrow])
+        for g in range(half // LANES):
+            kseg = seg_ref[krow][:, g * LANES : (g + 1) * LANES].astype(F32)
+            qpos = quarter * half + lax.broadcasted_iota(jnp.int32, (half, LANES), 0)
+            kp = j * half + g * LANES + lax.broadcasted_iota(jnp.int32, (half, LANES), 1)
+            mask[t, :, g * LANES : (g + 1) * LANES] = jnp.where((kp <= qpos) & (qseg == kseg), BIG, NEG)
+        return carry
+
+    lax.fori_loop(0, 5, see, 0)
+    for j in range(4):
+        vpos[j * half : (j + 1) * half, LANES:] = jnp.ones((half, LANES), BF16)
+
+    def kv_send(m):
+        return remote(qkv.at[m], kvo.at[m - 1], sem_ks.at[m - 1], sem_kr.at[m - 1], to[CORE])
+
+    sub = 512
+
+    def project(m):
+        def part(i, carry):
+            off = pl.multiple_of(m * CHUNK + i * sub, sub)
+            wide = w[:, :, pl.ds(off, sub)].reshape(width, sub)
+            proj = dot(n1[...], wide) + par_ref[0:1, pl.ds(pl.multiple_of(4 * width + off, sub), sub)]
+            turned = m < 2
+            for g in range(sub // LANES):
+                piece = proj[:, g * LANES : (g + 1) * LANES]
+                piece = jnp.where(turned, turn(piece, tab[0], tab[1], tab[2]), piece)
+                qkv[m, :, pl.ds(pl.multiple_of(i * sub + g * LANES, LANES), LANES)] = piece.astype(BF16)
+            return carry
+
+        lax.fori_loop(0, CHUNK // sub, part, 0)
+
+    def upward(k):
+        def part(i, carry):
+            off = pl.multiple_of(k * CHUNK + i * sub, sub)
+            wide = w[:, :, pl.ds(pl.multiple_of(4 * width + off, sub), sub)].reshape(width, sub)
+            bias = par_ref[0:1, pl.ds(pl.multiple_of(8 * width + off, sub), sub)]
+            wide_u = dot(n2[...], wide) + bias
+            for g in range(sub // LANES):
+                u = wide_u[:, g * LANES : (g + 1) * LANES]
+                cdf = 0.5 * (1.0 + lax.erf(u * (1.0 / math.sqrt(2.0))))
+                pdf = jnp.exp(-0.5 * u * u) * (1.0 / math.sqrt(2.0 * math.pi))
+                at = pl.ds(pl.multiple_of(off + g * LANES, LANES), LANES)
+                hb[:, at] = (u * cdf).astype(BF16)
+                dg[:, at] = (cdf + u * pdf).astype(BF16)
+            return carry
+
+        lax.fori_loop(0, CHUNK // sub, part, 0)
+
+    def branch():
+        def part(i, carry):
+            at = pl.ds(pl.multiple_of(i * sub, sub), sub)
+            wide = w[:, :, pl.ds(pl.multiple_of(3 * width + i * sub, sub), sub)].reshape(width, sub)
+            bias = par_ref[0:1, pl.ds(pl.multiple_of(7 * width + i * sub, sub), sub)]
+            fy[:, at] = dot(ob[...], wide) + bias
+            return carry
+
+        lax.fori_loop(0, width // sub, part, 0)
+
+    def feed(k):
+        def part(i, carry):
+            at = pl.ds(pl.multiple_of(i * sub, sub), sub)
+            off = pl.ds(pl.multiple_of(4 * width + hidden + k * CHUNK, CHUNK), CHUNK)
+            tall = w[pl.ds(i * (sub // BS), sub // BS), :, off].reshape(sub, CHUNK)
+            fy[:, at] += dot_nt(hb[:, pl.ds(pl.multiple_of(k * CHUNK, CHUNK), CHUNK)], tall)
+            return carry
+
+        lax.fori_loop(0, width // sub, part, 0)
+
+    scale = jnp.asarray(HD**-0.5, BF16)
+
+    def attend(p):
+        lanes = pl.ds(pl.multiple_of(p * LANES, LANES), LANES)
+        place_keys(qkv.at[1, :, lanes], kvo.at[0, :, lanes], kpos, parity)
+        place_keys(qkv.at[2, :, lanes], kvo.at[1, :, lanes], vpos.at[:, 0:LANES], parity)
+        top[...] = jnp.full_like(top, NEG)
+        acc[...] = jnp.zeros_like(acc)
+
+        def score(t, carry):
+            b, j = key_tile(t, parity)
+            both = split_heads(qkv[0, pl.ds(pl.multiple_of(b * half, half), half), lanes] * scale)
+            keys = kpos[pl.ds(pl.multiple_of(j * half, half), half), :]
+            got = dot_nt(both, keys)
+            m = mask[t]
+            got = jnp.concatenate([jnp.minimum(got[:half], m), jnp.minimum(got[half:], m)], axis=0)
+            sc[t] = got
+            best = top[b]
+            for g in range(half // LANES):
+                best = jnp.maximum(best, got[:, g * LANES : (g + 1) * LANES])
+            top[b] = best
+            return carry
+
+        lax.fori_loop(0, 5, score, 0)
         for b in range(2):
-            quarter = parity if b == 0 else 3 - parity
-
-            def one(j, carry):
-                qpos = quarter * half + lax.broadcasted_iota(jnp.int32, (half, half), 0)
-                kpos_ = j * half + lax.broadcasted_iota(jnp.int32, (half, half), 1)
-                same = qseg_ref[b * half : (b + 1) * half, :] == kseg_ref[pl.ds(j, 1), :]
-                mask[b, j] = jnp.where((kpos_ <= qpos) & same, BIG, NEG)
+            top[b] = jnp.broadcast_to(jnp.max(top[b], axis=1, keepdims=True), top.shape[1:])
+
+        def weigh(t, carry):
+            b, j = key_tile(t, parity)
+            best = top[b]
+            prob = jnp.exp(sc[t] - jnp.concatenate([best] * (half // LANES), axis=1)).astype(BF16)
+            acc[b] += dot(prob, vpos[pl.ds(pl.multiple_of(j * half, half), half), :])
+            return carry
+
+        lax.fori_loop(0, 5, weigh, 0)
+        for b in range(2):
+            at = slice(b * half, (b + 1) * half)
+            den = acc[b, :, LANES:]
+            lse = (top[b] + jnp.log(den)).T[0:1, :]
+            lse_ref[p, 0:1, at] = lse[:, :half]
+            lse_ref[p, 1:2, at] = lse[:, half:]
+            got = join_heads(acc[b, :, :LANES] / den).astype(BF16)
+            ob[at, lanes] = got
+            n2t[p, :, at] = got.T
+
+    pairs = width // LANES
+    first_att = 6
+    each = 2
+
+    def tick(k, carry):
+        @pl.when(k < chunks)
+        def _():
+            forward(k)
+
+        @pl.when(k + 2 < chunks)
+        def _():
+            send(k + 2)
+
+        @pl.when((k >= 1) & (k - 1 < chunks))
+        def _():
+            corner(k - 1)
+
+        done = k - 2
+
+        @pl.when(done >= 0)
+        def _():
+            finish(done)
+
+        for h in range(hops):
+            @pl.when(k == h + 1)
+            def _():
+                hop(h).wait()
+                cnt[h + 1] = cnt[h] + cnt_in[h]
+                if h + 1 < hops:
+                    hop(h + 1).start()
+
+        @pl.when((done >= 0) & (done < 3))
+        def _():
+            project(done)
+
+        for m in (1, 2):
+            @pl.when(done == m)
+            def _():
+                kv_send(m).start()
+
+        @pl.when((done >= 4) & (done < 4 + per))
+        def _():
+            upward(done - 4)
+
+        @pl.when(k == first_att)
+        def _():
+            for m in (1, 2):
+                kv_send(m).wait()
+            writes[3].start()
+            writes[4].start()
+            writes[5].start()
+            writes[1].wait()
+
+        @pl.when((k >= first_att) & (k < first_att + pairs // each))
+        def _():
+            def pair(i, carry):
+                attend((k - first_att) * each + i)
                 return carry
 
-            lax.fori_loop(0, 4, one, 0)
-        for j in range(4):
-            vpos[j * half : (j + 1) * half, LANES:] = jnp.ones((half, LANES), BF16)
-
-    place_keys(k_ref, ko_ref, kpos, parity)
-    place_keys(v_ref, vo_ref, vpos.at[:, 0:LANES], parity)
-    for b in range(2):
-        quarter = parity if b == 0 else 3 - parity
-        at = slice(b * half, (b + 1) * half)
-        both = q_ref[at, :] * jnp.asarray(HD**-0.5, BF16)
-        outs = []
-        for h in range(2):
-            mine = (lane < HD) if h == 0 else (lane >= HD)
-            qh = jnp.where(mine, both, jnp.zeros_like(both))
-
-            def score(j, top):
-                keys = kpos[pl.ds(pl.multiple_of(j * half, half), half), :]
-                s = jnp.minimum(dot_nt(qh, keys), mask[b, j])
-                sc[j] = s
-                for g in range(half // LANES):
-                    top = jnp.maximum(top, s[:, g * LANES : (g + 1) * LANES])
-                return top
-
-            top = lax.fori_loop(0, quarter + 1, score, jnp.full((half, LANES), NEG, F32))
-            top = jnp.broadcast_to(jnp.max(top, axis=1, keepdims=True), (half, LANES))
-            top_wide = jnp.concatenate([top] * (half // LANES), axis=1)
-
-            def weigh(j, acc):
-                p = jnp.exp(sc[j] - top_wide).astype(BF16)
-                return acc + dot(p, vpos[pl.ds(pl.multiple_of(j * half, half), half), :])
-
-            acc = lax.fori_loop(0, quarter + 1, weigh, jnp.zeros((half, 2 * LANES), F32))
-            den = acc[:, LANES:]
-            outs.append(acc[:, :LANES] / den)
-            lse = top + jnp.log(den)
-            lse_ref[0, h : h + 1, at] = lse.T[0:1, :]
-        out = jnp.where(lane < HD, outs[0], outs[1]).astype(BF16)
-        o_ref[at, :] = out
-        ot_ref[0, :, at] = out.T
-
-
-def att_fwd(parity, q, kv, kvo, qseg, kseg):
-    rows, width = q.shape
-    pairs = width // LANES
+            lax.fori_loop(0, each, pair, 0)
+
+        @pl.when(k == first_att + pairs // each)
+        def _():
+            writes[6].start()
+            writes[9].start()
+            branch()
+            writes[7].start()
+            writes[8].start()
+
+        @pl.when(done >= 4 + per)
+        def _():
+            feed(done - 4 - per)
+
+        return carry
+
+    lax.fori_loop(0, chunks + 2, tick, 0)
+    count = cnt[hops]
+    weight = rows * (1 << hops) / count
+    scale_ref[...] = weight
+    writes[0].wait()
+    some = 128
+
+    def loss(i, carry):
+        at = pl.ds(pl.multiple_of(i * some, some), some)
+        bias = par_ref[0:1, pl.ds(pl.multiple_of(8 * width + hidden + i * some, some), some)]
+        out_y = x_ref[:, at].astype(F32) + (fy[:, at] + bias)
+        g = weight[0:1, :] * valid_ref[...] * (out_y - t_ref[:, at].astype(F32))
+        low = g.astype(BF16)
+        fy[:, at] = g
+        n1[:, at] = low
+        n1t[i] = low.T
+        sum_ref[0:1, at] = jnp.sum(low.astype(F32), axis=0, keepdims=True)
+        return carry
+
+    lax.fori_loop(0, width // some, loss, 0)
+    for k in (10, 11, 12):
+        writes[k].start()
+    for k in range(2, 13):
+        if k != 1:
+            writes[k].wait()
+
+    def drain(c, carry):
+        w_copy(c).wait()
+        return carry
+
+    lax.fori_loop(0, chunks, drain, 0)
+
+
+def forward_pass(master, vec, tokens, targets, valid, seg, replicas, total):
+    rows, width = tokens.shape
     half = rows // 2
-    col = lambda off: pl.BlockSpec((rows, LANES), lambda p, r: (0, p + off))
-    return call(
-        att_fwd_kernel,
-        (pairs,),
-        [col(0), col(0), col(pairs), col(0), col(pairs), whole((rows, 1)), whole((4, half))],
-        [
-            col(0),
-            pl.BlockSpec((1, LANES, rows), lambda p, r: (p, 0, 0)),
-            pl.BlockSpec((1, 2, rows), lambda p, r: (p, 0, 0)),
+    stack = master.shape[1]
+    chunks = stack // CHUNK
+    hidden = (stack - 4 * width) // 2
+    replica_bits = replicas.bit_length() - 1
+    assert replicas == 1 << replica_bits
+    blocks = width // BS
+    hops = 3 + replica_bits
+    anyspace = pl.BlockSpec(memory_space=pl.ANY)
+    vmem = pl.BlockSpec(memory_space=pltpu.VMEM)
+    dma = pltpu.SemaphoreType.DMA
+    turned = sds((blocks, BS, rows), BF16)
+    flat = sds((rows, width), BF16)
+    two = sds((2, rows, width), BF16)
+    tall = sds((rows, hidden), BF16)
+    return pl.pallas_call(
+        partial(fwd_kernel, total, replica_bits),
+        out_shape=[
+            sds((blocks, BS, stack), BF16), turned, turned, turned, turned, flat, two, two, flat, tall, tall,
+            sds((rows, width), F32), flat, sds((3, rows, LANES), F32),
+            sds((blocks, 2, rows), F32), sds((1, width), F32), sds((1, total), F32), sds((8, LANES), F32),
         ],
-        [sds((rows, width), BF16), sds((pairs, LANES, rows), BF16), sds((pairs, 2, rows), F32)],
-        [
-            pltpu.VMEM((2, 4, half, half), F32),
+        in_specs=[anyspace] + [vmem] * 5,
+        out_specs=[anyspace] * 14 + [vmem] * 4,
+        scratch_shapes=[
+            pltpu.VMEM((blocks, BS, stack), BF16),
+            pltpu.VMEM((3, BS, CHUNK), F32),
+            pltpu.VMEM((8, 16, LANES), F32),
+            pltpu.VMEM((rows, width), BF16),
+            pltpu.VMEM((rows, width), BF16),
+            pltpu.VMEM((blocks, BS, rows), BF16),
+            pltpu.VMEM((blocks, BS, rows), BF16),
+            pltpu.VMEM((3, rows, width), BF16),
+            pltpu.VMEM((2, rows, width), BF16),
+            pltpu.VMEM((rows, hidden), BF16),
+            pltpu.VMEM((rows, hidden), BF16),
+            pltpu.VMEM((rows, width), BF16),
+            pltpu.VMEM((rows, width), F32),
+            pltpu.VMEM((5, rows, half), F32),
+            pltpu.VMEM((2, rows, LANES), F32),
+            pltpu.VMEM((2, rows, 2 * LANES), F32),
+            pltpu.VMEM((5, half, half), F32),
             pltpu.VMEM((2 * rows, LANES), BF16),
             pltpu.VMEM((2 * rows, 2 * LANES), BF16),
-            pltpu.VMEM((4, half, half), F32),
+            pltpu.VMEM((3, rows, LANES), F32),
+            pltpu.VMEM((hops + 1, 8, LANES), F32),
+            pltpu.VMEM((hops, 8, LANES), F32),
+            dma((3,)), dma((chunks,)), dma((8, chunks)), dma((8, chunks)), dma((7,)), dma((7,)),
+            dma((2,)), dma((2,)), dma((hops,)), dma((hops,)), dma((13,)),
         ],
-        prefetch=1,
-        cost=cost(4 * rows * 2 * rows * width, 2 * 8 * rows * width, 2 * rows * rows * width // HD),
-    )(parity, q, kv, kv, kvo, kvo, qseg, kseg)
+        compiler_params=pltpu.CompilerParams(
+            collective_id=1, has_side_effects=True, vmem_limit_bytes=59 * MIB
+        ),
+    )(master, vec, tokens, targets, valid, seg)
 
 
 def att_bwd_kernel(
     par_ref, q_ref, k_ref, v_ref, ko_ref, vo_ref, g_ref, o_ref, lse_ref, qseg_ref, kseg_ref, c_ref, lo_ref, hi_ref,
-    dq_ref, dk_ref, dv_ref, dko_ref, dvo_ref, mask, kpos, vpos, dkpos, dvpos,
+    dq_ref, dk_ref, dv_ref, dko_ref, dvo_ref, mask, kpos, vpos, dkpos, dvpos, dqs, qcat, gcat, rowsum,
 ):
     rows = q_ref.shape[0]
     half = rows // 2
     parity = par_ref[0]
-    lane = lax.broadcasted_iota(jnp.int32, (half, LANES), 1)
-    lane_k = lane
 
     @pl.when(pl.program_id(0) == 0)
     def _():
-        for b in range(2):
-            quarter = parity if b == 0 else 3 - parity
-
-            def one(j, carry):
-                kp = j * half + lax.broadcasted_iota(jnp.int32, (half, half), 0)
-                qp = quarter * half + lax.broadcasted_iota(jnp.int32, (half, half), 1)
-                same = kseg_ref[pl.ds(pl.multiple_of(j * half, half), half), :] == qseg_ref[b : b + 1, :]
-                mask[b, j] = jnp.where((kp <= qp) & same, BIG, NEG)
-                return carry
-
-            lax.fori_loop(0, 4, one, 0)
+        def one(t, carry):
+            b, j = key_tile(t, parity)
+            quarter = jnp.where(b == 0, parity, 3 - parity)
+            kp = j * half + lax.broadcasted_iota(jnp.int32, (half, half), 0)
+            qp = quarter * half + lax.broadcasted_iota(jnp.int32, (half, half), 1)
+            same = kseg_ref[pl.ds(pl.multiple_of(j * half, half), half), :] == qseg_ref[pl.ds(b, 1), :]
+            mask[t] = jnp.where((kp <= qp) & same, BIG, NEG)
+            return carry
+
+        lax.fori_loop(0, 5, one, 0)
 
     place_keys(k_ref, ko_ref, kpos, parity)
     place_keys(v_ref, vo_ref, vpos, parity)
     dkpos[...] = jnp.zeros_like(dkpos)
     dvpos[...] = jnp.zeros_like(dvpos)
+    dqs[...] = jnp.zeros_like(dqs)
     scale = HD**-0.5
     for b in range(2):
-        quarter = parity if b == 0 else 3 - parity
         at = slice(b * half, (b + 1) * half)
-        qs = q_ref[at, :] * jnp.asarray(scale, BF16)
+        qcat[b] = split_heads(q_ref[at, :] * jnp.asarray(scale, BF16))
         gs = g_ref[at, :]
+        gcat[b] = split_heads(gs)
         prod = (gs.astype(F32) * o_ref[at, :].astype(F32)).T
-        zero = jnp.zeros_like(qs)
-        parts = []
-        for h in range(2):
-            mine = (lane < HD) if h == 0 else (lane >= HD)
-            qh = jnp.where(mine, qs, zero)
-            gh = jnp.where(mine, gs, zero)
-            lse = lse_ref[0, h : h + 1, at]
-            delta = jnp.sum(prod[h * HD : (h + 1) * HD, :], axis=0, keepdims=True)
-
-            def tile(j, acc):
-                ks = pl.ds(pl.multiple_of(j * half, half), half)
-                keys = kpos[ks, :]
-                s = jnp.minimum(dot_nt(keys, qh), mask[b, j])
-                p = jnp.exp(s - lse)
-                dp = dot_nt(vpos[ks, :], gh)
-                ds = (p * (dp - delta)).astype(BF16)
-                dvpos[ks, :] += dot(p.astype(BF16), gh)
-                dkpos[ks, :] += dot(ds, qh)
-                return acc + dot(ds, keys, ((0,), (0,)))
-
-            parts.append(lax.fori_loop(0, quarter + 1, tile, jnp.zeros((half, LANES), F32)))
-        dq = jnp.where(lane < HD, parts[0], parts[1]) * scale
+        rowsum[b, 0:1, :half] = lse_ref[0, 0:1, at]
+        rowsum[b, 0:1, half:] = lse_ref[0, 1:2, at]
+        rowsum[b, 1:2, :half] = jnp.sum(prod[:HD, :], axis=0, keepdims=True)
+        rowsum[b, 1:2, half:] = jnp.sum(prod[HD:, :], axis=0, keepdims=True)
+
+    def tile(t, carry):
+        b, j = key_tile(t, parity)
+        ks = pl.ds(pl.multiple_of(j * half, half), half)
+        keys = kpos[ks, :]
+        qh, gh = qcat[b], gcat[b]
+        m = mask[t]
+        s = dot_nt(keys, qh)
+        s = jnp.concatenate([jnp.minimum(s[:, :half], m), jnp.minimum(s[:, half:], m)], axis=1)
+        p = jnp.exp(s - rowsum[b, 0:1, :])
+        dp = dot_nt(vpos[ks, :], gh)
+        ds = (p * (dp - rowsum[b, 1:2, :])).astype(BF16)
+        dvpos[ks, :] += dot(p.astype(BF16), gh)
+        dkpos[ks, :] += dot(ds, qh)
+        dqs[b] += dot(ds, keys, ((0,), (0,)))
+        return carry
+
+    lax.fori_loop(0, 5, tile, 0)
+    for b in range(2):
+        at = slice(b * half, (b + 1) * half)
+        dq = join_heads(dqs[b]) * scale
         dq_ref[at, :] = turn(dq, c_ref[at, :], -lo_ref[at, :], -hi_ref[at, :]).astype(BF16)
     for src, mine, theirs in ((dkpos, dk_ref, dko_ref), (dvpos, dv_ref, dvo_ref)):
         for b in range(2):
@@ -318,87 +641,34 @@
     pairs = width // LANES
     half = rows // 2
     col = lambda off: pl.BlockSpec((rows, LANES), lambda p, r: (0, p + off))
+    kvc = lambda which: pl.BlockSpec((None, rows, LANES), lambda p, r: (which, 0, p))
     out = sds((rows, width), F32)
     low = sds((rows, width), BF16)
     return call(
         att_bwd_kernel,
         (pairs,),
         [
-            col(0), col(0), col(pairs), col(0), col(pairs), col(0), col(0),
+            col(0), kvc(0), kvc(1), kvc(0), kvc(1), col(0), col(0),
             pl.BlockSpec((1, 2, rows), lambda p, r: (p, 0, 0)),
             whole((2, half)), whole((2 * rows, 1)),
-            whole((rows, LANES)), whole((rows, LANES)), whole((rows, LANES)),
+            *[pl.BlockSpec((None, rows, LANES), lambda p, r, k=k: (k, 0, 0)) for k in range(3)],
         ],
         [col(0)] * 5,
         [low, out, out, low, low],
         [
-            pltpu.VMEM((2, 4, half, half), F32),
+            pltpu.VMEM((5, half, half), F32),
             pltpu.VMEM((2 * rows, LANES), BF16),
             pltpu.VMEM((2 * rows, LANES), BF16),
             pltpu.VMEM((2 * rows, LANES), F32),
             pltpu.VMEM((2 * rows, LANES), F32),
+            pltpu.VMEM((2, rows, LANES), F32),
+            pltpu.VMEM((2, rows, LANES), BF16),
+            pltpu.VMEM((2, rows, LANES), BF16),
+            pltpu.VMEM((2, 8, rows), F32),
         ],
         prefetch=1,
         cost=cost(10 * rows * 2 * rows * width, 2 * 16 * rows * width, 2 * rows * rows * width // HD),
-    )(parity, q, kv, kv, kvo, kvo, gob, ob, lse, qseg, kseg, *tables)
-
-
-def up_kernel(n2_ref, w_ref, b_ref, h_ref, dg_ref):
-    u_all = dot(n2_ref[...], w_ref[...]) + b_ref[...]
-    for g in range(u_all.shape[1] // LANES):
-        at = slice(g * LANES, (g + 1) * LANES)
-        u = u_all[:, at]
-        cdf = 0.5 * (1.0 + lax.erf(u * (1.0 / math.sqrt(2.0))))
-        h_ref[:, at] = (u * cdf).astype(BF16)
-        pdf = jnp.exp(-0.5 * u * u) * (1.0 / math.sqrt(2.0 * math.pi))
-        dg_ref[:, at] = (cdf + u * pdf).astype(BF16)
-
-
-def up(n2, w, b):
-    rows, width = n2.shape
-    hidden = w.shape[1]
-    cols = 512
-    blk = pl.BlockSpec((rows, cols), lambda j: (0, j))
-    return call(
-        up_kernel,
-        (hidden // cols,),
-        [whole((rows, width)), pl.BlockSpec((width, cols), lambda j: (0, j)), pl.BlockSpec((1, cols), lambda j: (0, j))],
-        [blk, blk],
-        [sds((rows, hidden), BF16), sds((rows, hidden), BF16)],
-        cost=cost(2 * rows * width * hidden, 2 * (width * hidden + 2 * rows * hidden), 2 * rows * hidden),
-    )(n2, w, b)
-
-
-def out_kernel(ob_ref, hb_ref, wo_ref, wd_ref, bo_ref, bd_ref, x_ref, t_ref, valid_ref, gy_ref, gb_ref, gbt_ref, sum_ref):
-    branch = dot(ob_ref[...], wo_ref[...]) + bo_ref[...]
-    feed = dot_nt(hb_ref[...], wd_ref[...]) + bd_ref[...]
-    y = x_ref[...].astype(F32) + (branch + feed)
-    g = valid_ref[...] * (y - t_ref[...].astype(F32))
-    low = g.astype(BF16)
-    gy_ref[...] = g
-    gb_ref[...] = low
-    gbt_ref[...] = low.T
-    sum_ref[...] = jnp.sum(low.astype(F32), axis=0, keepdims=True)
-
-
-def out_grad(ob, hb, wo, wd, bo, bd, x, t, valid):
-    rows, width = ob.shape
-    hidden = hb.shape[1]
-    cols = 256
-    col = pl.BlockSpec((rows, cols), lambda j: (0, j))
-    vec = pl.BlockSpec((1, cols), lambda j: (0, j))
-    return call(
-        out_kernel,
-        (width // cols,),
-        [
-            whole((rows, width)), whole((rows, hidden)),
-            pl.BlockSpec((width, cols), lambda j: (0, j)), pl.BlockSpec((cols, hidden), lambda j: (j, 0)),
-            vec, vec, col, col, whole((rows, 1)),
-        ],
-        [col, col, pl.BlockSpec((cols, rows), lambda j: (j, 0)), vec],
-        [sds((rows, width), F32), sds((rows, width), BF16), sds((width, rows), BF16), sds((1, width), F32)],
-        cost=cost(2 * rows * width * (width + hidden), 2 * (width * (width + hidden) + 6 * rows * width)),
-    )(ob, hb, wo, wd, bo, bd, x, t, valid)
+    )(parity, q, kv, kv, kvo, kvo, gob, ob, lse, qseg, kseg, tables, tables, tables)
 
 
 def dgrad_kernel(gb_ref, wo_ref, wd_ref, wu_ref, dg_ref, gob_ref, gub_ref, sum_ref, gn2_ref):
@@ -414,20 +684,23 @@
     gn2_ref[...] += dot_nt(gub, wu_ref[...])
 
 
-def dgrad(gb, wo, wd, wu, dg):
+def dgrad(gb, w, dg):
     rows, width = gb.shape
     hidden = dg.shape[1]
     cols = 512
     blk = pl.BlockSpec((rows, cols), lambda j: (0, j))
-    wblk = pl.BlockSpec((width, cols), lambda j: (0, j))
+    wblk = lambda off: pl.BlockSpec((width, cols), lambda j: (0, j + off // cols))
     return call(
         dgrad_kernel,
         (hidden // cols,),
-        [whole((rows, width)), whole((width, width)), wblk, wblk, blk],
+        [
+            whole((rows, width)), pl.BlockSpec((width, width), lambda j: (0, 3)),
+            wblk(4 * width + hidden), wblk(4 * width), blk,
+        ],
         [whole((rows, width)), blk, pl.BlockSpec((1, cols), lambda j: (0, j)), whole((rows, width))],
         [sds((rows, width), BF16), sds((rows, hidden), BF16), sds((1, hidden), F32), sds((rows, width), F32)],
         cost=cost(2 * rows * width * (width + 2 * hidden), 2 * (width * (width + 2 * hidden) + 6 * rows * width)),
-    )(gb, wo, wd, wu, dg)
+    )(gb, w, w, w, dg)
 
 
 def last_kernel(
@@ -496,7 +769,7 @@
         (3 * nq,),
         [
             at(0), at(1), at(2), at(1), at(2),
-            whole((rows, LANES)), whole((rows, LANES)), whole((rows, LANES)),
+            *[pl.BlockSpec((None, rows, LANES), lambda j, k=k: (k, 0, 0)) for k in range(3)],
             pl.BlockSpec((width, cols), lambda j: (0, j)),
             whole((rows, width)), whole(vec4.shape), whole((rows, width)), whole((rows, width)),
         ],
@@ -507,7 +780,7 @@
         [sds((rows, 3 * width), BF16), sds((rows, width), F32), sds((4, width), F32), sds((1, 3 * width), F32)],
         [pltpu.VMEM((rows, width), F32)],
         cost=cost(6 * rows * width * width, 2 * (3 * width * width + 20 * rows * width)),
-    )(dq, dk, dv, dko, dvo, *tables, w, x, vec4, gn2, gy)
+    )(dq, dk, dv, dko, dvo, tables, tables, tables, w, x, vec4, gn2, gy)
 
 
 def update_kernel(f_ref, g_ref, ls_ref, rs_ref, lr_ref, rr_ref, m_ref, nl_ref, nr_ref, nm_ref, mc_ref):
@@ -544,10 +817,6 @@
 
 PAIR = 1024
 TILE = PAIR // 2
-
-
-def bits_of(index, count):
-    return [(index // (1 << b)) % 2 for b in range(count)]
 
 
 def reduce_kernel(plan, levels, replica_bits, *refs):
@@ -568,15 +837,7 @@
     to_z = [{"dp": z + (1 - 2 * zb[l]) * (1 << l)} for l in range(replica_bits)]
     peers = [to_core, to_x, to_y] + to_z
 
-    barrier = pltpu.get_barrier_semaphore()
-    for peer in peers:
-        pl.semaphore_signal(barrier, inc=1, device_id=peer, device_id_type=pl.DeviceIdType.MESH)
-    pl.semaphore_wait(barrier, len(peers))
-
-    def remote(src, dst, send, recv, peer):
-        return pltpu.make_async_remote_copy(
-            src_ref=src, dst_ref=dst, send_sem=send, recv_sem=recv, device_id=peer, device_id_type=pl.DeviceIdType.MESH
-        )
+    meet(peers)
 
     first = [sum(plan[:w]) for w in range(groups + 1)]
 
@@ -837,21 +1098,6 @@
     )(*[a.reshape(4, 2, BS, tokens) for a in ats], *bs, vec)
 
 
-def angles(positions):
-    half_rot = ROT // 2
-    frequency = jnp.power(10000.0, -2.0 * jnp.arange(half_rot, dtype=F32) / ROT)
-    grid = positions.astype(F32)[:, None] * frequency[None, :]
-    cosine, sine = jnp.cos(grid), jnp.sin(grid)
-    rows = positions.shape[0]
-    ones = jnp.ones((rows, HD - ROT), F32)
-    zero = jnp.zeros((rows, HD - ROT), F32)
-    blank = jnp.zeros((rows, half_rot), F32)
-    c = jnp.concatenate([cosine, cosine, ones] * 2, axis=1)
-    lo = jnp.concatenate([-sine, blank, zero] * 2, axis=1)
-    hi = jnp.concatenate([blank, sine, zero] * 2, axis=1)
-    return c, lo, hi
-
-
 def body(
     tokens, targets, segments, valid, master, vectors, left_stat, right_stat, left_root, right_root, vector_stat,
 ):
@@ -866,39 +1112,21 @@
     par = parity.astype(jnp.int32).reshape(1)
     swap = [(i, i ^ 1) for i in range(shards)]
 
-    low = master.astype(BF16)
-    w_qkv = lax.all_gather(low[:, : 3 * width], "shard", axis=0, tiled=True)
-    w_rest = lax.all_gather(low[:, 3 * width :], "shard", axis=0, tiled=True)
-    params = lax.all_gather(vectors.astype(BF16), "shard", axis=0, tiled=True).astype(F32)
-    w_out = w_rest[:, :width]
-    w_up = w_rest[:, width : width + hidden]
-    w_down = w_rest[:, width + hidden :]
-
-    vec4 = params[: 4 * width].reshape(4, width)
-    b_qkv = params[4 * width : 7 * width].reshape(1, -1)
-    b_out = params[7 * width : 8 * width].reshape(1, -1)
-    b_up = params[8 * width : 8 * width + hidden].reshape(1, -1)
-    b_down = params[8 * width + hidden :].reshape(1, -1)
-
-    valid_float = valid.astype(F32)
-
-    local = jnp.arange(half, dtype=jnp.int32)
-    positions = jnp.concatenate([parity * half + local, (3 - parity) * half + local])
-    tables = angles(positions)
     start = (index - parity) * rows
     sequence = lax.dynamic_slice_in_dim(segments, start, 2 * rows).reshape(4, half)
     key_seg = jnp.stack([sequence[0], sequence[2], sequence[3], sequence[1]])
     own_seg = lax.dynamic_slice_in_dim(segments, index * rows, rows)
 
-    n1t, n2, n2t, q, kv = pre(tokens, vec4, w_qkv, b_qkv, tables)
-    kvo = lax.ppermute(kv, "shard", swap)
-    hb, dg = up(n2, w_up, b_up)
-    ob, obt, lse = att_fwd(par, q, kv, kvo, own_seg.reshape(rows, 1), key_seg)
-    obt = obt.reshape(width, rows)
-    gy, gb, gbt, gb_sum = out_grad(
-        ob, hb, w_out, w_down, b_out, b_down, tokens, targets, valid_float.reshape(rows, 1)
+    own_len = vectors.shape[0]
+    lines = own_len // LANES
+    vec = jnp.pad(vectors.reshape(lines, LANES), ((0, 16 - lines), (0, 0)))
+    (weights, n1t, n2t, obt, gbt, q, kv, kvo, ob, hb, dg, gy, gb, tables, lse, gb_sum, params, scales) = forward_pass(
+        master, vec, tokens, targets, valid.astype(F32).reshape(rows, 1), segments.reshape(-1, 1, half), replicas,
+        own_len * shards,
     )
-    gob, gub, gub_sum, gn2 = dgrad(gb, w_out, w_down, w_up, dg)
+    weights = weights.reshape(width, stack)
+    vec4 = params[0, : 4 * width].reshape(4, width)
+    gob, gub, gub_sum, gn2 = dgrad(gb, weights, dg)
 
     dq, dk, dv, dk_o, dv_o = att_bwd(
         par, q, kv, kvo, gob, ob, lse, own_seg.reshape(2, half), key_seg.reshape(2 * rows, 1), tables
@@ -906,27 +1134,22 @@
     dk_r = lax.ppermute(dk_o, "shard", swap)
     dv_r = lax.ppermute(dv_o, "shard", swap)
     gqkv, input_grad, vec_grad, gqkv_sum = last(
-        dq, dk, dv, dk_r, dv_r, tables, w_qkv, tokens, vec4, gn2, gy
+        dq, dk, dv, dk_r, dv_r, tables, weights, tokens, vec4, gn2, gy
     )
-    own_len = vectors.shape[0]
-    lines = own_len // LANES
     vector_grad = jnp.concatenate(
         [vec_grad.reshape(-1), gqkv_sum.reshape(-1), gb_sum.reshape(-1), gub_sum.reshape(-1), gb_sum.reshape(-1)]
     ).reshape(shards, lines, LANES)
-    tail = jnp.full((shards, 16 - lines, LANES), jnp.sum(valid.astype(F32)), F32)
-    packed = jnp.concatenate([vector_grad, tail], axis=1).reshape(2, 2, 2, 16, LANES)
+    packed = jnp.pad(vector_grad, ((0, 0), (0, 16 - lines), (0, 0))).reshape(2, 2, 2, 16, LANES)
     grads, vec_total, squares = reduce_grads((gbt, obt, n2t, n1t), (hb, gb, gub, gqkv), packed, replicas)
     own_vector = vec_total[:lines].reshape(own_len)
-    scale = rows * shards * replicas / vec_total[lines, 0]
     if replicas <= 8:
         square_sum = jnp.sum(squares)
     else:
         grads = lax.psum_scatter(grads, "dp", scatter_dimension=1, tiled=True)
         grads = lax.all_gather(grads, "dp", axis=1, tiled=True)
         square_sum = jnp.sum(squares) + lax.psum(jnp.sum(jnp.square(grads.astype(F32))), "shard")
-    input_grad = input_grad * scale
-    grad_norm = scale * jnp.sqrt(square_sum)
-    factor = scale * jnp.minimum(1.0, math.sqrt(width * stack / BS) / grad_norm)
+    grad_norm = jnp.sqrt(square_sum)
+    factor = jnp.minimum(1.0, math.sqrt(width * stack / BS) / grad_norm)
     new_left, new_right, new_master, master_copy = update(
         factor.reshape(1, 1), grads, left_stat, right_stat, left_root, right_root, master
     )

time: 479 us -> 375 us (0.78)
  waiting for transfers between devices: 70.7 us -> 3.21 us
  local copies, waits for them, and re-layouts: 37.7 us -> 10.8 us
  Pallas kernels: 331 us -> 354 us
  between operations: 16.9 us -> 2.65 us
  blocking collectives: 10.6 us -> 0 us
  other arithmetic: 9.97 us -> 3.3 us
    all_gather x2 -> x0, waiting for transfers between devices: 66.2 us -> none  [the longest x1 33.4 us: body(): w_qkv = lax.all_gather(low[:, :3 * width], 'shard', axis=0, tiled=True)]
    pallas_call x7 -> x4, Pallas kernels: 161 us -> 184 us  [the longest x1 119 us: forward_pass(): pl.pallas_call(partial(fwd_kernel, total, replica_bits), out_shape=[sds((...]
    slice x9 -> x1, local copies, waits for them, and re-layouts: 19.1 us -> 0.76 us  [body(): vec4 = params[0, :4 * width].reshape(4, width)]
    all_gather x1 -> x0, blocking collectives: 10.6 us -> none  [body(): lax.all_gather(vectors.astype(BF16), 'shard', axis=0, tiled=True)]
    unnamed x55 -> x28, local copies, waits for them, and re-layouts: 13.3 us -> 5.68 us
  transfers between devices with their start and end apart: 5 -> 2, of which waited for: 5 -> 2; matrix products, arithmetic and copies ran while one was open for 2% -> 0% of each run, Pallas kernels for 12% -> 0%
where the time goes in v3:
time: 375 us; the launch traced here: 374 us
  Pallas kernels  354 us (94%)
  local copies, waits for them, and re-layouts  10.8 us (3%)
    pallas_call x1, Pallas kernels, reduce_grads(): pl.pallas_call(partial(reduce_kernel, plan, levels, replica_bits), out_sh...  150 us
    pallas_call x1, Pallas kernels, forward_pass(): pl.pallas_call(partial(fwd_kernel, total, replica_bits), out_shape=[sds((...  119 us
    pallas_call x1, Pallas kernels, att_bwd(): call(att_bwd_kernel, (pairs,), [col(0), kvc(0), kvc(1), kvc(0), kvc(1), c...  31.5 us
    pallas_call x1, Pallas kernels, update(): call(update_kernel, (count // per,), [pl.BlockSpec(memory_space=pltpu.SME...  20.4 us
    pallas_call x1, Pallas kernels, last(): call(last_kernel, (3 * nq,), [at(0), at(1), at(2), at(1), at(2), *[pl.Blo...  16.7 us
    pallas_call x1, Pallas kernels, dgrad(): call(dgrad_kernel, (hidden // cols,), [whole((rows, width)), pl.BlockSpec...  16.4 us
  transfers between devices with their start and end apart: 2, of which 2 were waited for; matrix products, arithmetic and copies ran while one was open for 0% of the time, Pallas kernels for 0%

profile of v3, /device:TPU:0, one launch (start us, length us, event | category | flops | bytes accessed | tf_op | source)
XLA Modules:
  0.0 374.2 jit_solution(15802137287038386866)
XLA Ops:
  0.6 0.8 dynamic_slice.6
  1.4 0.7 convert_element_type.7
  2.1 0.8 dynamic_slice.7
  2.9 0.9 copy.19.valid_ref
  3.8 0.2 copy.22
  4.0 1.3 pad.8.v_ref
  5.3 119.1 %shard_map.170 = (bf16[8,128,12288]{2,1,0:T(8,128)(2,1)}, bf16[8,128,512]{2,1,0:T(8,128)(2,1)}, bf16[8,128,512]{2,1,0:T(8,128)(2,1)}, bf16[8,128,512]{2,1,0:T(8,...) custom-call(f32[128,12288]{1,0:T(8,128)} %m_ref.3, ...), custom_call_target="tpu_custom_call" | custom-call | tf_op jit(solution)/shard_map/pallas_call | solution.py:530
  124.5 0.0 copy-start.1
  124.5 1.2 copy-done.1
  125.7 0.0 copy-start
  125.7 0.0 copy-start.5
  125.7 0.0 copy-start.7
  125.7 16.4 %shard_map.171 = (bf16[512,1024]{1,0:T(8,128)(2,1)S(1)}, bf16[512,4096]{1,0:T(8,128)(2,1)}, f32[1,4096]{1,0:T(1,128)S(1)}, f32[512,1024]{1,0:T(8,128)S(1)}) custom-call(bf16[512,1024]{1,0:T(8,128)(2,1)S(1)} %copy-done.1, bf16[1024,12288]{1,0:T(8,128)(2,1)} %bitcast.38, bf16[1024,12288]{1,0:T(8,128)(2,1)} %bitcast.39, bf16[1024,12288]{1,0:T(8,128)(2,1)} %bitcast.40, ...), custom_call_target="tpu_custom_call" | custom-call | flops 9663676416 | bytes 25165824 | tf_op jit(solution)/shard_map/pallas_call | solution.py:693
  142.1 0.0 copy-start.4
  142.1 1.3 copy-done.4
  143.5 0.0 copy-start.6
  143.5 1.0 copy-done.6
  144.4 0.0 copy-done
  144.4 0.0 copy-done.5
  144.4 0.0 copy-done.7
  144.4 0.0 copy-start.2
  144.4 31.5 %shard_map.172 = (bf16[512,1024]{1,0:T(8,128)(2,1)S(1)}, f32[512,1024]{1,0:T(8,128)}, f32[512,1024]{1,0:T(8,128)}, bf16[512,1024]{1,0:T(8,128)(2,1)}, bf16[512,1024]{1,0:T(8,128)(2,1)}) custom-call(s32[1]{0:T(128)} %bitcast.par_ref, bf16[512,1024]{1,0:T(8,128)(2,1)S(1)} %copy-done.5, bf16[2,512,1024]{2,1,0:T(8,128)(2,1)} %get-tuple-element.46.k_ref.v_ref, ...), custom_call_target="tpu_custom_call" | custom-call | flops 5368709120 | bytes 16777216 | tf_op jit(solution)/shard_map/pallas_call | solution.py:647
  175.9 0.0 collective-permute-start
  176.0 0.5 collective-permute-start.1
  176.5 0.8 slice_reduce_fusion
  177.3 1.7 collective-permute-done.dko_ref
  179.0 1.5 collective-permute-done.1.dvo_ref
  180.5 0.0 copy-done.2
  180.5 0.0 copy-start.9
  180.5 16.7 %shard_map.173 = (bf16[512,3072]{1,0:T(8,128)(2,1)}, f32[512,1024]{1,0:T(8,128)}, f32[4,1024]{1,0:T(4,128)S(1)}, f32[1,3072]{1,0:T(1,128)S(1)}) custom-call(bf16[512,1024]{1,0:T(8,128)(2,1)S(1)} %get-tuple-element.55.dq_ref, f32[512,1024]{1,0:T(8,128)} %get-tuple-element.56.dk_ref, f32[512,1024]{1,0:T(8,128)} %get-tuple-element.57.dv_ref, ...), custom_call_target="tpu_custom_call" | custom-call | flops 3221225472 | bytes 27262976 | tf_op jit(solution)/shard_map/pallas_call | solution.py:767
  197.1 0.0 copy-done.9
  197.2 0.6 pad.9
  197.8 0.0 copy-start.8
  197.8 0.0 copy-start.10
  197.9 149.6 %shard_map.174 = (bf16[128,12288]{1,0:T(8,128)(2,1)}, f32[16,128]{1,0:T(8,128)}, f32[8,128]{1,0:T(8,128)}) custom-call(bf16[4,2,128,512]{3,2,1,0:T(8,128)(2,1)} %bitcast.45, bf16[4,2,128,512]{3,2,1,0:T(8,128)(2,1)} %bitcast.44, bf16[4,2,128,512]{3,2,1,0:T(8,128)(2,1)} %bitcast.43, bf16[4,2,128,512]{3,2,1,0:T(8,128)(2,1)} %bitcast.42, ...), custom_call_target="tpu_custom_call" | custom-call | tf_op jit(solution)/shard_map/pallas_call | solution.py:1087
  347.4 1.3 reduce_sum.9
  349.4 0.0 copy-done.8
  349.5 0.0 copy-done.10
  349.5 1.3 fusion.2
  350.8 0.0 copy-start.3
  350.8 1.9 copy-done.3
  352.7 20.4 %shard_map.175 = (f32[1,96,128,128]{3,2,1,0:T(8,128)}, f32[1,96,128,128]{3,2,1,0:T(8,128)}, f32[128,12288]{1,0:T(8,128)}, bf16[128,12288]{1,0:T(8,128)(2,1)}) custom-call(f32[1,1]{1,0:T(1,128)} %bitcast.17.f_ref, bf16[128,12288]{1,0:T(8,128)(2,1)S(1)} %copy-done.3, f32[1,96,128,128]{3,2,1,0:T(8,128)} %ls_ref.1, f32[1,96,128,128]{3,2,1,0:T(8,128)} %rs_ref.1, ...), custom_call_target="tpu_custom_call" | custom-call | flops 1610612736 | bytes 50331648 | tf_op jit(solution)/shard_map/pallas_call | solution.py:808
  (11 shorter events, 0.1 us)
Async XLA Ops:
  124.5 1.2 copy-start.1
  125.7 18.7 %copy-start = (f32[3,512,128]{2,1,0:T(8,128)S(1)}, f32[3,512,128]{2,1,0:T(8,128)}, u32[]{:S(2)}) copy-start(f32[3,512,128]{2,1,0:T(8,128)} %get-tuple-element.54.c_ref.lo_ref.hi_ref) | copy-start | bytes 2359300
  125.7 18.7 %copy-start.5 = (bf16[512,1024]{1,0:T(8,128)(2,1)S(1)}, bf16[512,1024]{1,0:T(8,128)(2,1)}, u32[]{:S(2)}) copy-start(bf16[512,1024]{1,0:T(8,128)(2,1)} %get-tuple-element.45.q_ref) | copy-start | bytes 3145732
  125.7 18.7 %copy-start.7 = (f32[8,2,512]{2,1,0:T(2,128)S(1)}, f32[8,2,512]{2,1,0:T(2,128)}, u32[]{:S(2)}) copy-start(f32[8,2,512]{2,1,0:T(2,128)} %get-tuple-element.53.lse_ref) | copy-start | bytes 98308
  142.1 1.3 copy-start.4
  143.5 1.0 copy-start.6
  144.4 36.0 %copy-start.2 = (bf16[512,1024]{1,0:T(8,128)(2,1)S(1)}, bf16[512,1024]{1,0:T(8,128)(2,1)}, u32[]{:S(2)}) copy-start(bf16[512,1024]{1,0:T(8,128)(2,1)} %x_ref.3) | copy-start | bytes 3145732
  175.9 3.0 collective-permute-start
  176.0 4.5 %collective-permute-start.1 = (bf16[512,1024]{1,0:T(8,128)(2,1)}, bf16[512,1024]{1,0:T(8,128)(2,1)}, u32[]{:S(2)}, u32[]{:S(2)}) collective-permute-start(bf16[512,1024]{1,0:T(8,128)(2,1)} %get-tuple-element.59), channel_id=1, source_target_pairs={{0,1},{1,0},{2,3},{3,2},{4,5},{5,4},{6,7},{7,6},{8,9},{9,8},{10,11... | collective-permute-start | bytes 3145736 | tf_op jit(solution)/shard_map/ppermute | solution.py:1135
  180.5 16.7 %copy-start.9 = (f32[1,1024]{1,0:T(1,128)S(1)}, f32[1,1024]{1,0:T(1,128)}, u32[]{:S(2)}) copy-start(f32[1,1024]{1,0:T(1,128)} %get-tuple-element.73) | copy-start | bytes 12292
  197.8 151.6 %copy-start.8 = (f32[1664]{0:T(1024)S(1)}, f32[1664]{0:T(1024)}, u32[]{:S(2)}) copy-start(f32[1664]{0:T(1024)} %param.16) | copy-start | bytes 19972
  197.8 151.6 %copy-start.10 = (f32[1664]{0:T(1024)S(1)}, f32[1664]{0:T(1024)}, u32[]{:S(2)}) copy-start(f32[1664]{0:T(1024)} %param.21) | copy-start | bytes 19972
  350.8 1.9 copy-start.3

commit v4 on v3

--- a/solution.py
+++ b/solution.py
@@ -568,221 +568,6 @@
     )(master, vec, tokens, targets, valid, seg)
 
 
-def att_bwd_kernel(
-    par_ref, q_ref, k_ref, v_ref, ko_ref, vo_ref, g_ref, o_ref, lse_ref, qseg_ref, kseg_ref, c_ref, lo_ref, hi_ref,
-    dq_ref, dk_ref, dv_ref, dko_ref, dvo_ref, mask, kpos, vpos, dkpos, dvpos, dqs, qcat, gcat, rowsum,
-):
-    rows = q_ref.shape[0]
-    half = rows // 2
-    parity = par_ref[0]
-
-    @pl.when(pl.program_id(0) == 0)
-    def _():
-        def one(t, carry):
-            b, j = key_tile(t, parity)
-            quarter = jnp.where(b == 0, parity, 3 - parity)
-            kp = j * half + lax.broadcasted_iota(jnp.int32, (half, half), 0)
-            qp = quarter * half + lax.broadcasted_iota(jnp.int32, (half, half), 1)
-            same = kseg_ref[pl.ds(pl.multiple_of(j * half, half), half), :] == qseg_ref[pl.ds(b, 1), :]
-            mask[t] = jnp.where((kp <= qp) & same, BIG, NEG)
-            return carry
-
-        lax.fori_loop(0, 5, one, 0)
-
-    place_keys(k_ref, ko_ref, kpos, parity)
-    place_keys(v_ref, vo_ref, vpos, parity)
-    dkpos[...] = jnp.zeros_like(dkpos)
-    dvpos[...] = jnp.zeros_like(dvpos)
-    dqs[...] = jnp.zeros_like(dqs)
-    scale = HD**-0.5
-    for b in range(2):
-        at = slice(b * half, (b + 1) * half)
-        qcat[b] = split_heads(q_ref[at, :] * jnp.asarray(scale, BF16))
-        gs = g_ref[at, :]
-        gcat[b] = split_heads(gs)
-        prod = (gs.astype(F32) * o_ref[at, :].astype(F32)).T
-        rowsum[b, 0:1, :half] = lse_ref[0, 0:1, at]
-        rowsum[b, 0:1, half:] = lse_ref[0, 1:2, at]
-        rowsum[b, 1:2, :half] = jnp.sum(prod[:HD, :], axis=0, keepdims=True)
-        rowsum[b, 1:2, half:] = jnp.sum(prod[HD:, :], axis=0, keepdims=True)
-
-    def tile(t, carry):
-        b, j = key_tile(t, parity)
-        ks = pl.ds(pl.multiple_of(j * half, half), half)
-        keys = kpos[ks, :]
-        qh, gh = qcat[b], gcat[b]
-        m = mask[t]
-        s = dot_nt(keys, qh)
-        s = jnp.concatenate([jnp.minimum(s[:, :half], m), jnp.minimum(s[:, half:], m)], axis=1)
-        p = jnp.exp(s - rowsum[b, 0:1, :])
-        dp = dot_nt(vpos[ks, :], gh)
-        ds = (p * (dp - rowsum[b, 1:2, :])).astype(BF16)
-        dvpos[ks, :] += dot(p.astype(BF16), gh)
-        dkpos[ks, :] += dot(ds, qh)
-        dqs[b] += dot(ds, keys, ((0,), (0,)))
-        return carry
-
-    lax.fori_loop(0, 5, tile, 0)
-    for b in range(2):
-        at = slice(b * half, (b + 1) * half)
-        dq = join_heads(dqs[b]) * scale
-        dq_ref[at, :] = turn(dq, c_ref[at, :], -lo_ref[at, :], -hi_ref[at, :]).astype(BF16)
-    for src, mine, theirs in ((dkpos, dk_ref, dko_ref), (dvpos, dv_ref, dvo_ref)):
-        for b in range(2):
-            at = slice(b * half, (b + 1) * half)
-            own = parity if b == 0 else 3 - parity
-            other = 1 - parity if b == 0 else 2 + parity
-            mine[at, :] = src[pl.ds(pl.multiple_of(own * half, half), half), :].astype(mine.dtype)
-            theirs[at, :] = src[pl.ds(pl.multiple_of(other * half, half), half), :].astype(BF16)
-
-
-def att_bwd(parity, q, kv, kvo, gob, ob, lse, qseg, kseg, tables):
-    rows, width = q.shape
-    pairs = width // LANES
-    half = rows // 2
-    col = lambda off: pl.BlockSpec((rows, LANES), lambda p, r: (0, p + off))
-    kvc = lambda which: pl.BlockSpec((None, rows, LANES), lambda p, r: (which, 0, p))
-    out = sds((rows, width), F32)
-    low = sds((rows, width), BF16)
-    return call(
-        att_bwd_kernel,
-        (pairs,),
-        [
-            col(0), kvc(0), kvc(1), kvc(0), kvc(1), col(0), col(0),
-            pl.BlockSpec((1, 2, rows), lambda p, r: (p, 0, 0)),
-            whole((2, half)), whole((2 * rows, 1)),
-            *[pl.BlockSpec((None, rows, LANES), lambda p, r, k=k: (k, 0, 0)) for k in range(3)],
-        ],
-        [col(0)] * 5,
-        [low, out, out, low, low],
-        [
-            pltpu.VMEM((5, half, half), F32),
-            pltpu.VMEM((2 * rows, LANES), BF16),
-            pltpu.VMEM((2 * rows, LANES), BF16),
-            pltpu.VMEM((2 * rows, LANES), F32),
-            pltpu.VMEM((2 * rows, LANES), F32),
-            pltpu.VMEM((2, rows, LANES), F32),
-            pltpu.VMEM((2, rows, LANES), BF16),
-            pltpu.VMEM((2, rows, LANES), BF16),
-            pltpu.VMEM((2, 8, rows), F32),
-        ],
-        prefetch=1,
-        cost=cost(10 * rows * 2 * rows * width, 2 * 16 * rows * width, 2 * rows * rows * width // HD),
-    )(parity, q, kv, kv, kvo, kvo, gob, ob, lse, qseg, kseg, tables, tables, tables)
-
-
-def dgrad_kernel(gb_ref, wo_ref, wd_ref, wu_ref, dg_ref, gob_ref, gub_ref, sum_ref, gn2_ref):
-    @pl.when(pl.program_id(0) == 0)
-    def _():
-        gob_ref[...] = dot_nt(gb_ref[...], wo_ref[...]).astype(BF16)
-        gn2_ref[...] = jnp.zeros_like(gn2_ref)
-
-    act = dot(gb_ref[...], wd_ref[...])
-    gub = (act * dg_ref[...].astype(F32)).astype(BF16)
-    gub_ref[...] = gub
-    sum_ref[...] = jnp.sum(gub.astype(F32), axis=0, keepdims=True)
-    gn2_ref[...] += dot_nt(gub, wu_ref[...])
-
-
-def dgrad(gb, w, dg):
-    rows, width = gb.shape
-    hidden = dg.shape[1]
-    cols = 512
-    blk = pl.BlockSpec((rows, cols), lambda j: (0, j))
-    wblk = lambda off: pl.BlockSpec((width, cols), lambda j: (0, j + off // cols))
-    return call(
-        dgrad_kernel,
-        (hidden // cols,),
-        [
-            whole((rows, width)), pl.BlockSpec((width, width), lambda j: (0, 3)),
-            wblk(4 * width + hidden), wblk(4 * width), blk,
-        ],
-        [whole((rows, width)), blk, pl.BlockSpec((1, cols), lambda j: (0, j)), whole((rows, width))],
-        [sds((rows, width), BF16), sds((rows, hidden), BF16), sds((1, hidden), F32), sds((rows, width), F32)],
-        cost=cost(2 * rows * width * (width + 2 * hidden), 2 * (width * (width + 2 * hidden) + 6 * rows * width)),
-    )(gb, w, w, w, dg)
-
-
-def last_kernel(
-    dq_ref, dk_ref, dv_ref, dko_ref, dvo_ref, c_ref, lo_ref, hi_ref, w_ref, x_ref, vec_ref, gn2_ref, gy_ref,
-    gqkv_ref, in_ref, vg_ref, sum_ref, gn1,
-):
-    j = pl.program_id(0)
-    rows, width = x_ref.shape
-    cols = w_ref.shape[1]
-    nq = width // cols
-
-    @pl.when(j == 0)
-    def _():
-        gn1[...] = jnp.zeros_like(gn1)
-
-    @pl.when(j < nq)
-    def _():
-        gqkv_ref[...] = dq_ref[...]
-
-    @pl.when((j >= nq) & (j < 2 * nq))
-    def _():
-        for g in range(cols // LANES):
-            at = slice(g * LANES, (g + 1) * LANES)
-            grad = dk_ref[:, at] + dko_ref[:, at].astype(F32)
-            gqkv_ref[:, at] = turn(grad, c_ref[...], -lo_ref[...], -hi_ref[...]).astype(BF16)
-
-    @pl.when(j >= 2 * nq)
-    def _():
-        gqkv_ref[...] = (dv_ref[...] + dvo_ref[...].astype(F32)).astype(BF16)
-
-    low = gqkv_ref[...]
-    sum_ref[...] = jnp.sum(low.astype(F32), axis=0, keepdims=True)
-    gn1[...] += dot_nt(low, w_ref[...])
-
-    @pl.when(j == 3 * nq - 1)
-    def _():
-        step = 64
-        vg_ref[...] = jnp.zeros_like(vg_ref)
-
-        def chunk(i, carry):
-            at = pl.ds(pl.multiple_of(i * step, step), step)
-            xh, rstd = normed(x_ref[at, :].astype(F32))
-            total = gy_ref[at, :]
-            sums = []
-            for g_n, gain in ((gn1[at, :], vec_ref[0:1, :]), (gn2_ref[at, :], vec_ref[2:3, :])):
-                sums.append(jnp.sum(g_n * xh, axis=0, keepdims=True))
-                sums.append(jnp.sum(g_n, axis=0, keepdims=True))
-                e = g_n * gain
-                mean = jnp.mean(e, axis=-1, keepdims=True)
-                along = jnp.mean(e * xh, axis=-1, keepdims=True)
-                total = total + rstd * (e - mean - xh * along)
-            in_ref[at, :] = total
-            vg_ref[...] += jnp.concatenate(sums, axis=0)
-            return carry
-
-        lax.fori_loop(0, rows // step, chunk, 0)
-
-
-def last(dq, dk, dv, dko, dvo, tables, w, x, vec4, gn2, gy):
-    rows, width = x.shape
-    cols = 512
-    nq = width // cols
-    at = lambda lo: pl.BlockSpec((rows, cols), lambda j: (0, jnp.clip(j - lo * nq, 0, nq - 1)))
-    return call(
-        last_kernel,
-        (3 * nq,),
-        [
-            at(0), at(1), at(2), at(1), at(2),
-            *[pl.BlockSpec((None, rows, LANES), lambda j, k=k: (k, 0, 0)) for k in range(3)],
-            pl.BlockSpec((width, cols), lambda j: (0, j)),
-            whole((rows, width)), whole(vec4.shape), whole((rows, width)), whole((rows, width)),
-        ],
-        [
-            pl.BlockSpec((rows, cols), lambda j: (0, j)), whole((rows, width)), whole((4, width)),
-            pl.BlockSpec((1, cols), lambda j: (0, j)),
-        ],
-        [sds((rows, 3 * width), BF16), sds((rows, width), F32), sds((4, width), F32), sds((1, 3 * width), F32)],
-        [pltpu.VMEM((rows, width), F32)],
-        cost=cost(6 * rows * width * width, 2 * (3 * width * width + 20 * rows * width)),
-    )(dq, dk, dv, dko, dvo, tables, tables, tables, w, x, vec4, gn2, gy)
-
-
 def update_kernel(f_ref, g_ref, ls_ref, rs_ref, lr_ref, rr_ref, m_ref, nl_ref, nr_ref, nm_ref, mc_ref):
     factor = f_ref[0, 0]
     half_sq = 0.5 * factor * factor
@@ -819,88 +604,127 @@
 TILE = PAIR // 2
 
 
-def reduce_kernel(plan, levels, replica_bits, *refs):
+def bwd_kernel(plan, levels, replica_bits, lines, *refs):
     groups = len(plan)
     pairs = sum(plan)
-    at_refs, b_refs = refs[:groups], refs[groups : 2 * groups]
-    v_ref, g_out, vec_out, sq_out = refs[2 * groups : 2 * groups + 4]
-    (a_own, a_oth, b_own, b_oth, s1, r1, r2, zs, gs, vr, vd, sq, sq_in,
+    at_refs = refs[:groups]
+    (hb_ref, gb_ref, dg_ref, w_ref, q_ref, kv_ref, kvo_ref, ob_ref, gy_ref, x_ref, tab_ref,
+     lse_ref, par_ref, gbs_ref, seg_ref,
+     g_out, in_out, bo, vec_out, sq_out,
+     a_own, a_oth, b_own, b_oth, s1, r1, r2, zs, gb, gub, gob, gqkv, wr, att, mask, kpos, vpos, dkpos, dvpos, dqs, qcat, gcat,
+     rowsum, own_kv, snd_kv, rcv_kv, tab, gn1, gn2, gy, xs, vg, gus, qs, v, vr, vd, sq, sq_in,
      sem_l, sem_b, sem_as, sem_ar, sem_bs, sem_br, sem_1s, sem_1r, sem_2s, sem_2r,
-     sem_zs, sem_zr, sem_gs, sem_gr, sem_vs, sem_vr, sem_qs, sem_qr, sem_o) = refs[2 * groups + 4 :]
+     sem_zs, sem_zr, sem_gs, sem_gr, sem_vs, sem_vr, sem_qs, sem_qr, sem_o, sem_w, sem_t, sem_i, sem_ks, sem_kr) = refs[groups:]
+    rows, width = gb.shape
+    half = rows // 2
+    hidden = gub.shape[1]
     s = lax.axis_index("shard")
     z = lax.axis_index("dp")
     core, x, y = bits_of(s, 3)
+    parity = core
     zb = bits_of(z, replica_bits)
     to_core = {"shard": s + 1 - 2 * core}
     to_x = {"shard": s + 2 - 4 * x}
     to_y = {"shard": s + 4 - 8 * y}
     to_z = [{"dp": z + (1 - 2 * zb[l]) * (1 << l)} for l in range(replica_bits)]
     peers = [to_core, to_x, to_y] + to_z
-
+    first = [sum(plan[:k]) for k in range(groups + 1)]
+    last = first[3]
+
+    def local(k, src, dst):
+        return pltpu.make_async_copy(src, dst, sem_i.at[k])
+
+    loads = [
+        local(0, gb_ref, gb), local(1, dg_ref, gub), local(2, tab_ref, tab), local(3, gy_ref, gy), local(4, x_ref, xs),
+    ]
+
+    def cols(c):
+        return pl.ds(pl.multiple_of(c * PAIR, PAIR), PAIR)
+
+    chunks_qkv = plan[3]
+    per = plan[2]
+
+    def w_load(c, slot):
+        return pltpu.make_async_copy(w_ref.at[:, :, cols(c)], wr.at[slot], sem_w.at[slot])
+
+    down0 = chunks_qkv + 1 + per
+    up0 = chunks_qkv + 1
+
+    def att_load(p, k):
+        lanes = pl.ds(pl.multiple_of(p * LANES, LANES), LANES)
+        src = (
+            q_ref.at[:, lanes], kv_ref.at[0, :, lanes], kv_ref.at[1, :, lanes],
+            kvo_ref.at[0, :, lanes], kvo_ref.at[1, :, lanes], ob_ref.at[:, lanes],
+        )[k]
+        return pltpu.make_async_copy(src, att.at[p % 2, k], sem_t.at[p % 2, k])
+
+    def a_local(k):
+        return pltpu.make_async_copy(at_refs[k].at[:, core], a_own.at[k], sem_l.at[k])
+
+    def a_send(k):
+        return remote(at_refs[k].at[:, 1 - core], a_oth.at[k], sem_as.at[k], sem_ar.at[k], to_core)
+
+    def b_src(k, i):
+        off = cols(i - first[k])
+        return (hb_ref.at[:, off], gb_ref, gub.at[:, off], gqkv.at[:, off])[k]
+
+    def b_send(k, i):
+        return remote(b_src(k, i), bo.at[i], sem_bs.at[i], sem_br.at[i], to_core)
+
+    def by_group(i, act):
+        for k in range(groups):
+            @pl.when((i >= first[k]) & (i < first[k + 1]))
+            def _():
+                act(k)
+
+    def fetch(i):
+        slot = i % 2
+
+        def act(k):
+            b_send(k, i).wait()
+            pltpu.make_async_copy(b_src(k, i), b_own.at[slot], sem_b.at[0, slot]).start()
+            pltpu.make_async_copy(bo.at[i], b_oth.at[slot], sem_b.at[1, slot]).start()
+
+        by_group(i, act)
+
+    w_load(chunks_qkv, 2).start()
+    loads[0].start()
+    w_load(down0, 0).start()
+    w_load(up0, 1).start()
+    loads[1].start()
+    loads[2].start()
+    for k in range(6):
+        att_load(0, k).start()
     meet(peers)
-
-    first = [sum(plan[:w]) for w in range(groups + 1)]
-
-    def a_local(w):
-        return pltpu.make_async_copy(at_refs[w].at[:, core], a_own.at[w], sem_l.at[w])
-
-    def a_send(w):
-        return remote(at_refs[w].at[:, 1 - core], a_oth.at[w], sem_as.at[w], sem_ar.at[w], to_core)
-
-    def b_cols(w, i):
-        return b_refs[w].at[:, pl.ds(pl.multiple_of((i - first[w]) * PAIR, PAIR), PAIR)]
-
-    def b_send(w, i):
-        return remote(b_cols(w, i), b_oth.at[i], sem_bs.at[i], sem_br.at[i], to_core)
-
-    def b_local(w, i):
-        return pltpu.make_async_copy(b_cols(w, i), b_own.at[i % 2], sem_b.at[i % 2])
-
-    for w in range(groups):
-        a_local(w).start()
-        a_send(w).start()
-        if w == 0:
-            b_local(0, 0).start()
-
-        def launch(i, carry, w=w):
-            b_send(w, i).start()
-            return carry
-
-        lax.fori_loop(first[w], first[w + 1], launch, 0)
-
-    v4 = v_ref
-    vecs = [
-        (v4.at[:, :, 1 - core], vr.at[0, :, :], to_core),
-        (vr.at[0, :, 1 - x], vr.at[1, 0, :], to_x),
-        (vr.at[1, 0, 1 - y], vr.at[1, 1, 0], to_y),
-    ]
-
-    def v_copy(k):
-        if k < 3:
-            src, dst, peer = vecs[k]
-        else:
-            src, dst, peer = vd.at[2 * (k - 3)], vd.at[2 * (k - 3) + 1], to_z[k - 3]
-        return remote(src, dst, sem_vs.at[k], sem_vr.at[k], peer)
-
-    def v_done(k):
-        v_copy(k).wait()
+    for k in range(groups):
+        a_local(k).start()
+        a_send(k).start()
         if k == 0:
-            vr[0] = vr[0] + v4[:, :, core]
-        elif k == 1:
-            vr[1, 0] = vr[1, 0] + vr[0, :, x]
-        else:
-            if k == 2:
-                total = vr[1, 1, 0] + vr[1, 0, y]
-            else:
-                total = vd[2 * (k - 3)] + vd[2 * (k - 3) + 1]
-            vd[2 * (k - 2)] = total
-
-    v_hops = 3 + replica_bits
-    v_copy(0).start()
-    sq[...] = jnp.zeros_like(sq)
+            for i in range(plan[0]):
+                b_send(0, i).start()
+        if k == 1:
+            b_send(1, first[1]).start()
+    loads[3].start()
+    loads[4].start()
+
+    first_row = 4 * (s // 2)
+
+    def see(t, carry):
+        b, j = key_tile(t, parity)
+        quarter = jnp.where(b == 0, parity, 3 - parity)
+        qrow = first_row + 2 * parity + b
+        krow = first_row + jnp.where(j == 0, 0, jnp.where(j == 3, 1, j + 1))
+        kseg = column(seg_ref[krow])
+        for g in range(half // LANES):
+            qseg = seg_ref[qrow][:, g * LANES : (g + 1) * LANES].astype(F32)
+            kp = j * half + lax.broadcasted_iota(jnp.int32, (half, LANES), 0)
+            qp = quarter * half + g * LANES + lax.broadcasted_iota(jnp.int32, (half, LANES), 1)
+            mask[t, :, g * LANES : (g + 1) * LANES] = jnp.where((kp <= qp) & (kseg == qseg), BIG, NEG)
+        return carry
 
     def copy1(i, t):
-        src = s1.at[i, t, :, 1 - x] if t == 0 else s1.at[i, t, 1 - y]
+        slot = i % 2
+        src = s1.at[slot, t, :, 1 - x] if t == 0 else s1.at[slot, t, 1 - y]
         return remote(src, r1.at[i, t], sem_1s.at[i, t], sem_1r.at[i, t], to_x if t == 0 else to_y)
 
     def copy2(i, t):
@@ -917,9 +741,9 @@
     def z_rows(l):
         return pl.ds(starts[l], BS >> (l + 1))
 
-    def level_src(i, l, half):
+    def level_src(i, l, which):
         size = BS >> (l + 1)
-        off = pl.multiple_of(half * size, size)
+        off = pl.multiple_of(which * size, size)
         if l == 0:
             return r2.at[i, pl.ds(off, size)]
         return zs.at[i, pl.ds(pl.multiple_of(starts[l - 1] + off, size), size)]
@@ -929,54 +753,45 @@
             level_src(i, l, 1 - zb[l]), zs.at[i, z_rows(l)], sem_zs.at[i, l], sem_zr.at[i, l], to_z[l]
         )
 
-    def g_rows(l, mine):
-        base = sum((zb[m] * (BS >> (m + 1)) for m in range(l)), 0)
+    def g_rows(l):
+        base = sum((zb[m] * (BS >> (m + 1)) for m in range(l + 1)), 0)
         size = BS >> (l + 1)
-        half = zb[l] if mine else 1 - zb[l]
-        return pl.ds(pl.multiple_of(base + half * size, size), size)
+        return pl.ds(pl.multiple_of(base, size), size)
 
     def copy_g(i, l):
-        return remote(gs.at[i, g_rows(l, True)], gs.at[i, g_rows(l, True)], sem_gs.at[i, l], sem_gr.at[i, l], to_z[l])
-
-    def out_cols(i):
-        total = g_out.shape[1] // PAIR
-        spot = total - first[1] + i
+        return remote(r2.at[i, g_rows(l)], r2.at[i, g_rows(l)], sem_gs.at[i, l], sem_gr.at[i, l], to_z[l])
+
+    def out_copy(i):
+        spot = pairs - first[1] + i
         spot = jnp.where(i >= first[1], i - first[1] + plan[3], spot)
         spot = jnp.where(i >= first[3], i - first[3], spot)
-        return pl.ds(pl.multiple_of(spot * PAIR, PAIR), PAIR)
-
-    def out_copy(i):
-        src = gs.at[i] if levels else r2.at[i]
-        return pltpu.make_async_copy(src, g_out.at[:, out_cols(i)], sem_o.at[i])
+        return pltpu.make_async_copy(r2.at[i], g_out.at[:, cols(spot)], sem_o.at[i])
 
     def stage_a(i):
-        group = sum((jnp.where(i >= first[w], 1, 0) for w in range(1, groups)), 0)
-        for w in range(groups):
-            @pl.when(i == first[w])
+        slot = i % 2
+        group = sum((jnp.where(i >= first[k], 1, 0) for k in range(1, groups)), 0)
+        for k in range(groups):
+            @pl.when(i == first[k])
             def _():
-                a_local(w).wait()
-                a_send(w).wait()
-
-            @pl.when((i + 1 >= first[w]) & (i + 1 < first[w + 1]))
-            def _():
-                b_local(w, i + 1).start()
-
-        slot = i % 2
-        pltpu.make_async_copy(b_oth.at[i], b_own.at[slot], sem_b.at[slot]).wait()
-        remote(b_own.at[slot], b_oth.at[i], sem_bs.at[i], sem_br.at[i], to_core).wait()
+                a_local(k).wait()
+                a_send(k).wait()
+
+        pltpu.make_async_copy(bo.at[i], b_own.at[slot], sem_b.at[0, slot]).wait()
+        pltpu.make_async_copy(bo.at[i], b_oth.at[slot], sem_b.at[1, slot]).wait()
         size = 4 * BS
-        own = a_own[group].reshape(size, a_own.shape[-1])
-        oth = a_oth[group].reshape(size, a_oth.shape[-1])
+        own = a_own[group].reshape(size, rows)
+        oth = a_oth[group].reshape(size, rows)
         for t in range(2):
             at = slice(t * TILE, (t + 1) * TILE)
-            acc = dot(own, b_own[slot, :, at]) + dot(oth, b_oth[i, :, at])
-            s1[i, t] = acc.astype(BF16).reshape(2, 2, BS, TILE)
+            acc = dot(own, b_own[slot, :, at]) + dot(oth, b_oth[slot, :, at])
+            s1[slot, t] = acc.astype(BF16).reshape(2, 2, BS, TILE)
             copy1(i, t).start()
 
     def stage_b(i):
+        slot = i % 2
         for t in range(2):
             copy1(i, t).wait()
-            kept = s1[i, t, :, x] if t == 0 else s1[i, t, y]
+            kept = s1[slot, t, :, x] if t == 0 else s1[slot, t, y]
             r1[i, t] = (r1[i, t].astype(F32) + kept.astype(F32)).astype(BF16)
             copy2(i, t).start()
 
@@ -999,7 +814,7 @@
                 zs[i, z_rows(l)] = total.astype(BF16)
                 copy_z(i, l + 1).start()
             else:
-                gs[i, g_rows(l, True)] = total.astype(BF16)
+                r2[i, g_rows(l)] = total.astype(BF16)
                 copy_g(i, l).start()
         return run
 
@@ -1009,35 +824,251 @@
             if l:
                 copy_g(i, l - 1).start()
             else:
-                part = gs[i].astype(F32)
+                part = r2[i].astype(F32)
                 part = jnp.sum((part * part).reshape(BS // 8, 8, PAIR), axis=0)
                 sq[0] += sum(part[:, g * LANES : (g + 1) * LANES] for g in range(PAIR // LANES))
                 out_copy(i).start()
         return run
 
+    sub = 512
+
+    def attention_grad():
+        loads[0].wait()
+        w_load(0, 2).wait()
+        for i in range(width // sub):
+            tall = wr[2, i * (sub // BS) : (i + 1) * (sub // BS)].reshape(sub, width)
+            gob[:, i * sub : (i + 1) * sub] = dot_nt(gb[...], tall).astype(BF16)
+        w_load(2, 2).start()
+        loads[1].wait()
+        loads[2].wait()
+        gn2[...] = jnp.zeros_like(gn2)
+        gn1[...] = jnp.zeros_like(gn1)
+
+    def feed_grad(k):
+        w_load(0, 0).wait()
+        w_load(0, 1).wait()
+
+        def part(i, carry):
+            inner = pl.ds(pl.multiple_of(i * sub, sub), sub)
+            at = pl.ds(pl.multiple_of(k * PAIR + i * sub, sub), sub)
+            act = dot(gb[...], wr[0, :, :, inner].reshape(width, sub))
+            low = (act * gub[:, at].astype(F32)).astype(BF16)
+            gub[:, at] = low
+            gus[0:1, at] = jnp.sum(low.astype(F32), axis=0, keepdims=True)
+            gn2[...] += dot_nt(low, wr[1, :, :, inner].reshape(width, sub))
+            return carry
+
+        lax.fori_loop(0, PAIR // sub, part, 0)
+        b_send(2, first[2] + k).start()
+        more = k + 1 < per
+        w_load(jnp.where(more, down0 + k + 1, 0), 0).start()
+        w_load(jnp.where(more, up0 + k + 1, 1), 1).start()
+
+    scale = HD**-0.5
+
+    def attend(p):
+        slot = p % 2
+        for k in range(6):
+            att_load(p, k).wait()
+
+        @pl.when(p + 1 < width // LANES)
+        def _():
+            for k in range(6):
+                att_load(p + 1, k).start()
+
+        lanes = pl.ds(pl.multiple_of(p * LANES, LANES), LANES)
+        place_keys(att.at[slot, 1], att.at[slot, 3], kpos, parity)
+        place_keys(att.at[slot, 2], att.at[slot, 4], vpos, parity)
+        dkpos[...] = jnp.zeros_like(dkpos)
+        dvpos[...] = jnp.zeros_like(dvpos)
+        dqs[...] = jnp.zeros_like(dqs)
+        for b in range(2):
+            at = slice(b * half, (b + 1) * half)
+            qcat[b] = split_heads(att[slot, 0, at, :] * jnp.asarray(scale, BF16))
+            gs = gob[at, lanes]
+            gcat[b] = split_heads(gs)
+            prod = (gs.astype(F32) * att[slot, 5, at, :].astype(F32)).T
+            rowsum[b, 0:1, :half] = lse_ref[p, 0:1, at]
+            rowsum[b, 0:1, half:] = lse_ref[p, 1:2, at]
+            rowsum[b, 1:2, :half] = jnp.sum(prod[:HD, :], axis=0, keepdims=True)
+            rowsum[b, 1:2, half:] = jnp.sum(prod[HD:, :], axis=0, keepdims=True)
+
+        def tile(t, carry):
+            b, j = key_tile(t, parity)
+            ks = pl.ds(pl.multiple_of(j * half, half), half)
+            keys = kpos[ks, :]
+            qh, gh = qcat[b], gcat[b]
+            m = mask[t]
+            got = dot_nt(keys, qh)
+            got = jnp.concatenate([jnp.minimum(got[:, :half], m), jnp.minimum(got[:, half:], m)], axis=1)
+            prob = jnp.exp(got - rowsum[b, 0:1, :])
+            dp = dot_nt(vpos[ks, :], gh)
+            ds = (prob * (dp - rowsum[b, 1:2, :])).astype(BF16)
+            dvpos[ks, :] += dot(prob.astype(BF16), gh)
+            dkpos[ks, :] += dot(ds, qh)
+            dqs[b] += dot(ds, keys, ((0,), (0,)))
+            return carry
+
+        lax.fori_loop(0, 5, tile, 0)
+        for b in range(2):
+            at = slice(b * half, (b + 1) * half)
+            dq = join_heads(dqs[b]) * scale
+            gqkv[at, lanes] = turn(dq, tab[0, at, :], -tab[1, at, :], -tab[2, at, :]).astype(BF16)
+        for k, src in enumerate((dkpos, dvpos)):
+            for b in range(2):
+                at = slice(b * half, (b + 1) * half)
+                mine = parity if b == 0 else 3 - parity
+                other = 1 - parity if b == 0 else 2 + parity
+                own_kv[slot, k, at, :] = src[pl.ds(pl.multiple_of(mine * half, half), half), :]
+                snd_kv[slot, k, at, :] = src[pl.ds(pl.multiple_of(other * half, half), half), :].astype(BF16)
+        kv_back(p).start()
+
+    def kv_back(p):
+        return remote(snd_kv.at[p % 2], rcv_kv.at[p], sem_ks.at[p], sem_kr.at[p], to_core)
+
+    def settle(p):
+        kv_back(p).wait()
+        slot = p % 2
+        key = own_kv[slot, 0] + rcv_kv[p, 0].astype(F32)
+        gqkv[:, pl.ds(pl.multiple_of(width + p * LANES, LANES), LANES)] = turn(key, tab[0], -tab[1], -tab[2]).astype(BF16)
+        value = own_kv[slot, 1] + rcv_kv[p, 1].astype(F32)
+        gqkv[:, pl.ds(pl.multiple_of(2 * width + p * LANES, LANES), LANES)] = value.astype(BF16)
+
+    def qkv_grad(m):
+        w_load(0, m).wait()
+        part = gqkv[:, cols(m)]
+        qs[0:1, cols(m)] = jnp.sum(part.astype(F32), axis=0, keepdims=True)
+        for i in range(width // sub):
+            tall = wr[m, i * (sub // BS) : (i + 1) * (sub // BS)].reshape(sub, PAIR)
+            gn1[:, i * sub : (i + 1) * sub] += dot_nt(part, tall)
+
+    in_copy = pltpu.make_async_copy(gy, in_out, sem_i.at[5])
+
+    def norm_grad():
+        loads[3].wait()
+        loads[4].wait()
+        step = 64
+        vg[...] = jnp.zeros_like(vg)
+
+        def chunk(i, carry):
+            at = pl.ds(pl.multiple_of(i * step, step), step)
+            xh, rstd = normed(xs[at, :].astype(F32))
+            total = gy[at, :]
+            sums = []
+            for g_n, gain in ((gn1[at, :], par_ref[0:1, 0:width]), (gn2[at, :], par_ref[0:1, 2 * width : 3 * width])):
+                sums.append(jnp.sum(g_n * xh, axis=0, keepdims=True))
+                sums.append(jnp.sum(g_n, axis=0, keepdims=True))
+                e = g_n * gain
+                mean = jnp.mean(e, axis=-1, keepdims=True)
+                along = jnp.mean(e * xh, axis=-1, keepdims=True)
+                total = total + rstd * (e - mean - xh * along)
+            gy[at, :] = total
+            vg[...] += jnp.concatenate(sums, axis=0)
+            return carry
+
+        lax.fori_loop(0, rows // step, chunk, 0)
+        in_copy.start()
+        v[...] = jnp.zeros_like(v)
+        pieces = [(vg, r, width) for r in range(4)] + [(qs, 0, 3 * width), (gbs_ref, 0, width), (gus, 0, hidden), (gbs_ref, 0, width)]
+        spot = 0
+        for ref, r, size in pieces:
+            for g in range(size // LANES):
+                owner, line = spot // lines, spot % lines
+                v[owner // 4, (owner // 2) % 2, owner % 2, line : line + 1, :] = ref[r : r + 1, g * LANES : (g + 1) * LANES]
+                spot += 1
+        v_copy(0).start()
+
+    vecs = [
+        (v.at[:, :, 1 - core], vr.at[0, :, :], to_core),
+        (vr.at[0, :, 1 - x], vr.at[1, 0, :], to_x),
+        (vr.at[1, 0, 1 - y], vr.at[1, 1, 0], to_y),
+    ]
+
+    def v_copy(k):
+        if k < 3:
+            src, dst, peer = vecs[k]
+        else:
+            src, dst, peer = vd.at[2 * (k - 3)], vd.at[2 * (k - 3) + 1], to_z[k - 3]
+        return remote(src, dst, sem_vs.at[k], sem_vr.at[k], peer)
+
+    def v_done(k):
+        v_copy(k).wait()
+        if k == 0:
+            vr[0] = vr[0] + v[:, :, core]
+        elif k == 1:
+            vr[1, 0] = vr[1, 0] + vr[0, :, x]
+        else:
+            if k == 2:
+                total = vr[1, 1, 0] + vr[1, 0, y]
+            else:
+                total = vd[2 * (k - 3)] + vd[2 * (k - 3) + 1]
+            vd[2 * (k - 2)] = total
+
+    v_hops = 3 + replica_bits
+    sq[...] = jnp.zeros_like(sq)
     stages = [stage_a, stage_b, stage_c]
     stages += [stage_z(l) for l in range(levels)] + [stage_g(l) for l in reversed(range(levels))]
     lags = len(stages)
+    att_pairs = width // LANES
+    fetch(0)
+    lax.fori_loop(0, 5, see, 0)
 
     def step(i, carry):
+        @pl.when(i == last)
+        def _():
+            settle(att_pairs - 1)
+            for m in range(plan[3]):
+                b_send(3, last + m).start()
+            fetch(last)
+
         for lag, stage in enumerate(stages):
             @pl.when((i >= lag) & (i < pairs + lag))
             def _():
                 stage(i - lag)
 
+            if lag == 0:
+                @pl.when((i + 1 < pairs) & (i + 1 != last))
+                def _():
+                    fetch(i + 1)
+
+        @pl.when(i == 0)
+        def _():
+            attention_grad()
+
+        @pl.when(i < per)
+        def _():
+            feed_grad(i)
+
+        @pl.when((i >= 2) & (i - 2 < att_pairs - 1))
+        def _():
+            settle(i - 2)
+
+        @pl.when((i >= 1) & (i - 1 < att_pairs))
+        def _():
+            attend(i - 1)
+
+        for m in range(plan[3]):
+            @pl.when(i == last + m)
+            def _():
+                qkv_grad(m)
+
+        @pl.when(i == pairs)
+        def _():
+            norm_grad()
+
         for k in range(v_hops):
-            @pl.when(i == k + 1)
+            @pl.when(i == pairs + k + 1)
             def _():
                 v_done(k)
                 if k + 1 < v_hops:
                     v_copy(k + 1).start()
         return carry
 
-    lax.fori_loop(0, pairs + lags - 1, step, 0)
+    lax.fori_loop(0, pairs + max(lags - 1, v_hops + 1), step, 0)
     total = vd[2 * replica_bits]
     vec_out[...] = total
-    rows13 = lax.broadcasted_iota(jnp.int32, total.shape, 0) < 13
-    square = jnp.where(rows13, total * total, 0.0)
+    real = lax.broadcasted_iota(jnp.int32, total.shape, 0) < lines
+    square = jnp.where(real, total * total, 0.0)
     sq[0] += square[0:8] + square[8:16]
     for k, peer in enumerate((to_core, to_x, to_y)):
         hop = remote(sq.at[k], sq_in.at[k], sem_qs.at[k], sem_qr.at[k], peer)
@@ -1045,6 +1076,7 @@
         hop.wait()
         sq[k + 1] = sq[k] + sq_in[k]
     sq_out[...] = sq[3]
+    in_copy.wait()
 
     def drain(i, carry):
         out_copy(i).wait()
@@ -1053,49 +1085,59 @@
     lax.fori_loop(0, pairs, drain, 0)
 
 
-def reduce_grads(ats, bs, vec, replicas):
-    plan = [b.shape[1] // PAIR for b in bs]
+def backward_pass(ats, hb, gb, dg, weights, q, kv, kvo, ob, gy, x, tables, lse, params, gb_sum, seg, replicas, lines):
+    rows, width = gb.shape
+    half = rows // 2
+    hidden = hb.shape[1]
+    plan = [hidden // PAIR, width // PAIR, hidden // PAIR, 3 * width // PAIR]
     pairs = sum(plan)
-    tokens = bs[0].shape[0]
+    groups = len(plan)
     replica_bits = replicas.bit_length() - 1
-    assert replicas == 1 << replica_bits
     levels = replica_bits if replicas <= 8 else 0
-    groups = len(plan)
     dma = pltpu.SemaphoreType.DMA
     lv, vh = max(levels, 1), 3 + replica_bits
+    att_pairs = width // LANES
+    blocks = width // BS
+    vm = pltpu.VMEM
     scratch = [
-        pltpu.VMEM((groups, 4, BS, tokens), BF16),
-        pltpu.VMEM((groups, 4, BS, tokens), BF16),
-        pltpu.VMEM((2, tokens, PAIR), BF16),
-        pltpu.VMEM((pairs, tokens, PAIR), BF16),
-        pltpu.VMEM((pairs, 2, 2, 2, BS, TILE), BF16),
-        pltpu.VMEM((pairs, 2, 2, BS, TILE), BF16),
-        pltpu.VMEM((pairs, BS, PAIR), BF16),
-        pltpu.VMEM((pairs, BS if levels else 16, PAIR), BF16),
-        pltpu.VMEM((pairs if levels else 1, BS, PAIR), BF16),
-        pltpu.VMEM((2, 2, 2, 16, LANES), F32),
-        pltpu.VMEM((2 * replica_bits + 2, 16, LANES), F32),
-        pltpu.VMEM((4, 8, LANES), F32),
-        pltpu.VMEM((3, 8, LANES), F32),
-        dma((groups,)), dma((2,)), dma((groups,)), dma((groups,)), dma((pairs,)), dma((pairs,)),
+        vm((groups, 4, BS, rows), BF16), vm((groups, 4, BS, rows), BF16),
+        vm((2, rows, PAIR), BF16), vm((2, rows, PAIR), BF16),
+        vm((2, 2, 2, 2, BS, TILE), BF16), vm((pairs, 2, 2, BS, TILE), BF16),
+        vm((pairs, BS, PAIR), BF16), vm((pairs, max(BS - (BS >> levels), 16), PAIR), BF16),
+        vm((rows, width), BF16), vm((rows, hidden), BF16), vm((rows, width), BF16), vm((rows, 3 * width), BF16),
+        vm((3, blocks, BS, PAIR), BF16),
+        vm((2, 6, rows, LANES), BF16), vm((5, half, half), F32),
+        vm((2 * rows, LANES), BF16), vm((2 * rows, LANES), BF16), vm((2 * rows, LANES), F32), vm((2 * rows, LANES), F32),
+        vm((2, rows, LANES), F32), vm((2, rows, LANES), BF16), vm((2, rows, LANES), BF16), vm((2, 8, rows), F32),
+        vm((2, 2, rows, LANES), F32), vm((2, 2, rows, LANES), BF16), vm((att_pairs, 2, rows, LANES), BF16),
+        vm((3, rows, LANES), F32), vm((rows, width), F32), vm((rows, width), F32), vm((rows, width), F32),
+        vm((rows, width), BF16), vm((4, width), F32), vm((1, hidden), F32), vm((1, 3 * width), F32),
+        vm((2, 2, 2, 16, LANES), F32), vm((2, 2, 2, 16, LANES), F32), vm((2 * replica_bits + 2, 16, LANES), F32),
+        vm((4, 8, LANES), F32), vm((3, 8, LANES), F32),
+        dma((groups,)), dma((2, 2)), dma((groups,)), dma((groups,)), dma((pairs,)), dma((pairs,)),
         dma((pairs, 2)), dma((pairs, 2)), dma((pairs, 2)), dma((pairs, 2)),
         dma((pairs, lv)), dma((pairs, lv)), dma((pairs, lv)), dma((pairs, lv)),
-        dma((vh,)), dma((vh,)), dma((3,)), dma((3,)), dma((pairs,)),
+        dma((vh,)), dma((vh,)), dma((3,)), dma((3,)), dma((pairs,)), dma((3,)), dma((2, 6)), dma((6,)),
+        dma((att_pairs,)), dma((att_pairs,)),
     ]
     anyspace = pl.BlockSpec(memory_space=pl.ANY)
     vmem = pl.BlockSpec(memory_space=pltpu.VMEM)
     return pl.pallas_call(
-        partial(reduce_kernel, plan, levels, replica_bits),
+        partial(bwd_kernel, plan, levels, replica_bits, lines),
         out_shape=[
-            sds((BS, pairs * PAIR), BF16), sds((16, LANES), F32), sds((8, LANES), F32)
+            sds((BS, pairs * PAIR), BF16), sds((rows, width), F32), sds((pairs, rows, PAIR), BF16),
+            sds((16, LANES), F32), sds((8, LANES), F32),
         ],
-        in_specs=[anyspace] * (2 * groups) + [vmem],
-        out_specs=[anyspace, vmem, vmem],
+        in_specs=[anyspace] * (groups + 11) + [vmem] * 4,
+        out_specs=[anyspace] * 3 + [vmem] * 2,
         scratch_shapes=scratch,
         compiler_params=pltpu.CompilerParams(
-            collective_id=0, has_side_effects=True, vmem_limit_bytes=58 * MIB
+            collective_id=0, has_side_effects=True, vmem_limit_bytes=60 * MIB
         ),
-    )(*[a.reshape(4, 2, BS, tokens) for a in ats], *bs, vec)
+    )(
+        *[a.reshape(4, 2, BS, rows) for a in ats], hb, gb, dg, weights, q, kv, kvo, ob, gy, x, tables,
+        lse, params, gb_sum, seg,
+    )
 
 
 def body(
@@ -1103,44 +1145,20 @@
 ):
     rows, width = tokens.shape
     stack = master.shape[1]
-    hidden = (stack - 4 * width) // 2
     half = rows // 2
     shards = lax.axis_size("shard")
     replicas = lax.axis_size("dp")
-    index = lax.axis_index("shard")
-    parity = index % 2
-    par = parity.astype(jnp.int32).reshape(1)
-    swap = [(i, i ^ 1) for i in range(shards)]
-
-    start = (index - parity) * rows
-    sequence = lax.dynamic_slice_in_dim(segments, start, 2 * rows).reshape(4, half)
-    key_seg = jnp.stack([sequence[0], sequence[2], sequence[3], sequence[1]])
-    own_seg = lax.dynamic_slice_in_dim(segments, index * rows, rows)
-
     own_len = vectors.shape[0]
     lines = own_len // LANES
     vec = jnp.pad(vectors.reshape(lines, LANES), ((0, 16 - lines), (0, 0)))
-    (weights, n1t, n2t, obt, gbt, q, kv, kvo, ob, hb, dg, gy, gb, tables, lse, gb_sum, params, scales) = forward_pass(
-        master, vec, tokens, targets, valid.astype(F32).reshape(rows, 1), segments.reshape(-1, 1, half), replicas,
-        own_len * shards,
+    seg = segments.reshape(-1, 1, half)
+    (weights, n1t, n2t, obt, gbt, q, kv, kvo, ob, hb, dg, gy, gb, tables, lse, gb_sum, params, _) = forward_pass(
+        master, vec, tokens, targets, valid.astype(F32).reshape(rows, 1), seg, replicas, own_len * shards
     )
-    weights = weights.reshape(width, stack)
-    vec4 = params[0, : 4 * width].reshape(4, width)
-    gob, gub, gub_sum, gn2 = dgrad(gb, weights, dg)
-
-    dq, dk, dv, dk_o, dv_o = att_bwd(
-        par, q, kv, kvo, gob, ob, lse, own_seg.reshape(2, half), key_seg.reshape(2 * rows, 1), tables
+    grads, input_grad, _, vec_total, squares = backward_pass(
+        (gbt, obt, n2t, n1t), hb, gb, dg, weights, q, kv, kvo, ob, gy, tokens, tables, lse, params, gb_sum, seg,
+        replicas, lines,
     )
-    dk_r = lax.ppermute(dk_o, "shard", swap)
-    dv_r = lax.ppermute(dv_o, "shard", swap)
-    gqkv, input_grad, vec_grad, gqkv_sum = last(
-        dq, dk, dv, dk_r, dv_r, tables, weights, tokens, vec4, gn2, gy
-    )
-    vector_grad = jnp.concatenate(
-        [vec_grad.reshape(-1), gqkv_sum.reshape(-1), gb_sum.reshape(-1), gub_sum.reshape(-1), gb_sum.reshape(-1)]
-    ).reshape(shards, lines, LANES)
-    packed = jnp.pad(vector_grad, ((0, 0), (0, 16 - lines), (0, 0))).reshape(2, 2, 2, 16, LANES)
-    grads, vec_total, squares = reduce_grads((gbt, obt, n2t, n1t), (hb, gb, gub, gqkv), packed, replicas)
     own_vector = vec_total[:lines].reshape(own_len)
     if replicas <= 8:
         square_sum = jnp.sum(squares)

time: 375 us -> 313 us (0.83)
  Pallas kernels: 354 us -> 301 us
  local copies, waits for them, and re-layouts: 10.8 us -> 5.38 us
    pallas_call x4 -> x1, Pallas kernels: 214 us -> 161 us  [backward_pass(): pl.pallas_call(partial(bwd_kernel, plan, levels, replica_bits, lines), ou...]
  transfers between devices with their start and end apart: 2 -> 0, of which waited for: 2 -> 0; matrix products, arithmetic and copies ran while one was open for 0% -> 0% of each run, Pallas kernels for 0% -> 0%
where the time goes in v4:
time: 313 us; the launch traced here: 312 us
  Pallas kernels  301 us (96%)
  local copies, waits for them, and re-layouts  5.38 us (2%)
  other arithmetic  3.28 us (1%)
    pallas_call x1, Pallas kernels, backward_pass(): pl.pallas_call(partial(bwd_kernel, plan, levels, replica_bits, lines), ou...  161 us
    pallas_call x1, Pallas kernels, forward_pass(): pl.pallas_call(partial(fwd_kernel, total, replica_bits), out_shape=[sds((...  119 us
    pallas_call x1, Pallas kernels, update(): call(update_kernel, (count // per,), [pl.BlockSpec(memory_space=pltpu.SME...  20.6 us

profile of v4, /device:TPU:0, one launch (start us, length us, event | category | flops | bytes accessed | tf_op | source)
XLA Modules:
  0.0 312.3 jit_solution(16126243495635967772)
XLA Ops:
  0.6 0.7 convert_element_type.5
  1.3 1.3 pad.4.v_ref
  2.6 0.9 copy.19.valid_ref
  3.5 119.3 %shard_map.170 = (bf16[8,128,12288]{2,1,0:T(8,128)(2,1)}, bf16[8,128,512]{2,1,0:T(8,128)(2,1)}, bf16[8,128,512]{2,1,0:T(8,128)(2,1)}, bf16[8,128,512]{2,1,0:T(8,...) custom-call(f32[128,12288]{1,0:T(8,128)} %m_ref.3, ...), custom_call_target="tpu_custom_call" | custom-call | tf_op jit(solution)/shard_map/pallas_call | solution.py:530
  122.8 0.0 copy-start.2
  122.8 0.0 copy-start.3
  122.8 161.2 %shard_map.171 = (bf16[128,12288]{1,0:T(8,128)(2,1)}, f32[512,1024]{1,0:T(8,128)}, bf16[12,512,1024]{2,1,0:T(8,128)(2,1)}, f32[16,128]{1,0:T(8,128)}, f32[8,128]{1,0:T(8,128)}) custom-call(bf16[4,2,128,512]{3,2,1,0:T(8,128)(2,1)} %bitcast.19, bf16[4,2,128,512]{3,2,1,0:T(8,128)(2,1)} %bitcast.18, bf16[4,2,128,512]{3,2,1,0:T(8,128)(2,1)} %bitcast.17, ...), custom_call_target="tpu_custom_call" | custom-call | tf_op jit(solution)/shard_map/pallas_call | solution.py:1125
  284.0 1.3 reduce_sum.9
  286.0 0.0 copy-done.2
  286.0 0.0 copy-done.3
  286.0 1.3 fusion.2
  287.4 0.0 copy-start
  287.4 1.9 copy-done
  289.2 0.0 copy-start.1
  289.3 20.6 %shard_map.172 = (f32[1,96,128,128]{3,2,1,0:T(8,128)}, f32[1,96,128,128]{3,2,1,0:T(8,128)}, f32[128,12288]{1,0:T(8,128)}, bf16[128,12288]{1,0:T(8,128)(2,1)}) custom-call(f32[1,1]{1,0:T(1,128)} %bitcast.7.f_ref, bf16[128,12288]{1,0:T(8,128)(2,1)S(1)} %copy-done, f32[1,96,128,128]{3,2,1,0:T(8,128)} %ls_ref.1, f32[1,96,128,128]{3,2,1,0:T(8,128)} %rs_ref.1, ...), custom_call_target="tpu_custom_call" | custom-call | flops 1610612736 | bytes 50331648 | tf_op jit(solution)/shard_map/pallas_call | solution.py:593
  309.8 0.0 copy-done.1
  309.9 1.3 copy.21
Async XLA Ops:
  122.8 163.3 %copy-start.2 = (f32[1664]{0:T(1024)S(1)}, f32[1664]{0:T(1024)}, u32[]{:S(2)}) copy-start(f32[1664]{0:T(1024)} %param.16) | copy-start | bytes 19972
  122.8 163.3 %copy-start.3 = (f32[1664]{0:T(1024)S(1)}, f32[1664]{0:T(1024)}, u32[]{:S(2)}) copy-start(f32[1664]{0:T(1024)} %param.21) | copy-start | bytes 19972
  287.4 1.9 copy-start
  289.2 20.6 %copy-start.1 = (f32[512,1024]{1,0:T(8,128)S(1)}, f32[512,1024]{1,0:T(8,128)}, u32[]{:S(2)}) copy-start(f32[512,1024]{1,0:T(8,128)} %get-tuple-element.68) | copy-start | bytes 6291460
